TPU v7x, 128 devices: a whole 4x4x4 slice. The times are simulated.
128 devices in a mesh: leaf: 16 (over x, z), sub: 8 (over y, core).
Axes of the slice: x: 4, y: 4, z: 4, core: 2. Of those that a mesh axis runs over, the one named last changes fastest.
Arguments:
- beads: float32 [262144, 128], P(('leaf', 'sub')), may hold values from -6 to 6
- rot_perm: int32 [262144], P(('leaf', 'sub')), may hold values from 0 to 262143, as said below
- pool_ids: int32 [262144], P(('leaf', 'sub')), may hold values from 0 to 32767, as said below
- ball_counts: int32 [16, 8], P('leaf'), may hold values from 1 to 24, 64 in all within a row
- fine_qkv: bfloat16 [2, 128, 384], replicated
- fine_out: bfloat16 [2, 128, 128], replicated, may hold values from -0.5 to 0.5
- pool_weight: bfloat16 [1024, 512], replicated, may hold values from -0.1875 to 0.1875
- coarse_qkv: bfloat16 [2, 512, 1536], replicated
- coarse_out: bfloat16 [2, 512, 512], replicated, may hold values from -0.25 to 0.25
- unpool_weight: bfloat16 [512, 1024], replicated, may hold values from -0.25 to 0.25
Outputs:
- denoised: float32 [262144, 128], P(('leaf', 'sub'))
Inputs may be any that keep to these rules, and one draw needn't show every extreme that they name: `rot_perm`: a permutation of all 262144 beads; the 2048 rotated-order positions of each device name exactly 16 beads of every device, devices counted in the order of the arrays' rows. `pool_ids`: the 2048 beads of the device in row block d fall into 256 groups of exactly eight, numbered d * 256 to (d + 1) * 256 - 1. `ball_counts`: each row sums to 64.
All inputs are finite; a program needn't handle non-finite values.
Results may differ from a plain program's by a relative error of at most 0.017.
The roundings to bfloat16 on the way count: a program that leaves them out, or rounds other values in their place, can miss the bound.
Values may be sent and summed in bfloat16 or wider, within the bound.
No kernel may reach another device: no remote copies, remote signals or barrier semaphores. Data moves between devices by JAX's collectives and lax.ppermute only.
A program may use at most 128 MiB of HBM per device.

v0:
```python
import functools
import math

import jax
import jax.numpy as jnp
from jax import lax
from jax.experimental import pallas as pl
from jax.experimental.pallas import tpu as pltpu
from jax.sharding import PartitionSpec as P

HEADS = 4
CHEADS = 8
BALL = 256
GRAN = 32
LOG2E = 1.4426950408889634
NEG = -1e30
F32 = jnp.float32
BF16 = jnp.bfloat16


def vmem():
    return pl.BlockSpec(memory_space=pltpu.VMEM)


def smem():
    return pl.BlockSpec(memory_space=pltpu.SMEM)


def dot(a, b, dims=((1,), (0,))):
    return lax.dot_general(a, b, (dims, ((), ())), preferred_element_type=F32)


def call(kernel, out_shape, in_specs, out_specs, scratch=(), flops=0, nbytes=0, name=None):
    return pl.pallas_call(
        kernel,
        out_shape=out_shape,
        in_specs=in_specs,
        out_specs=out_specs,
        scratch_shapes=list(scratch),
        cost_estimate=pl.CostEstimate(flops=flops, bytes_accessed=nbytes, transcendentals=0),
        name=name,
    )


def ranks(classes, of_ref, count, total):
    step = 256
    tri = (
        lax.broadcasted_iota(jnp.int32, (step, step), 0)
        <= lax.broadcasted_iota(jnp.int32, (step, step), 1)
    )
    tri = jnp.where(tri, 1.0, 0.0).astype(BF16)
    names = lax.broadcasted_iota(jnp.int32, (count, step), 0)
    carried = jnp.zeros((count, 1), F32)
    hots, found = [], []
    for row in range(total // step):
        hot = jnp.where(names == classes[row], 1.0, 0.0)
        hot16 = hot.astype(BF16)
        running = dot(hot16, tri) + carried
        found.append(jnp.sum(hot * running, axis=0, keepdims=True) - 1.0)
        hots.append(hot16)
        carried = running[:, step - 1 : step]
    return hots, found


def route_kernel(rot_ref, wanted_ref, slot_ref, *, own, devices):
    rows = own // 256
    bucket = own // devices
    dest = [rot_ref[r : r + 1, :] // own for r in range(rows)]
    hots, found = ranks(dest, rot_ref, devices, own)
    lanes = lax.broadcasted_iota(jnp.int32, (bucket, 256), 0)
    total = jnp.zeros((devices, 2 * bucket), F32)
    for r in range(rows):
        rank = found[r].astype(jnp.int32)
        slot_ref[r : r + 1, :] = dest[r] * bucket + rank
        local = rot_ref[r : r + 1, :] % own
        here = lanes == rank
        high = jnp.where(here, (local // 64).astype(F32), 0.0)
        low = jnp.where(here, (local % 64).astype(F32), 0.0)
        parts = jnp.concatenate([high, low], axis=0).astype(BF16)
        total = total + dot(hots[r], parts, ((1,), (1,)))
    wanted = total[:, :bucket] * 64.0 + total[:, bucket:]
    wanted_ref[...] = jnp.zeros_like(wanted_ref)
    wanted_ref[:, :bucket] = wanted.astype(jnp.int32)


def place_kernel(pool_ref, place_ref, *, own, nodes):
    rows = own // 256
    node = [pool_ref[r : r + 1, :] % nodes for r in range(rows)]
    _, found = ranks(node, pool_ref, nodes, own)
    for r in range(rows):
        place_ref[r : r + 1, :] = found[r].astype(jnp.int32) * nodes + node[r]


def norm_rows(x):
    centre = x - jnp.mean(x, axis=-1, keepdims=True)
    spread = jnp.mean(centre * centre, axis=-1, keepdims=True)
    return (centre * lax.rsqrt(spread + 1e-5)).astype(BF16)


def norm_columns(x):
    centre = x - jnp.mean(x, axis=0, keepdims=True)
    spread = jnp.mean(centre * centre, axis=0, keepdims=True)
    return (centre * lax.rsqrt(spread + 1e-5)).astype(BF16)


def ball(x, key_weight, qv_weight, out_weight):
    rows, channels = x.shape
    size = channels // HEADS
    normed = norm_rows(x)
    keys = dot(normed, key_weight).astype(BF16)
    qv = dot(qv_weight, normed, ((1,), (1,))).astype(BF16)
    ones = jnp.ones((16, rows), BF16)
    attended = []
    for head in range(HEADS):
        mine = slice(head * size, (head + 1) * size)
        above, below = head * size, channels - (head + 1) * size
        pieces = [qv[mine]]
        if above:
            pieces = [jnp.zeros((above, rows), BF16)] + pieces
        if below:
            pieces = pieces + [jnp.zeros((below, rows), BF16)]
        queries = jnp.concatenate(pieces, axis=0)
        scores = dot(keys, queries)
        most = jnp.max(scores, axis=0, keepdims=True)
        weights = jnp.exp2((scores - most) * (LOG2E / math.sqrt(size))).astype(BF16)
        values = jnp.concatenate([qv[channels + head * size : channels + (head + 1) * size], ones], 0)
        summed = dot(values, weights)
        attended.append((summed[:size] / summed[size : size + 1]).astype(BF16))
    attended = jnp.concatenate(attended, axis=0)
    return x + dot(attended, out_weight, ((0,), (0,)))


def first_kernel(x_ref, key_ref, qv_ref, out_ref, y_ref):
    def one(at, _):
        rows = pl.ds(pl.multiple_of(at * BALL, BALL), BALL)
        y_ref[rows, :] = ball(x_ref[rows, :], key_ref[...], qv_ref[...], out_ref[...])
        return 0

    lax.fori_loop(0, x_ref.shape[0] // BALL, one, 0)


def answer_kernel(wanted_ref, x_ref, out_ref, rows_ref, *, bucket):
    def one(device, _):
        for j in range(bucket):
            rows_ref[pl.ds(device * bucket + j, 1), :] = x_ref[pl.ds(wanted_ref[device, j], 1), :]
        return 0

    lax.fori_loop(0, wanted_ref.shape[0], one, 0)
    out_ref[...] = rows_ref[...].astype(BF16)


def second_kernel(slot_ref, x_ref, key_ref, qv_ref, out_ref, y_ref, from_ref, to_ref, ball_ref):
    from_ref[...] = x_ref[...].astype(F32)

    def one(at, _):
        def take(step, _):
            for j in range(16):
                row = step * 16 + j
                ball_ref[pl.ds(row, 1), :] = from_ref[pl.ds(slot_ref[at, row], 1), :]
            return 0

        lax.fori_loop(0, BALL // 16, take, 0)
        ball_ref[...] = ball(ball_ref[...], key_ref[...], qv_ref[...], out_ref[...])

        def give(step, _):
            for j in range(16):
                row = step * 16 + j
                to_ref[pl.ds(slot_ref[at, row], 1), :] = ball_ref[pl.ds(row, 1), :]
            return 0

        lax.fori_loop(0, BALL // 16, give, 0)
        return 0

    lax.fori_loop(0, x_ref.shape[0] // BALL, one, 0)
    y_ref[...] = to_ref[...].astype(BF16)


def send_projected(features, weight_ref, message_ref):
    normed = norm_columns(features)
    channels = features.shape[0]
    size = channels // CHEADS
    for part in range(3):
        projected = dot(weight_ref[part * channels : (part + 1) * channels, :], normed).astype(BF16)
        for head in range(CHEADS):
            message_ref[head, part * size : (part + 1) * size, :] = projected[
                head * size : (head + 1) * size
            ]


def pool_kernel(
    wanted_ref, place_ref, x_ref, pool_ref, qkv_ref, message_ref, pooled_ref, placed_ref, from_ref, *, bucket
):
    from_ref[...] = x_ref[...].astype(F32)

    def one(device, _):
        for j in range(bucket):
            bead = wanted_ref[device, j]
            placed_ref[pl.ds(place_ref[bead // 256, bead % 256], 1), :] = from_ref[
                pl.ds(device * bucket + j, 1), :
            ]
        return 0

    lax.fori_loop(0, wanted_ref.shape[0], one, 0)
    nodes = x_ref.shape[0] // 8
    channels = x_ref.shape[1]
    pooled = None
    for k in range(8):
        part = dot(
            pool_ref[:, k * channels : (k + 1) * channels],
            placed_ref[k * nodes : (k + 1) * nodes, :].astype(BF16),
            ((1,), (1,)),
        )
        pooled = part if pooled is None else pooled + part
    pooled = pooled.astype(BF16).astype(F32)
    pooled_ref[...] = pooled
    send_projected(pooled, qkv_ref, message_ref)


def coarse_kernel(counts_ref, x_ref, out_ref, keys_ref, of_ref, first_ref, last_ref):
    tiles, parts, width = x_ref.shape
    size = parts // 3
    balls = counts_ref.shape[1]
    per_tile = width // GRAN
    for t in range(tiles):
        keys_ref[t] = x_ref[t, size : 2 * size, :].astype(F32).T.astype(BF16)
    start = 0
    ends = []
    for e in range(balls):
        end = start + counts_ref[0, e]

        def mark(block, _, e=e, start=start, end=end):
            of_ref[block] = e
            first_ref[block] = start
            last_ref[block] = end - 1
            return 0

        lax.fori_loop(start, end, mark, 0)
        ends.append(end)
        start = end
    ones = jnp.ones((16, width), BF16)

    def one(tile, _):
        queries = x_ref[tile, :size, :]
        blocks = tile * per_tile + lax.broadcasted_iota(jnp.int32, (1, width), 1) // GRAN
        own = jnp.zeros((1, width), jnp.int32)
        for e in range(balls):
            own = own + jnp.where(blocks >= ends[e], 1, 0)
        low = first_ref[tile * per_tile] // per_tile
        high = last_ref[tile * per_tile + per_tile - 1] // per_tile

        def add(chunk, carry):
            most, total = carry
            scores = dot(keys_ref[chunk], queries)
            masked = []
            for g in range(per_tile):
                seen = own == of_ref[chunk * per_tile + g]
                masked.append(jnp.where(seen, scores[g * GRAN : (g + 1) * GRAN], NEG))
            scores = jnp.concatenate(masked, axis=0)
            now = jnp.maximum(most, jnp.max(scores, axis=0, keepdims=True))
            scale = LOG2E / math.sqrt(size)
            weights = jnp.exp2((scores - now) * scale).astype(BF16)
            values = jnp.concatenate([x_ref[chunk, 2 * size :, :], ones], axis=0)
            return now, total * jnp.exp2((most - now) * scale) + dot(values, weights)

        begin = (jnp.full((1, width), NEG, F32), jnp.zeros((size + 16, width), F32))
        _, total = lax.fori_loop(low, high + 1, add, begin)
        out_ref[tile] = (total[:size] / total[size : size + 1]).astype(BF16)
        return 0

    lax.fori_loop(0, tiles, one, 0)


def between_kernel(x_ref, features_ref, out_weight_ref, qkv_ref, message_ref, next_ref):
    heads, size, width = x_ref.shape
    features = features_ref[...] + dot(out_weight_ref[...], x_ref[...].reshape(heads * size, width))
    next_ref[...] = features
    send_projected(features, qkv_ref, message_ref)


def last_kernel(place_ref, x_ref, features_ref, out_weight_ref, unpool_ref, placed_ref, out_ref, sum_ref):
    heads, size, width = x_ref.shape
    features = features_ref[...] + dot(out_weight_ref[...], x_ref[...].reshape(heads * size, width))
    features = features.astype(BF16).astype(F32)
    normed = norm_columns(features).astype(F32).T.astype(BF16)
    channels = placed_ref.shape[1]
    for k in range(8):
        rows = slice(k * width, (k + 1) * width)
        expanded = dot(normed, unpool_ref[:, k * channels : (k + 1) * channels])
        sum_ref[rows, :] = placed_ref[rows, :] + expanded

    def one(step, _):
        for j in range(16):
            row = step * 16 + j
            out_ref[pl.ds(row, 1), :] = sum_ref[pl.ds(place_ref[row // 256, row % 256], 1), :]
        return 0

    lax.fori_loop(0, out_ref.shape[0] // 16, one, 0)


def shaped(shape, dtype):
    return jax.ShapeDtypeStruct(shape, dtype)


def exchange(value, axes):
    return lax.all_to_all(value, axes, split_axis=0, concat_axis=0, tiled=True)


def shards(
    beads,
    rot_perm,
    pool_ids,
    ball_counts,
    fine_qkv,
    fine_out,
    pool_weight,
    coarse_qkv,
    coarse_out,
    unpool_weight,
):
    own, channels = beads.shape
    both = ("leaf", "sub")
    subs = lax.axis_size("sub")
    devices = lax.axis_size("leaf") * subs
    bucket = own // devices
    nodes = own // 8
    wide = pool_weight.shape[1]
    size = wide // CHEADS
    rows = own // 256

    wanted, slots = call(
        functools.partial(route_kernel, own=own, devices=devices),
        (shaped((devices, 128), jnp.int32), shaped((rows, 256), jnp.int32)),
        [vmem()],
        (vmem(), vmem()),
        flops=2 * devices * own * 256,
        nbytes=100000,
        name="route",
    )(rot_perm.reshape(rows, 256))
    requested = exchange(wanted.reshape(devices, 1, 128), both).reshape(devices, 128)
    places = call(
        functools.partial(place_kernel, own=own, nodes=nodes),
        shaped((rows, 256), jnp.int32),
        [vmem()],
        vmem(),
        flops=2 * nodes * own * 256,
        nbytes=20000,
        name="place",
    )(pool_ids.reshape(rows, 256))

    key_weights = fine_qkv[:, :, channels : 2 * channels]
    qv_weights = jnp.concatenate(
        [fine_qkv[:, :, :channels], fine_qkv[:, :, 2 * channels :]], axis=2
    ).transpose(0, 2, 1)
    pool_turned = pool_weight.T
    coarse_turned = coarse_qkv.transpose(0, 2, 1)
    out_turned = coarse_out.transpose(0, 2, 1)
    ball_flops = own * channels * channels * 8 + own * BALL * channels * 16

    after_tree = call(
        first_kernel,
        shaped((own, channels), F32),
        [vmem()] * 4,
        vmem(),
        flops=ball_flops,
        nbytes=own * channels * 8,
        name="first",
    )(beads, key_weights[0], qv_weights[0], fine_out[0])
    answer = call(
        functools.partial(answer_kernel, bucket=bucket),
        shaped((own, channels), BF16),
        [smem(), vmem()],
        vmem(),
        [pltpu.VMEM((own, channels), F32)],
        nbytes=own * channels * 6,
        name="answer",
    )(requested, after_tree)
    arrived = exchange(answer.reshape(devices, bucket, channels), both).reshape(own, channels)
    outgoing = call(
        second_kernel,
        shaped((own, channels), BF16),
        [smem()] + [vmem()] * 4,
        vmem(),
        [pltpu.VMEM((own, channels), F32)] * 2 + [pltpu.VMEM((BALL, channels), F32)],
        flops=ball_flops,
        nbytes=own * channels * 4,
        name="second",
    )(slots, arrived, key_weights[1], qv_weights[1], fine_out[1])
    coming = exchange(outgoing.reshape(devices, bucket, channels), both).reshape(own, channels)
    message, features, placed = call(
        functools.partial(pool_kernel, bucket=bucket),
        (
            shaped((CHEADS, 3 * size, nodes), BF16),
            shaped((wide, nodes), F32),
            shaped((own, channels), F32),
        ),
        [smem(), smem()] + [vmem()] * 3,
        (vmem(), vmem(), vmem()),
        [pltpu.VMEM((own, channels), F32)],
        flops=2 * nodes * wide * (own // 2 + 3 * wide),
        nbytes=own * channels * 8,
        name="pool",
    )(requested, places, coming, pool_turned, coarse_turned[0])
    for layer in range(2):
        received = exchange(message, "sub")
        attended = call(
            coarse_kernel,
            shaped((subs, size, nodes), BF16),
            [smem(), vmem()],
            vmem(),
            [pltpu.VMEM((subs, nodes, size), BF16)] + [pltpu.SMEM((subs * nodes // GRAN,), jnp.int32)] * 3,
            flops=subs * nodes * nodes * 3 * size * 4,
            nbytes=subs * nodes * size * 8,
            name="coarse",
        )(ball_counts, received)
        back = exchange(attended, "sub")
        if layer == 0:
            message, features = call(
                between_kernel,
                (shaped((CHEADS, 3 * size, nodes), BF16), shaped((wide, nodes), F32)),
                [vmem()] * 4,
                (vmem(), vmem()),
                flops=2 * nodes * wide * 4 * wide,
                nbytes=nodes * wide * 8,
                name="between",
            )(back, features, out_turned[0], coarse_turned[1])
    return call(
        last_kernel,
        shaped((own, channels), F32),
        [smem()] + [vmem()] * 5,
        vmem(),
        [pltpu.VMEM((own, channels), F32)],
        flops=2 * nodes * wide * 3 * wide,
        nbytes=own * channels * 8,
        name="last",
    )(places, back, features, out_turned[1], unpool_weight, placed)


def solution(mesh):
    placed = (
        P(("leaf", "sub"), None),
        P(("leaf", "sub")),
        P(("leaf", "sub")),
        P("leaf", None),
        P(),
        P(),
        P(),
        P(),
        P(),
        P(),
    )
    return jax.shard_map(
        shards, mesh=mesh, in_specs=placed, out_specs=P(("leaf", "sub"), None), check_vma=False
    )
```

profile of v0, /device:TPU:6, one launch (start us, length us, event | category | flops | bytes accessed | tf_op | source)
XLA Modules:
  0.0 239.5 jit_solution(2331054515365240330)
XLA Ops:
  0.0 1.3 reshape.25.rot_ref
  1.3 2.3 route.1
  3.6 10.5 %all-to-all-start = ((s32[128,1,128]{2,1,0:T(1,128)}), s32[128,1,128]{2,1,0:T(1,128)S(1)}, u32[]{:S(2)}, u32[]{:S(2)}) async-start(s32[128,1,128]{2,1,0:T(1,128)} %bitcast.40), calls=%async_computation | async-start | bytes 131072 | tf_op jit(solution)/shard_map/all_to_all | solution.py:305
  14.1 0.9 fusion
  15.2 0.7 slice_bitcast_fusion.4
  15.9 1.4 slice_bitcast_fusion.6
  17.3 14.0 %first.1.x_ref = f32[2048,128]{1,0:T(8,128)} custom-call(f32[2048,128]{1,0:T(8,128)} %x_ref.1, bf16[128,128]{1,0:T(8,128)(2,1)} %get-tuple-element.31.key_ref, bf16[256,128]{1,0:T(8,128)(2,1)} %get-tuple-element.28.qv_ref, bf16[128,128]{1,0:T(8,128)(2,1)} %get-tuple-element.30.out_ref), custom_call_target="tpu_custom_call" | custom-call | flops 1342177280 | bytes 2097152 | tf_op jit(solution)/shard_map/first/pallas_call | solution.py:359
  31.3 0.6 copy-done.3
  31.9 4.9 %answer.1 = bf16[2048,128]{1,0:T(8,128)(2,1)} custom-call(s32[128,128]{1,0:T(8,128)} %bitcast.37, f32[2048,128]{1,0:T(8,128)} %first.1.x_ref), custom_call_target="tpu_custom_call" | custom-call | bytes 1572864 | tf_op jit(solution)/shard_map/answer/pallas_call | solution.py:368
  36.8 10.2 %all-to-all-start.1 = ((bf16[128,16,128]{2,1,0:T(8,128)(2,1)}), bf16[128,16,128]{2,1,0:T(8,128)(2,1)}, u32[]{:S(2)}, u32[]{:S(2)}) async-start(bf16[128,16,128]{2,1,0:T(8,128)(2,1)} %bitcast.36), calls=%async_computation.1 | async-start | bytes 1048576 | tf_op jit(solution)/shard_map/all_to_all | solution.py:305
  47.0 3.2 %copy.20 = bf16[2,512,1536]{1,2,0:T(8,128)(2,1)S(1)} copy(bf16[2,512,1536]{2,1,0:T(8,128)(2,1)} %param.17) | data formatting | bytes 6291456 | tf_op args[7]
  50.9 2.3 copy.19
  53.1 2.1 place.1.place_ref
  55.2 4.0 %all-to-all-done.1 = bf16[128,16,128]{2,1,0:T(8,128)(2,1)} async-done(((bf16[128,16,128]{2,1,0:T(8,128)(2,1)}), bf16[128,16,128]{2,1,0:T(8,128)(2,1)}, u32[]{:S(2)}, u32[]{:S(2)}) %all-to-all-start.1) | async-done | bytes 524320 | tf_op jit(solution)/shard_map/all_to_all | solution.py:305
  59.2 24.9 %second.1 = bf16[2048,128]{1,0:T(8,128)(2,1)} custom-call(s32[8,256]{1,0:T(8,128)} %get-tuple-element.13.slot_ref, bf16[2048,128]{1,0:T(8,128)(2,1)} %bitcast.8.x_ref, bf16[128,128]{1,0:T(8,128)(2,1)} %get-tuple-element.32.key_ref, bf16[256,128]{1,0:T(8,128)(2,1)} %get-tuple-element.27.qv_ref, bf16[128,128]{1,0:T(8,128)(2,1)} %get-tuple-element.29.out_ref), custom_call_target="tpu_custom_call" | custom-call | flops 1342177280 | bytes 1048576 | tf_op jit(solution)/shard_map/second/pallas_call | solution.py:378
  84.1 6.6 %all-to-all-start.2 = ((bf16[128,16,128]{2,1,0:T(8,128)(2,1)}), bf16[128,16,128]{2,1,0:T(8,128)(2,1)}, u32[]{:S(2)}, u32[]{:S(2)}) async-start(bf16[128,16,128]{2,1,0:T(8,128)(2,1)} %bitcast.39), calls=%async_computation.2 | async-start | bytes 1048576 | tf_op jit(solution)/shard_map/all_to_all | solution.py:305
  90.7 1.8 slice_bitcast_fusion
  92.6 10.4 %all-to-all-done.2 = bf16[128,16,128]{2,1,0:T(8,128)(2,1)} async-done(((bf16[128,16,128]{2,1,0:T(8,128)(2,1)}), bf16[128,16,128]{2,1,0:T(8,128)(2,1)}, u32[]{:S(2)}, u32[]{:S(2)}) %all-to-all-start.2) | async-done | bytes 524320 | tf_op jit(solution)/shard_map/all_to_all | solution.py:305
  103.0 23.6 %pool.1 = (bf16[8,192,256]{2,1,0:T(8,128)(2,1)}, f32[512,256]{1,0:T(8,128)}, f32[2048,128]{1,0:T(8,128)}) custom-call(s32[128,128]{1,0:T(8,128)} %bitcast.38, s32[8,256]{1,0:T(8,128)} %place.1.place_ref, bf16[2048,128]{1,0:T(8,128)(2,1)} %bitcast.13.x_ref, bf16[512,1024]{1,0:T(8,128)(2,1)} %bitcast.34, bf16[1536,512]{1,0:T(8,128)(2,1)} %get-tuple-element.20.qkv_ref), custom_call_target="tpu_custom_call" | custom-call | flops 671088640 | bytes 2097152 | tf_op jit(solution)/shard_map/pool/pallas_call | solution.py:389
  126.6 3.7 %all-to-all-start.3 = ((bf16[8,192,256]{2,1,0:T(8,128)(2,1)}), bf16[8,192,256]{2,1,0:T(8,128)(2,1)S(1)}, u32[]{:S(2)}, u32[]{:S(2)}) async-start(bf16[8,192,256]{2,1,0:T(8,128)(2,1)} %get-tuple-element.14), calls=%async_computation.3 | async-start | bytes 1572864 | tf_op jit(solution)/shard_map/all_to_all | solution.py:305
  130.8 12.5 %all-to-all-done.3.x_ref = bf16[8,192,256]{2,1,0:T(8,128)(2,1)S(1)} async-done(((bf16[8,192,256]{2,1,0:T(8,128)(2,1)}), bf16[8,192,256]{2,1,0:T(8,128)(2,1)S(1)}, u32[]{:S(2)}, u32[]{:S(2)}) %all-to-all-start.3) | async-done | bytes 786464 | tf_op jit(solution)/shard_map/all_to_all | solution.py:305
  143.3 0.9 copy-done.2
  144.2 14.4 %coarse.2 = bf16[8,64,256]{2,1,0:T(8,128)(2,1)} custom-call(s32[1,8]{1,0:T(1,128)} %counts_ref.3, bf16[8,192,256]{2,1,0:T(8,128)(2,1)} %copy-done.2), custom_call_target="tpu_custom_call" | custom-call | flops 402653184 | bytes 1048576 | tf_op jit(solution)/shard_map/coarse/pallas_call | solution.py:405
  158.5 3.4 %all-to-all-start.4 = ((bf16[8,64,256]{2,1,0:T(8,128)(2,1)}), bf16[8,64,256]{2,1,0:T(8,128)(2,1)S(1)}, u32[]{:S(2)}, u32[]{:S(2)}) async-start(bf16[8,64,256]{2,1,0:T(8,128)(2,1)} %coarse.2), calls=%async_computation.4 | async-start | bytes 524288 | tf_op jit(solution)/shard_map/all_to_all | solution.py:305
  162.0 1.1 slice_bitcast_fusion.2
  163.0 6.4 %all-to-all-done.4.x_ref = bf16[8,64,256]{2,1,0:T(8,128)(2,1)S(1)} async-done(((bf16[8,64,256]{2,1,0:T(8,128)(2,1)}), bf16[8,64,256]{2,1,0:T(8,128)(2,1)S(1)}, u32[]{:S(2)}, u32[]{:S(2)}) %all-to-all-start.4) | async-done | bytes 262176 | tf_op jit(solution)/shard_map/all_to_all | solution.py:305
  169.4 0.7 copy-done.1
  170.1 3.9 %between.1 = (bf16[8,192,256]{2,1,0:T(8,128)(2,1)}, f32[512,256]{1,0:T(8,128)}) custom-call(bf16[8,64,256]{2,1,0:T(8,128)(2,1)} %copy-done.1, f32[512,256]{1,0:T(8,128)} %get-tuple-element.15.features_ref, bf16[512,512]{1,0:T(8,128)(2,1)} %get-tuple-element.22.out_weight_ref, bf16[1536,512]{1,0:T(8,128)(2,1)} %get-tuple-element.19.qkv_ref), custom_call_target="tpu_custom_call" | custom-call | flops 536870912 | bytes 1048576 | tf_op jit(solution)/shard_map/between/pallas_call | solution.py:417
  174.0 17.4 %all_to_all.35.x_ref = bf16[8,192,256]{2,1,0:T(8,128)(2,1)} all-to-all(bf16[8,192,256]{2,1,0:T(8,128)(2,1)} %get-tuple-element.16), channel_id=1, replica_groups=mesh['leaf'=16,'sub'=8] {'sub'}, dimensions={0} | all-to-all | bytes 1572864 | tf_op jit(solution)/shard_map/all_to_all | solution.py:305
  191.4 14.4 %coarse.3 = bf16[8,64,256]{2,1,0:T(8,128)(2,1)} custom-call(s32[1,8]{1,0:T(1,128)} %counts_ref.3, bf16[8,192,256]{2,1,0:T(8,128)(2,1)} %all_to_all.35.x_ref), custom_call_target="tpu_custom_call" | custom-call | flops 402653184 | bytes 1048576 | tf_op jit(solution)/shard_map/coarse/pallas_call | solution.py:405
  205.7 11.5 %all_to_all.36.x_ref = bf16[8,64,256]{2,1,0:T(8,128)(2,1)} all-to-all(bf16[8,64,256]{2,1,0:T(8,128)(2,1)} %coarse.3), channel_id=1, replica_groups=mesh['leaf'=16,'sub'=8] {'sub'}, dimensions={0} | all-to-all | bytes 524288 | tf_op jit(solution)/shard_map/all_to_all | solution.py:305
  217.3 22.2 %last.1 = f32[2048,128]{1,0:T(8,128)} custom-call(s32[8,256]{1,0:T(8,128)} %place.1.place_ref, bf16[8,64,256]{2,1,0:T(8,128)(2,1)} %all_to_all.36.x_ref, f32[512,256]{1,0:T(8,128)} %get-tuple-element.17.features_ref, bf16[512,512]{1,0:T(8,128)(2,1)} %get-tuple-element.21.out_weight_ref, bf16[512,1024]{1,0:T(8,128)(2,1)} %unpool_ref.1, ...), custom_call_target="tpu_custom_call" | custom-call | flops 402653184 | bytes 2097152 | tf_op jit(solution)/shard_map/last/pallas_call | solution.py:426
  (15 shorter events, 1.4 us)
Async XLA Ops:
  0.0 15.9 %copy-start.4 = (bf16[2,128,128]{2,1,0:T(8,128)(2,1)S(1)}, bf16[2,128,128]{2,1,0:T(8,128)(2,1)}, u32[]{:S(2)}) copy-start(bf16[2,128,128]{2,1,0:T(8,128)(2,1)} %param.15) | copy-start | bytes 196612
  3.6 27.7 %all-to-all-start = ((s32[128,1,128]{2,1,0:T(1,128)}), s32[128,1,128]{2,1,0:T(1,128)S(1)}, u32[]{:S(2)}, u32[]{:S(2)}) async-start(s32[128,1,128]{2,1,0:T(1,128)} %bitcast.40), calls=%async_computation | async-start | bytes 131072 | tf_op jit(solution)/shard_map/all_to_all | solution.py:305
  31.3 0.6 copy-start.3
  36.8 22.4 %all-to-all-start.1 = ((bf16[128,16,128]{2,1,0:T(8,128)(2,1)}), bf16[128,16,128]{2,1,0:T(8,128)(2,1)}, u32[]{:S(2)}, u32[]{:S(2)}) async-start(bf16[128,16,128]{2,1,0:T(8,128)(2,1)} %bitcast.36), calls=%async_computation.1 | async-start | bytes 1048576 | tf_op jit(solution)/shard_map/all_to_all | solution.py:305
  47.0 3.2 %copy-start.5 = (s32[2048]{0:T(1024)S(1)}, s32[2048]{0:T(1024)}, u32[]{:S(2)}) copy-start(s32[2048]{0:T(1024)} %param.12) | copy-start | bytes 24580
  84.1 18.8 %all-to-all-start.2 = ((bf16[128,16,128]{2,1,0:T(8,128)(2,1)}), bf16[128,16,128]{2,1,0:T(8,128)(2,1)}, u32[]{:S(2)}, u32[]{:S(2)}) async-start(bf16[128,16,128]{2,1,0:T(8,128)(2,1)} %bitcast.39), calls=%async_computation.2 | async-start | bytes 1048576 | tf_op jit(solution)/shard_map/all_to_all | solution.py:305
  126.6 3.7 %copy-start = (bf16[2,512,512]{2,1,0:T(8,128)(2,1)S(1)}, bf16[2,512,512]{2,1,0:T(8,128)(2,1)}, u32[]{:S(2)}) copy-start(bf16[2,512,512]{2,1,0:T(8,128)(2,1)} %param.18) | copy-start | bytes 3145732
  126.6 16.7 %all-to-all-start.3 = ((bf16[8,192,256]{2,1,0:T(8,128)(2,1)}), bf16[8,192,256]{2,1,0:T(8,128)(2,1)S(1)}, u32[]{:S(2)}, u32[]{:S(2)}) async-start(bf16[8,192,256]{2,1,0:T(8,128)(2,1)} %get-tuple-element.14), calls=%async_computation.3 | async-start | bytes 1572864 | tf_op jit(solution)/shard_map/all_to_all | solution.py:305
  143.3 0.9 copy-start.2
  158.5 10.8 %all-to-all-start.4 = ((bf16[8,64,256]{2,1,0:T(8,128)(2,1)}), bf16[8,64,256]{2,1,0:T(8,128)(2,1)S(1)}, u32[]{:S(2)}, u32[]{:S(2)}) async-start(bf16[8,64,256]{2,1,0:T(8,128)(2,1)} %coarse.2), calls=%async_computation.4 | async-start | bytes 524288 | tf_op jit(solution)/shard_map/all_to_all | solution.py:305
  169.4 0.7 copy-start.1
where the time goes:
time: 241 us; the launch traced here: 240 us
  Pallas kernels  127 us (53%)
  starting transfers between devices  34.4 us (14%)
  waiting for transfers between devices  33.3 us (14%)
  blocking collectives  28.9 us (12%)
  local copies, waits for them, and re-layouts  16.2 us (7%)
    all_to_all x5, starting transfers between devices, exchange(): return lax.all_to_all(value, axes, split_axis=0, concat_axis=0, tiled=True)  34.4 us
    all_to_all x5, waiting for transfers between devices, exchange(): return lax.all_to_all(value, axes, split_axis=0, concat_axis=0, tiled=True)  33.3 us
    all_to_all x2, blocking collectives, exchange(): return lax.all_to_all(value, axes, split_axis=0, concat_axis=0, tiled=True)  28.9 us
    pallas_call x2, Pallas kernels, shards(): call(coarse_kernel, shaped((subs, size, nodes), BF16), [smem(), vmem()],...  28.7 us
    pallas_call x1, Pallas kernels, shards(): call(second_kernel, shaped((own, channels), BF16), [smem()] + [vmem()] *...  24.9 us
    pallas_call x1, Pallas kernels, shards(): call(functools.partial(pool_kernel, bucket=bucket), (shaped((CHEADS, 3 *...  23.6 us
    pallas_call x1, Pallas kernels, shards(): call(last_kernel, shaped((own, channels), F32), [smem()] + [vmem()] * 5,...  22.2 us
    pallas_call x1, Pallas kernels, shards(): call(first_kernel, shaped((own, channels), F32), [vmem()] * 4, vmem(), fl...  14 us
  transfers between devices with their start and end apart: 5, of which 4 were waited for; matrix products, arithmetic and copies ran while one was open for 5% of the time, Pallas kernels for 7%

commit v1 on v0

v1 whole, which is shorter than its diff:
```python
import functools
import math

import jax
import jax.numpy as jnp
from jax import lax
from jax.experimental import pallas as pl
from jax.experimental.pallas import tpu as pltpu
from jax.sharding import PartitionSpec as P

HEADS = 4
CHEADS = 8
BALL = 256
GRAN = 32
LOG2E = 1.4426950408889634
NEG = -1e30
F32 = jnp.float32
BF16 = jnp.bfloat16


def vmem():
    return pl.BlockSpec(memory_space=pltpu.VMEM)


def smem():
    return pl.BlockSpec(memory_space=pltpu.SMEM)


def dot(a, b, dims=((1,), (0,))):
    return lax.dot_general(a, b, (dims, ((), ())), preferred_element_type=F32)


def call(kernel, out_shape, in_specs, out_specs, scratch=(), flops=0, nbytes=0, name=None, mib=16):
    return pl.pallas_call(
        kernel,
        out_shape=out_shape,
        in_specs=in_specs,
        out_specs=out_specs,
        scratch_shapes=list(scratch),
        cost_estimate=pl.CostEstimate(flops=flops, bytes_accessed=nbytes, transcendentals=0),
        compiler_params=pltpu.CompilerParams(vmem_limit_bytes=mib << 20),
        name=name,
    )


def ranks(classes, count):
    step = 256
    tri = (
        lax.broadcasted_iota(jnp.int32, (step, step), 0)
        <= lax.broadcasted_iota(jnp.int32, (step, step), 1)
    )
    tri = jnp.where(tri, 1.0, 0.0).astype(BF16)
    names = lax.broadcasted_iota(jnp.int32, (count, step), 0)
    carried = jnp.zeros((count, 1), F32)
    hots, found = [], []
    for row in classes:
        hot = jnp.where(names == row, 1.0, 0.0)
        hot16 = hot.astype(BF16)
        running = dot(hot16, tri) + carried
        found.append((jnp.sum(hot * running, axis=0, keepdims=True) - 1.0).astype(jnp.int32))
        hots.append(hot16)
        carried = running[:, step - 1 : step]
    return hots, found


def row_pairs(ref):
    return [
        jnp.concatenate([ref[2 * r : 2 * r + 1, :], ref[2 * r + 1 : 2 * r + 2, :]], axis=1)
        for r in range(ref.shape[0] // 2)
    ]


def store_pair(ref, r, value):
    ref[2 * r : 2 * r + 1, :] = value[:, :128]
    ref[2 * r + 1 : 2 * r + 2, :] = value[:, 128:]


def route_kernel(rot_ref, wanted_ref, slot_ref, *, own, devices):
    bucket = own // devices
    named = row_pairs(rot_ref)
    dest = [row // own for row in named]
    hots, found = ranks(dest, devices)
    lanes = lax.broadcasted_iota(jnp.int32, (bucket, 256), 0)
    total = jnp.zeros((devices, 2 * bucket), F32)
    for r, row in enumerate(named):
        store_pair(slot_ref, r, dest[r] * bucket + found[r])
        local = row % own
        here = lanes == found[r]
        high = jnp.where(here, (local // 64).astype(F32), 0.0)
        low = jnp.where(here, (local % 64).astype(F32), 0.0)
        parts = jnp.concatenate([high, low], axis=0).astype(BF16)
        total = total + dot(hots[r], parts, ((1,), (1,)))
    wanted = total[:, :bucket] * 64.0 + total[:, bucket:]
    wanted_ref[...] = jnp.zeros_like(wanted_ref)
    wanted_ref[:, :bucket] = wanted.astype(jnp.int32)


def place_kernel(pool_ref, place_ref, *, nodes):
    node = [row % nodes for row in row_pairs(pool_ref)]
    _, found = ranks(node, nodes)
    for r in range(len(node)):
        store_pair(place_ref, r, found[r] * nodes + node[r])


def norm_rows(x):
    centre = x - jnp.mean(x, axis=-1, keepdims=True)
    spread = jnp.mean(centre * centre, axis=-1, keepdims=True)
    return (centre * lax.rsqrt(spread + 1e-5)).astype(BF16)


def norm_columns(x):
    centre = x - jnp.mean(x, axis=0, keepdims=True)
    spread = jnp.mean(centre * centre, axis=0, keepdims=True)
    return (centre * lax.rsqrt(spread + 1e-5)).astype(BF16)


def ball(x, qkv_weight, out_weight):
    channels = x.shape[1]
    size = channels // HEADS
    normed = norm_rows(x)
    queries = dot(normed, qkv_weight[:, :channels]).astype(BF16)
    keys = dot(normed, qkv_weight[:, channels : 2 * channels]).astype(BF16)
    values = dot(normed, qkv_weight[:, 2 * channels :]).astype(BF16)
    values = jnp.concatenate([values, jnp.ones_like(values)], axis=1)
    head_of = lax.broadcasted_iota(jnp.int32, (1, channels), 1) // size
    summed = total = None
    for head in range(HEADS):
        mine = head_of == head
        scores = dot(jnp.where(mine, queries, jnp.zeros_like(queries)), keys, ((1,), (1,)))
        most = jnp.max(scores, axis=1, keepdims=True)
        weights = jnp.exp2((scores - most) * (LOG2E / math.sqrt(size))).astype(BF16)
        both = dot(weights, values)
        part, weight = both[:, :channels], both[:, channels:]
        summed = part if head == 0 else jnp.where(mine, part, summed)
        total = weight if head == 0 else jnp.where(mine, weight, total)
    return x + dot((summed / total).astype(BF16), out_weight)


def balls(x_ref, qkv_ref, out_ref, y_ref):
    together = 4

    def some(step, _):
        for j in range(together):
            rows = pl.ds(pl.multiple_of((step * together + j) * BALL, BALL), BALL)
            y_ref[rows, :] = ball(x_ref[rows, :], qkv_ref[...], out_ref[...])
        return 0

    lax.fori_loop(0, x_ref.shape[0] // (together * BALL), some, 0)


def first_kernel(x_ref, qkv_ref, out_ref, y_ref):
    balls(x_ref, qkv_ref.at[0], out_ref.at[0], y_ref)


def each_row(count, move):
    together = 64

    def some(step, _):
        for j in range(together):
            move(step * together + j)
        return 0

    lax.fori_loop(0, count // together, some, 0)


def each_slot(devices, bucket, move):
    together = 4

    def some(step, _):
        for i in range(together):
            for j in range(bucket):
                device = step * together + i
                move(device, j, device * bucket + j)
        return 0

    lax.fori_loop(0, devices // together, some, 0)


def answer_kernel(wanted_ref, x_ref, out_ref, rows_ref, *, bucket):
    def move(device, j, slot):
        rows_ref[pl.ds(slot, 1), :] = x_ref[pl.ds(wanted_ref[device, j], 1), :]

    each_slot(wanted_ref.shape[0], bucket, move)
    out_ref[...] = rows_ref[...].astype(BF16)


def second_kernel(slot_ref, x_ref, qkv_ref, out_ref, y_ref, slot_rows_ref, rows_ref):
    slot_rows_ref[...] = x_ref[...].astype(F32)

    def take(row):
        rows_ref[pl.ds(row, 1), :] = slot_rows_ref[pl.ds(slot_ref[row], 1), :]

    def give(row):
        slot_rows_ref[pl.ds(slot_ref[row], 1), :] = rows_ref[pl.ds(row, 1), :]

    each_row(rows_ref.shape[0], take)
    balls(rows_ref, qkv_ref.at[1], out_ref.at[1], rows_ref)
    each_row(rows_ref.shape[0], give)
    y_ref[...] = slot_rows_ref[...].astype(BF16)


def send_projected(features, weight_ref, layer, message_ref):
    normed = norm_columns(features)
    channels = features.shape[0]
    size = channels // CHEADS
    for part in range(3):
        projected = dot(weight_ref[layer, part * channels : (part + 1) * channels, :], normed).astype(BF16)
        for head in range(CHEADS):
            message_ref[head, part * size : (part + 1) * size, :] = projected[
                head * size : (head + 1) * size
            ]


def pool_kernel(
    wanted_ref, place_ref, x_ref, pool_ref, qkv_ref, message_ref, pooled_ref, placed_ref, from_ref, *, bucket
):
    from_ref[...] = x_ref[...].astype(F32)

    def move(device, j, slot):
        placed_ref[pl.ds(place_ref[wanted_ref[device, j]], 1), :] = from_ref[pl.ds(slot, 1), :]

    each_slot(wanted_ref.shape[0], bucket, move)
    nodes = x_ref.shape[0] // 8
    channels = x_ref.shape[1]
    pooled = None
    for k in range(8):
        part = dot(
            pool_ref[:, k * channels : (k + 1) * channels],
            placed_ref[k * nodes : (k + 1) * nodes, :].astype(BF16),
            ((1,), (1,)),
        )
        pooled = part if pooled is None else pooled + part
    pooled = pooled.astype(BF16).astype(F32)
    pooled_ref[...] = pooled
    send_projected(pooled, qkv_ref, 0, message_ref)


def coarse_kernel(counts_ref, x_ref, out_ref, keys_ref, values_ref, of_ref, first_ref, last_ref):
    tiles, parts, width = x_ref.shape
    size = parts // 3
    balls_here = counts_ref.shape[1]
    per_tile = width // GRAN
    together = 4
    scale = LOG2E / math.sqrt(size)
    for t in range(tiles):
        keys_ref[t] = x_ref[t, size : 2 * size, :].astype(F32).T.astype(BF16)
        values_ref[t] = jnp.concatenate([x_ref[t, 2 * size :, :], jnp.ones((16, width), BF16)], axis=0)
    start = 0
    ends = []
    for e in range(balls_here):
        end = start + counts_ref[0, e]

        def mark(block, _, e=e, start=start, end=end):
            of_ref[block] = e
            first_ref[block] = start
            last_ref[block] = end - 1
            return 0

        lax.fori_loop(start, end, mark, 0)
        ends.append(end)
        start = end

    def one(tile, _):
        queries = x_ref[tile, :size, :]
        blocks = tile * per_tile + lax.broadcasted_iota(jnp.int32, (1, width), 1) // GRAN
        own = jnp.zeros((1, width), jnp.int32)
        for e in range(balls_here):
            own = own + jnp.where(blocks >= ends[e], 1, 0)
        low = first_ref[tile * per_tile] // per_tile
        high = last_ref[tile * per_tile + per_tile - 1] // per_tile

        def add(step, carry):
            most, total = carry
            now = most
            chunks, chunk_scores = [], []
            for c in range(together):
                chunk = low + step * together + c
                live = chunk <= high
                chunk = jnp.minimum(chunk, high)
                scores = dot(keys_ref[chunk], queries)
                masked = []
                for g in range(per_tile):
                    ball_of = jnp.where(live, of_ref[chunk * per_tile + g], -1)
                    masked.append(jnp.where(own == ball_of, scores[g * GRAN : (g + 1) * GRAN], NEG))
                scores = jnp.concatenate(masked, axis=0)
                chunks.append(chunk)
                chunk_scores.append(scores)
                now = jnp.maximum(now, jnp.max(scores, axis=0, keepdims=True))
            total = total * jnp.exp2((most - now) * scale)
            for chunk, scores in zip(chunks, chunk_scores):
                weights = jnp.exp2((scores - now) * scale).astype(BF16)
                total = total + dot(values_ref[chunk], weights)
            return now, total

        begin = (jnp.full((1, width), NEG, F32), jnp.zeros((size + 16, width), F32))
        _, total = lax.fori_loop(0, (high - low + together) // together, add, begin)
        out_ref[tile] = (total[:size] / total[size : size + 1]).astype(BF16)
        return 0

    lax.fori_loop(0, tiles, one, 0)


def between_kernel(x_ref, features_ref, out_weight_ref, qkv_ref, message_ref, next_ref):
    heads, size, width = x_ref.shape
    features = features_ref[...] + dot(out_weight_ref[0], x_ref[...].reshape(heads * size, width))
    next_ref[...] = features
    send_projected(features, qkv_ref, 1, message_ref)


def last_kernel(place_ref, x_ref, features_ref, out_weight_ref, unpool_ref, placed_ref, out_ref, sum_ref):
    heads, size, width = x_ref.shape
    features = features_ref[...] + dot(out_weight_ref[1], x_ref[...].reshape(heads * size, width))
    features = features.astype(BF16).astype(F32)
    normed = norm_columns(features).astype(F32).T.astype(BF16)
    channels = placed_ref.shape[1]
    for k in range(8):
        rows = slice(k * width, (k + 1) * width)
        expanded = dot(normed, unpool_ref[:, k * channels : (k + 1) * channels])
        sum_ref[rows, :] = placed_ref[rows, :] + expanded

    def move(row):
        out_ref[pl.ds(row, 1), :] = sum_ref[pl.ds(place_ref[row], 1), :]

    each_row(out_ref.shape[0], move)


def shaped(shape, dtype):
    return jax.ShapeDtypeStruct(shape, dtype)


def exchange(value, axes):
    return lax.all_to_all(value, axes, split_axis=0, concat_axis=0, tiled=True)


def shards(
    beads,
    rot_perm,
    pool_ids,
    ball_counts,
    fine_qkv,
    fine_out,
    pool_weight,
    coarse_qkv,
    coarse_out,
    unpool_weight,
):
    own, channels = beads.shape
    both = ("leaf", "sub")
    subs = lax.axis_size("sub")
    devices = lax.axis_size("leaf") * subs
    bucket = own // devices
    nodes = own // 8
    wide = pool_weight.shape[1]
    size = wide // CHEADS
    wanted, slots = call(
        functools.partial(route_kernel, own=own, devices=devices),
        (shaped((devices, 128), jnp.int32), shaped((own // 128, 128), jnp.int32)),
        [vmem()],
        (vmem(), vmem()),
        flops=2 * devices * own * 256,
        nbytes=100000,
        name="route",
    )(rot_perm.reshape(own // 128, 128))
    requested = exchange(wanted.reshape(devices, 1, 128), both).reshape(devices, 128)
    places = call(
        functools.partial(place_kernel, nodes=nodes),
        shaped((own // 128, 128), jnp.int32),
        [vmem()],
        vmem(),
        flops=2 * nodes * own * 256,
        nbytes=20000,
        name="place",
    )(pool_ids.reshape(own // 128, 128))

    slots = slots.reshape(own)
    places = places.reshape(own)
    pool_turned = pool_weight.T
    coarse_turned = coarse_qkv.transpose(0, 2, 1)
    out_turned = coarse_out.transpose(0, 2, 1)
    ball_flops = own * channels * channels * 8 + own * BALL * channels * 16

    after_tree = call(
        first_kernel,
        shaped((own, channels), F32),
        [vmem()] * 3,
        vmem(),
        flops=ball_flops,
        nbytes=own * channels * 8,
        name="first",
    )(beads, fine_qkv, fine_out)
    answer = call(
        functools.partial(answer_kernel, bucket=bucket),
        shaped((own, channels), BF16),
        [smem(), vmem()],
        vmem(),
        [pltpu.VMEM((own, channels), F32)],
        nbytes=own * channels * 6,
        name="answer",
    )(requested, after_tree)
    arrived = exchange(answer.reshape(devices, bucket, channels), both).reshape(own, channels)
    outgoing = call(
        second_kernel,
        shaped((own, channels), BF16),
        [smem()] + [vmem()] * 3,
        vmem(),
        [pltpu.VMEM((own, channels), F32)] * 2,
        flops=ball_flops,
        nbytes=own * channels * 4,
        name="second",
    )(slots, arrived, fine_qkv, fine_out)
    coming = exchange(outgoing.reshape(devices, bucket, channels), both).reshape(own, channels)
    message, features, placed = call(
        functools.partial(pool_kernel, bucket=bucket),
        (
            shaped((CHEADS, 3 * size, nodes), BF16),
            shaped((wide, nodes), F32),
            shaped((own, channels), F32),
        ),
        [smem(), smem()] + [vmem()] * 3,
        (vmem(), vmem(), vmem()),
        [pltpu.VMEM((own, channels), F32)],
        flops=2 * nodes * wide * (own // 2 + 3 * wide),
        nbytes=own * channels * 8,
        name="pool",
    )(requested, places, coming, pool_turned, coarse_turned)
    for layer in range(2):
        received = exchange(message, "sub")
        attended = call(
            coarse_kernel,
            shaped((subs, size, nodes), BF16),
            [smem(), vmem()],
            vmem(),
            [pltpu.VMEM((subs, nodes, size), BF16), pltpu.VMEM((subs, size + 16, nodes), BF16)]
            + [pltpu.SMEM((subs * nodes // GRAN,), jnp.int32)] * 3,
            flops=subs * nodes * nodes * 3 * size * 4,
            nbytes=subs * nodes * size * 8,
            name="coarse",
        )(ball_counts, received)
        back = exchange(attended, "sub")
        if layer == 0:
            message, features = call(
                between_kernel,
                (shaped((CHEADS, 3 * size, nodes), BF16), shaped((wide, nodes), F32)),
                [vmem()] * 4,
                (vmem(), vmem()),
                flops=2 * nodes * wide * 4 * wide,
                nbytes=nodes * wide * 8,
                name="between",
            )(back, features, out_turned, coarse_turned)
    return call(
        last_kernel,
        shaped((own, channels), F32),
        [smem()] + [vmem()] * 5,
        vmem(),
        [pltpu.VMEM((own, channels), F32)],
        flops=2 * nodes * wide * 3 * wide,
        nbytes=own * channels * 8,
        name="last",
    )(places, back, features, out_turned, unpool_weight, placed)


def solution(mesh):
    placed = (
        P(("leaf", "sub"), None),
        P(("leaf", "sub")),
        P(("leaf", "sub")),
        P("leaf", None),
        P(),
        P(),
        P(),
        P(),
        P(),
        P(),
    )
    return jax.shard_map(
        shards, mesh=mesh, in_specs=placed, out_specs=P(("leaf", "sub"), None), check_vma=False
    )
```

time: 241 us -> 167 us (0.69)
  the two profiles are of different devices: /device:TPU:6 before, /device:TPU:1 now
where the time goes in v1:
time: 167 us; the launch traced here: 165 us
  blocking collectives  64.2 us (38%)
  Pallas kernels  51.1 us (31%)
  starting transfers between devices  21.4 us (13%)
  local copies, waits for them, and re-layouts  16.6 us (10%)
  waiting for transfers between devices  11.2 us (7%)
    all_to_all x4, blocking collectives, exchange(): return lax.all_to_all(value, axes, split_axis=0, concat_axis=0, tiled=True)  64.2 us
    all_to_all x3, starting transfers between devices, exchange(): return lax.all_to_all(value, axes, split_axis=0, concat_axis=0, tiled=True)  21.4 us
    unnamed x37, local copies, waits for them, and re-layouts  16.6 us
    pallas_call x2, Pallas kernels, shards(): call(coarse_kernel, shaped((subs, size, nodes), BF16), [smem(), vmem()],...  13.5 us
    pallas_call x1, Pallas kernels, shards(): call(second_kernel, shaped((own, channels), BF16), [smem()] + [vmem()] *...  11.9 us
    all_to_all x3, waiting for transfers between devices, exchange(): return lax.all_to_all(value, axes, split_axis=0, concat_axis=0, tiled=True)  11.2 us
    pallas_call x1, Pallas kernels, shards(): call(functools.partial(pool_kernel, bucket=bucket), (shaped((CHEADS, 3 *...  7.13 us
    pallas_call x1, Pallas kernels, shards(): call(first_kernel, shaped((own, channels), F32), [vmem()] * 3, vmem(), fl...  6.77 us
  transfers between devices with their start and end apart: 3, of which 2 were waited for; matrix products, arithmetic and copies ran while one was open for 5% of the time, Pallas kernels for 5%

profile of v1, /device:TPU:1, one launch (start us, length us, event | category | flops | bytes accessed | tf_op | source)
XLA Modules:
  0.0 164.7 jit_solution(12899432469352703066)
XLA Ops:
  0.0 0.7 copy-done.14
  0.7 1.6 route.1
  2.3 11.5 %all-to-all-start = ((s32[128,1,128]{2,1,0:T(1,128)}), s32[128,1,128]{2,1,0:T(1,128)S(1)}, u32[]{:S(2)}, u32[]{:S(2)}) async-start(s32[128,1,128]{2,1,0:T(1,128)} %bitcast.4), calls=%async_computation | async-start | bytes 131072 | tf_op jit(solution)/shard_map/all_to_all | solution.py:332
  13.8 1.2 copy-done.9
  15.0 0.9 copy-done.10
  15.9 0.8 copy-done.12
  16.8 6.8 %first.1.x_ref = f32[2048,128]{1,0:T(8,128)S(1)} custom-call(f32[2048,128]{1,0:T(8,128)S(1)} %copy-done.9, bf16[2,128,384]{2,1,0:T(8,128)(2,1)S(1)} %copy-done.10, bf16[2,128,128]{2,1,0:T(8,128)(2,1)S(1)} %copy-done.12), custom_call_target="tpu_custom_call" | custom-call | flops 1342177280 | bytes 2097152 | tf_op jit(solution)/shard_map/first/pallas_call | solution.py:382
  23.6 3.4 %answer.1 = bf16[2048,128]{1,0:T(8,128)(2,1)S(1)} custom-call(s32[128,128]{1,0:T(8,128)S(1)} %bitcast.21, f32[2048,128]{1,0:T(8,128)S(1)} %first.1.x_ref), custom_call_target="tpu_custom_call" | custom-call | bytes 1572864 | tf_op jit(solution)/shard_map/answer/pallas_call | solution.py:391
  27.0 23.1 %all_to_all.35 = bf16[128,16,128]{2,1,0:T(8,128)(2,1)S(1)} all-to-all(bf16[128,16,128]{2,1,0:T(8,128)(2,1)S(1)} %bitcast.20), channel_id=1, replica_groups=mesh['leaf'=16,'sub'=8] {'leaf','sub'}, dimensions={0} | all-to-all | bytes 1048576 | tf_op jit(solution)/shard_map/all_to_all | solution.py:332
  50.0 11.9 %second.1 = bf16[2048,128]{1,0:T(8,128)(2,1)} custom-call(s32[2048]{0:T(1024)S(1)} %bitcast.28, bf16[2048,128]{1,0:T(8,128)(2,1)S(1)} %bitcast.23, bf16[2,128,384]{2,1,0:T(8,128)(2,1)S(1)} %copy-done.11, bf16[2,128,128]{2,1,0:T(8,128)(2,1)S(1)} %copy-done.13), custom_call_target="tpu_custom_call" | custom-call | flops 1342177280 | bytes 1048576 | tf_op jit(solution)/shard_map/second/pallas_call | solution.py:401
  61.9 5.6 %all-to-all-start.2 = ((bf16[128,16,128]{2,1,0:T(8,128)(2,1)}), bf16[128,16,128]{2,1,0:T(8,128)(2,1)}, u32[]{:S(2)}, u32[]{:S(2)}) async-start(bf16[128,16,128]{2,1,0:T(8,128)(2,1)} %bitcast.9), calls=%async_computation.2 | async-start | bytes 1048576 | tf_op jit(solution)/shard_map/all_to_all | solution.py:332
  67.5 0.0 copy-start.15
  67.5 3.2 %copy.16 = bf16[2,512,1536]{1,2,0:T(8,128)(2,1)S(1)} copy(bf16[2,512,1536]{2,1,0:T(8,128)(2,1)} %param.17) | data formatting | bytes 6291456 | tf_op args[7]
  70.7 2.3 %copy.15 = bf16[1024,512]{0,1:T(8,128)(2,1)} copy(bf16[1024,512]{1,0:T(8,128)(2,1)} %param.16) | data formatting | bytes 2097152 | tf_op args[6]
  73.0 0.8 place.1
  73.8 7.0 %all-to-all-done.2 = bf16[128,16,128]{2,1,0:T(8,128)(2,1)} async-done(((bf16[128,16,128]{2,1,0:T(8,128)(2,1)}), bf16[128,16,128]{2,1,0:T(8,128)(2,1)}, u32[]{:S(2)}, u32[]{:S(2)}) %all-to-all-start.2) | async-done | bytes 524320 | tf_op jit(solution)/shard_map/all_to_all | solution.py:332
  80.8 1.2 copy-done.2
  82.0 7.1 %pool.1 = (bf16[8,192,256]{2,1,0:T(8,128)(2,1)S(1)}, f32[512,256]{1,0:T(8,128)S(1)}, f32[2048,128]{1,0:T(8,128)S(1)}) custom-call(s32[128,128]{1,0:T(8,128)S(1)} %bitcast.22, s32[2048]{0:T(1024)S(1)} %bitcast.24, bf16[2048,128]{1,0:T(8,128)(2,1)} %bitcast.10.x_ref, bf16[512,1024]{1,0:T(8,128)(2,1)S(1)} %bitcast.19, bf16[2,1536,512]{2,1,0:T(8,128)(2,1)S(1)} %bitcast.15), custom_call_target="tpu_custom_call" | custom-call | flops 671088640 | bytes 2097152 | tf_op jit(solution)/shard_map/pool/pallas_call | solution.py:412
  89.2 1.0 copy-done.4
  90.2 15.6 %all_to_all.36.x_ref = bf16[8,192,256]{2,1,0:T(8,128)(2,1)S(1)} all-to-all(bf16[8,192,256]{2,1,0:T(8,128)(2,1)S(1)} %get-tuple-element.14), channel_id=1, replica_groups=mesh['leaf'=16,'sub'=8] {'sub'}, dimensions={0} | all-to-all | bytes 1572864 | tf_op jit(solution)/shard_map/all_to_all | solution.py:332
  105.8 6.8 %coarse.2 = bf16[8,64,256]{2,1,0:T(8,128)(2,1)S(1)} custom-call(s32[1,8]{1,0:T(1,128)S(1)} %copy-done.16, bf16[8,192,256]{2,1,0:T(8,128)(2,1)S(1)} %all_to_all.36.x_ref), custom_call_target="tpu_custom_call" | custom-call | flops 402653184 | bytes 1048576 | tf_op jit(solution)/shard_map/coarse/pallas_call | solution.py:428
  112.6 0.7 copy-done.8
  113.3 4.3 %all-to-all-start.4 = ((bf16[8,64,256]{2,1,0:T(8,128)(2,1)}), bf16[8,64,256]{2,1,0:T(8,128)(2,1)S(1)}, u32[]{:S(2)}, u32[]{:S(2)}) async-start(bf16[8,64,256]{2,1,0:T(8,128)(2,1)} %copy-done.8), calls=%async_computation.4 | async-start | bytes 524288 | tf_op jit(solution)/shard_map/all_to_all | solution.py:332
  117.7 2.3 %copy.17 = bf16[2,512,512]{1,2,0:T(8,128)(2,1)} copy(bf16[2,512,512]{2,1,0:T(8,128)(2,1)} %param.18) | data formatting | bytes 2097152 | tf_op args[8]
  120.0 4.2 %all-to-all-done.4.x_ref = bf16[8,64,256]{2,1,0:T(8,128)(2,1)S(1)} async-done(((bf16[8,64,256]{2,1,0:T(8,128)(2,1)}), bf16[8,64,256]{2,1,0:T(8,128)(2,1)S(1)}, u32[]{:S(2)}, u32[]{:S(2)}) %all-to-all-start.4) | async-done | bytes 262176 | tf_op jit(solution)/shard_map/all_to_all | solution.py:332
  124.2 1.2 copy-done
  125.4 1.0 copy-done.7
  126.5 1.2 between.1
  127.7 15.6 %all_to_all.37.x_ref = bf16[8,192,256]{2,1,0:T(8,128)(2,1)S(1)} all-to-all(bf16[8,192,256]{2,1,0:T(8,128)(2,1)S(1)} %get-tuple-element.16), channel_id=1, replica_groups=mesh['leaf'=16,'sub'=8] {'sub'}, dimensions={0} | all-to-all | bytes 1572864 | tf_op jit(solution)/shard_map/all_to_all | solution.py:332
  143.3 6.6 %coarse.3 = bf16[8,64,256]{2,1,0:T(8,128)(2,1)S(1)} custom-call(s32[1,8]{1,0:T(1,128)S(1)} %copy-done.16, bf16[8,192,256]{2,1,0:T(8,128)(2,1)S(1)} %all_to_all.37.x_ref), custom_call_target="tpu_custom_call" | custom-call | flops 402653184 | bytes 1048576 | tf_op jit(solution)/shard_map/coarse/pallas_call | solution.py:428
  149.9 9.9 %all_to_all.38.x_ref = bf16[8,64,256]{2,1,0:T(8,128)(2,1)S(1)} all-to-all(bf16[8,64,256]{2,1,0:T(8,128)(2,1)S(1)} %coarse.3), channel_id=1, replica_groups=mesh['leaf'=16,'sub'=8] {'sub'}, dimensions={0} | all-to-all | bytes 524288 | tf_op jit(solution)/shard_map/all_to_all | solution.py:332
  159.8 4.8 %last.1 = f32[2048,128]{1,0:T(8,128)} custom-call(s32[2048]{0:T(1024)S(1)} %bitcast.25, bf16[8,64,256]{2,1,0:T(8,128)(2,1)S(1)} %all_to_all.38.x_ref, f32[512,256]{1,0:T(8,128)S(1)} %get-tuple-element.17.features_ref, bf16[2,512,512]{2,1,0:T(8,128)(2,1)S(1)} %bitcast.18, bf16[512,1024]{1,0:T(8,128)(2,1)S(1)} %copy-done.3, f32[2048,128]{1,0:T(8,128)S(1)} %copy-done.5), custom_call_target="tpu_custom_call" | custom-call | flops 402653184 | bytes 2097152 | tf_op jit(solution)/shard_map/last/pallas_call | solution.py:450
  (25 shorter events, 0.0 us)
Async XLA Ops:
  0.0 0.7 copy-start.14
  2.3 21.3 %all-to-all-start = ((s32[128,1,128]{2,1,0:T(1,128)}), s32[128,1,128]{2,1,0:T(1,128)S(1)}, u32[]{:S(2)}, u32[]{:S(2)}) async-start(s32[128,1,128]{2,1,0:T(1,128)} %bitcast.4), calls=%async_computation | async-start | bytes 131072 | tf_op jit(solution)/shard_map/all_to_all | solution.py:332
  13.8 1.2 copy-start.9
  15.0 0.9 copy-start.10
  15.9 0.8 copy-start.12
  16.8 33.3 %copy-start.11 = (bf16[2,128,384]{2,1,0:T(8,128)(2,1)S(1)}, bf16[2,128,384]{2,1,0:T(8,128)(2,1)}, u32[]{:S(2)}) copy-start(bf16[2,128,384]{2,1,0:T(8,128)(2,1)} %qkv_ref.3) | copy-start | bytes 589828
  16.8 33.3 %copy-start.13 = (bf16[2,128,128]{2,1,0:T(8,128)(2,1)S(1)}, bf16[2,128,128]{2,1,0:T(8,128)(2,1)}, u32[]{:S(2)}) copy-start(bf16[2,128,128]{2,1,0:T(8,128)(2,1)} %out_ref.3) | copy-start | bytes 196612
  61.9 18.8 %all-to-all-start.2 = ((bf16[128,16,128]{2,1,0:T(8,128)(2,1)}), bf16[128,16,128]{2,1,0:T(8,128)(2,1)}, u32[]{:S(2)}, u32[]{:S(2)}) async-start(bf16[128,16,128]{2,1,0:T(8,128)(2,1)} %bitcast.9), calls=%async_computation.2 | async-start | bytes 1048576 | tf_op jit(solution)/shard_map/all_to_all | solution.py:332
  67.5 5.5 %copy-start.15 = (s32[2048]{0:T(1024)S(1)}, s32[2048]{0:T(1024)}, u32[]{:S(2)}) copy-start(s32[2048]{0:T(1024)} %param.12) | copy-start | bytes 24580
  80.8 1.2 copy-start.2
  82.0 23.8 %copy-start.16 = (s32[1,8]{1,0:T(1,128)S(1)}, s32[1,8]{1,0:T(1,128)}, u32[]{:S(2)}) copy-start(s32[1,8]{1,0:T(1,128)} %counts_ref.3) | copy-start | bytes 100
  89.1 1.0 copy-start.4
  90.2 15.6 %copy-start.6 = (f32[512,256]{1,0:T(8,128)}, f32[512,256]{1,0:T(8,128)S(1)}, u32[]{:S(2)}) copy-start(f32[512,256]{1,0:T(8,128)S(1)} %get-tuple-element.15.features_ref) | copy-start | bytes 1572868
  112.6 0.7 copy-start.8
  113.3 10.8 %all-to-all-start.4 = ((bf16[8,64,256]{2,1,0:T(8,128)(2,1)}), bf16[8,64,256]{2,1,0:T(8,128)(2,1)S(1)}, u32[]{:S(2)}, u32[]{:S(2)}) async-start(bf16[8,64,256]{2,1,0:T(8,128)(2,1)} %copy-done.8), calls=%async_computation.4 | async-start | bytes 524288 | tf_op jit(solution)/shard_map/all_to_all | solution.py:332
  124.2 1.2 copy-start
  125.4 1.0 copy-start.7
  126.5 33.4 %copy-start.1 = (bf16[2,512,512]{1,2,0:T(8,128)(2,1)S(1)}, bf16[2,512,512]{1,2,0:T(8,128)(2,1)}, u32[]{:S(2)}) copy-start(bf16[2,512,512]{1,2,0:T(8,128)(2,1)} %copy.17) | copy-start | bytes 3145732
  126.5 33.4 %copy-start.3 = (bf16[512,1024]{1,0:T(8,128)(2,1)S(1)}, bf16[512,1024]{1,0:T(8,128)(2,1)}, u32[]{:S(2)}) copy-start(bf16[512,1024]{1,0:T(8,128)(2,1)} %unpool_ref.1) | copy-start | bytes 3145732
  126.5 33.4 %copy-start.5 = (f32[2048,128]{1,0:T(8,128)S(1)}, f32[2048,128]{1,0:T(8,128)}, u32[]{:S(2)}) copy-start(f32[2048,128]{1,0:T(8,128)} %copy-done.4) | copy-start | bytes 3145732

commit v2 on v1

--- a/solution.py
+++ b/solution.py
@@ -24,6 +24,16 @@
 
 def smem():
     return pl.BlockSpec(memory_space=pltpu.SMEM)
+
+
+def hbm():
+    return pl.BlockSpec(memory_space=pltpu.HBM)
+
+
+def fetch(source, target, sem):
+    copy = pltpu.make_async_copy(source, target, sem)
+    copy.start()
+    return copy
 
 
 def dot(a, b, dims=((1,), (0,))):
@@ -136,20 +146,21 @@
     return x + dot((summed / total).astype(BF16), out_weight)
 
 
-def balls(x_ref, qkv_ref, out_ref, y_ref):
-    together = 4
-
-    def some(step, _):
-        for j in range(together):
-            rows = pl.ds(pl.multiple_of((step * together + j) * BALL, BALL), BALL)
-            y_ref[rows, :] = ball(x_ref[rows, :], qkv_ref[...], out_ref[...])
-        return 0
-
-    lax.fori_loop(0, x_ref.shape[0] // (together * BALL), some, 0)
-
-
-def first_kernel(x_ref, qkv_ref, out_ref, y_ref):
-    balls(x_ref, qkv_ref.at[0], out_ref.at[0], y_ref)
+def first_kernel(x_ref, qkv_ref, out_ref, y_ref, held_ref, qkv_held, out_held, sems):
+    rows = held_ref.shape[1]
+    weights = [fetch(qkv_ref.at[0], qkv_held, sems.at[0]), fetch(out_ref.at[0], out_held, sems.at[1])]
+    parts = [
+        fetch(x_ref.at[pl.ds(p * rows, rows), :], held_ref.at[p], sems.at[2 + p])
+        for p in range(held_ref.shape[0])
+    ]
+    for copy in weights:
+        copy.wait()
+    for p, copy in enumerate(parts):
+        copy.wait()
+        for j in range(rows // BALL):
+            mine = slice(j * BALL, (j + 1) * BALL)
+            at = p * rows + j * BALL
+            y_ref[at : at + BALL, :] = ball(held_ref[p, mine, :], qkv_held[...], out_held[...])
 
 
 def each_row(count, move):
@@ -163,48 +174,57 @@
     lax.fori_loop(0, count // together, some, 0)
 
 
-def each_slot(devices, bucket, move):
-    together = 4
+def answer_kernel(wanted_ref, x_ref, out_ref, named_ref, rows_ref, index_ref, sem, *, bucket):
+    devices = wanted_ref.shape[0]
+    per_row = 128 // bucket
+    named_ref[...] = jnp.concatenate(
+        [wanted_ref[pl.ds(i, devices // per_row, stride=per_row), :][:, :bucket] for i in range(per_row)],
+        axis=1,
+    )
+    fetch(named_ref, index_ref, sem).wait()
 
     def some(step, _):
-        for i in range(together):
-            for j in range(bucket):
-                device = step * together + i
-                move(device, j, device * bucket + j)
+        for j in range(128):
+            rows_ref[pl.ds(step * 128 + j, 1), :] = x_ref[pl.ds(index_ref[step, j], 1), :]
         return 0
 
-    lax.fori_loop(0, devices // together, some, 0)
-
-
-def answer_kernel(wanted_ref, x_ref, out_ref, rows_ref, *, bucket):
-    def move(device, j, slot):
-        rows_ref[pl.ds(slot, 1), :] = x_ref[pl.ds(wanted_ref[device, j], 1), :]
-
-    each_slot(wanted_ref.shape[0], bucket, move)
+    lax.fori_loop(0, index_ref.shape[0], some, 0)
     out_ref[...] = rows_ref[...].astype(BF16)
 
 
-def second_kernel(slot_ref, x_ref, qkv_ref, out_ref, y_ref, slot_rows_ref, rows_ref):
-    slot_rows_ref[...] = x_ref[...].astype(F32)
-
-    def take(row):
-        rows_ref[pl.ds(row, 1), :] = slot_rows_ref[pl.ds(slot_ref[row], 1), :]
-
-    def give(row):
-        slot_rows_ref[pl.ds(slot_ref[row], 1), :] = rows_ref[pl.ds(row, 1), :]
-
-    each_row(rows_ref.shape[0], take)
-    balls(rows_ref, qkv_ref.at[1], out_ref.at[1], rows_ref)
-    each_row(rows_ref.shape[0], give)
-    y_ref[...] = slot_rows_ref[...].astype(BF16)
-
-
-def send_projected(features, weight_ref, layer, message_ref):
+def second_kernel(slot_ref, x_ref, qkv_ref, out_ref, y_ref, from_ref, to_ref, in0, in1, out0, out1):
+    ins, outs = (in0, in1), (out0, out1)
+    count = x_ref.shape[0] // BALL
+    from_ref[...] = x_ref[...].astype(F32)
+
+    def take_first(row):
+        in0[pl.ds(row, 1), :] = from_ref[pl.ds(slot_ref[row], 1), :]
+
+    def give_last(row):
+        slot = slot_ref[(count - 1) * BALL + row]
+        to_ref[pl.ds(slot, 1), :] = outs[(count - 1) % 2][pl.ds(row, 1), :]
+
+    each_row(BALL, take_first)
+    for at in range(count):
+        if at + 1 < count:
+            for j in range(BALL):
+                slot = slot_ref[(at + 1) * BALL + j]
+                ins[(at + 1) % 2][j : j + 1, :] = from_ref[pl.ds(slot, 1), :]
+        outs[at % 2][...] = ball(ins[at % 2][...], qkv_ref[1], out_ref[1])
+        if at:
+            for j in range(BALL):
+                slot = slot_ref[(at - 1) * BALL + j]
+                to_ref[pl.ds(slot, 1), :] = outs[(at - 1) % 2][j : j + 1, :]
+    each_row(BALL, give_last)
+    y_ref[...] = to_ref[...].astype(BF16)
+
+
+def send_projected(features, weight_ref, message_ref):
     normed = norm_columns(features)
     channels = features.shape[0]
     size = channels // CHEADS
     for part in range(3):
-        projected = dot(weight_ref[layer, part * channels : (part + 1) * channels, :], normed).astype(BF16)
+        projected = dot(weight_ref[part * channels : (part + 1) * channels, :], normed).astype(BF16)
         for head in range(CHEADS):
             message_ref[head, part * size : (part + 1) * size, :] = projected[
                 head * size : (head + 1) * size
@@ -212,27 +232,48 @@
 
 
 def pool_kernel(
-    wanted_ref, place_ref, x_ref, pool_ref, qkv_ref, message_ref, pooled_ref, placed_ref, from_ref, *, bucket
+    named_ref,
+    place_ref,
+    x_ref,
+    pool_ref,
+    qkv_ref,
+    message_ref,
+    pooled_ref,
+    placed_ref,
+    from_ref,
+    rows_ref,
+    pool_held,
+    qkv_held,
+    pooled_held,
+    sems,
 ):
+    pool_copy = fetch(pool_ref, pool_held, sems.at[0])
+    qkv_copy = fetch(qkv_ref.at[0], qkv_held, sems.at[1])
     from_ref[...] = x_ref[...].astype(F32)
 
-    def move(device, j, slot):
-        placed_ref[pl.ds(place_ref[wanted_ref[device, j]], 1), :] = from_ref[pl.ds(slot, 1), :]
-
-    each_slot(wanted_ref.shape[0], bucket, move)
+    def move(slot):
+        rows_ref[pl.ds(place_ref[named_ref[slot]], 1), :] = from_ref[pl.ds(slot, 1), :]
+
+    each_row(from_ref.shape[0], move)
+    placed_copy = fetch(rows_ref, placed_ref, sems.at[2])
     nodes = x_ref.shape[0] // 8
     channels = x_ref.shape[1]
+    pool_copy.wait()
     pooled = None
     for k in range(8):
         part = dot(
-            pool_ref[:, k * channels : (k + 1) * channels],
-            placed_ref[k * nodes : (k + 1) * nodes, :].astype(BF16),
+            pool_held[:, k * channels : (k + 1) * channels],
+            rows_ref[k * nodes : (k + 1) * nodes, :].astype(BF16),
             ((1,), (1,)),
         )
         pooled = part if pooled is None else pooled + part
-    pooled = pooled.astype(BF16).astype(F32)
-    pooled_ref[...] = pooled
-    send_projected(pooled, qkv_ref, 0, message_ref)
+    pooled = pooled.astype(BF16)
+    pooled_held[...] = pooled
+    pooled_copy = fetch(pooled_held, pooled_ref, sems.at[3])
+    qkv_copy.wait()
+    send_projected(pooled.astype(F32), qkv_held, message_ref)
+    placed_copy.wait()
+    pooled_copy.wait()
 
 
 def coarse_kernel(counts_ref, x_ref, out_ref, keys_ref, values_ref, of_ref, first_ref, last_ref):
@@ -300,23 +341,56 @@
     lax.fori_loop(0, tiles, one, 0)
 
 
-def between_kernel(x_ref, features_ref, out_weight_ref, qkv_ref, message_ref, next_ref):
+def between_kernel(
+    x_ref, features_ref, turned_ref, qkv_ref, message_ref, next_ref, features_held, out_held, qkv_held, next_held, sems
+):
+    out_copy = fetch(turned_ref.at[0], out_held, sems.at[0])
+    features_copy = fetch(features_ref, features_held, sems.at[1])
+    qkv_copy = fetch(qkv_ref.at[1], qkv_held, sems.at[2])
     heads, size, width = x_ref.shape
-    features = features_ref[...] + dot(out_weight_ref[0], x_ref[...].reshape(heads * size, width))
-    next_ref[...] = features
-    send_projected(features, qkv_ref, 1, message_ref)
-
-
-def last_kernel(place_ref, x_ref, features_ref, out_weight_ref, unpool_ref, placed_ref, out_ref, sum_ref):
+    out_copy.wait()
+    added = dot(out_held[...], x_ref[...].reshape(heads * size, width))
+    features_copy.wait()
+    features = features_held[...].astype(F32) + added
+    next_held[...] = features
+    next_copy = fetch(next_held, next_ref, sems.at[3])
+    qkv_copy.wait()
+    send_projected(features, qkv_held, message_ref)
+    next_copy.wait()
+
+
+def last_kernel(
+    place_ref,
+    x_ref,
+    features_ref,
+    turned_ref,
+    unpool_ref,
+    placed_ref,
+    out_ref,
+    sum_ref,
+    features_held,
+    out_held,
+    unpool_held,
+    placed_held,
+    sems,
+):
+    out_copy = fetch(turned_ref.at[1], out_held, sems.at[0])
+    features_copy = fetch(features_ref, features_held, sems.at[1])
+    unpool_copy = fetch(unpool_ref, unpool_held, sems.at[2])
+    placed_copy = fetch(placed_ref, placed_held, sems.at[3])
     heads, size, width = x_ref.shape
-    features = features_ref[...] + dot(out_weight_ref[1], x_ref[...].reshape(heads * size, width))
-    features = features.astype(BF16).astype(F32)
+    out_copy.wait()
+    added = dot(out_held[...], x_ref[...].reshape(heads * size, width))
+    features_copy.wait()
+    features = (features_held[...] + added).astype(BF16).astype(F32)
     normed = norm_columns(features).astype(F32).T.astype(BF16)
     channels = placed_ref.shape[1]
+    unpool_copy.wait()
+    placed_copy.wait()
     for k in range(8):
         rows = slice(k * width, (k + 1) * width)
-        expanded = dot(normed, unpool_ref[:, k * channels : (k + 1) * channels])
-        sum_ref[rows, :] = placed_ref[rows, :] + expanded
+        expanded = dot(normed, unpool_held[:, k * channels : (k + 1) * channels])
+        sum_ref[rows, :] = placed_held[rows, :] + expanded
 
     def move(row):
         out_ref[pl.ds(row, 1), :] = sum_ref[pl.ds(place_ref[row], 1), :]
@@ -374,55 +448,76 @@
 
     slots = slots.reshape(own)
     places = places.reshape(own)
-    pool_turned = pool_weight.T
-    coarse_turned = coarse_qkv.transpose(0, 2, 1)
-    out_turned = coarse_out.transpose(0, 2, 1)
     ball_flops = own * channels * channels * 8 + own * BALL * channels * 16
 
     after_tree = call(
         first_kernel,
         shaped((own, channels), F32),
-        [vmem()] * 3,
+        [hbm()] * 3,
         vmem(),
+        [
+            pltpu.VMEM((2, own // 2, channels), F32),
+            pltpu.VMEM((channels, 3 * channels), BF16),
+            pltpu.VMEM((channels, channels), BF16),
+            pltpu.SemaphoreType.DMA((4,)),
+        ],
         flops=ball_flops,
         nbytes=own * channels * 8,
         name="first",
     )(beads, fine_qkv, fine_out)
-    answer = call(
+    answer, named = call(
         functools.partial(answer_kernel, bucket=bucket),
-        shaped((own, channels), BF16),
-        [smem(), vmem()],
-        vmem(),
-        [pltpu.VMEM((own, channels), F32)],
+        (shaped((own, channels), BF16), shaped((own // 128, 128), jnp.int32)),
+        [vmem(), vmem()],
+        (vmem(), vmem()),
+        [
+            pltpu.VMEM((own, channels), F32),
+            pltpu.SMEM((own // 128, 128), jnp.int32),
+            pltpu.SemaphoreType.DMA(()),
+        ],
         nbytes=own * channels * 6,
         name="answer",
     )(requested, after_tree)
+    named = named.reshape(own)
     arrived = exchange(answer.reshape(devices, bucket, channels), both).reshape(own, channels)
     outgoing = call(
         second_kernel,
         shaped((own, channels), BF16),
         [smem()] + [vmem()] * 3,
         vmem(),
-        [pltpu.VMEM((own, channels), F32)] * 2,
+        [pltpu.VMEM((own, channels), F32)] * 2 + [pltpu.VMEM((BALL, channels), F32)] * 4,
         flops=ball_flops,
         nbytes=own * channels * 4,
         name="second",
     )(slots, arrived, fine_qkv, fine_out)
     coming = exchange(outgoing.reshape(devices, bucket, channels), both).reshape(own, channels)
+    pool_turned = pool_weight.T
+    qkv_turned = coarse_qkv.transpose(0, 2, 1)
+    out_turned = coarse_out.transpose(0, 2, 1)
+    coming, pool_turned, qkv_turned, out_turned = lax.optimization_barrier(
+        (coming, pool_turned, qkv_turned, out_turned)
+    )
     message, features, placed = call(
-        functools.partial(pool_kernel, bucket=bucket),
+        pool_kernel,
         (
             shaped((CHEADS, 3 * size, nodes), BF16),
-            shaped((wide, nodes), F32),
+            shaped((wide, nodes), BF16),
             shaped((own, channels), F32),
         ),
-        [smem(), smem()] + [vmem()] * 3,
-        (vmem(), vmem(), vmem()),
-        [pltpu.VMEM((own, channels), F32)],
+        [smem(), smem(), vmem(), hbm(), hbm()],
+        (vmem(), hbm(), hbm()),
+        [
+            pltpu.VMEM((own, channels), F32),
+            pltpu.VMEM((own, channels), F32),
+            pltpu.VMEM((wide, own // 2), BF16),
+            pltpu.VMEM((3 * wide, wide), BF16),
+            pltpu.VMEM((wide, nodes), BF16),
+            pltpu.SemaphoreType.DMA((4,)),
+        ],
         flops=2 * nodes * wide * (own // 2 + 3 * wide),
         nbytes=own * channels * 8,
         name="pool",
-    )(requested, places, coming, pool_turned, coarse_turned)
+    )(named, places, coming, pool_turned, qkv_turned)
     for layer in range(2):
         received = exchange(message, "sub")
         attended = call(
@@ -441,18 +536,32 @@
             message, features = call(
                 between_kernel,
                 (shaped((CHEADS, 3 * size, nodes), BF16), shaped((wide, nodes), F32)),
-                [vmem()] * 4,
-                (vmem(), vmem()),
+                [vmem(), hbm(), hbm(), hbm()],
+                (vmem(), hbm()),
+                [
+                    pltpu.VMEM((wide, nodes), BF16),
+                    pltpu.VMEM((wide, wide), BF16),
+                    pltpu.VMEM((3 * wide, wide), BF16),
+                    pltpu.VMEM((wide, nodes), F32),
+                    pltpu.SemaphoreType.DMA((4,)),
+                ],
                 flops=2 * nodes * wide * 4 * wide,
                 nbytes=nodes * wide * 8,
                 name="between",
-            )(back, features, out_turned, coarse_turned)
+            )(back, features, out_turned, qkv_turned)
     return call(
         last_kernel,
         shaped((own, channels), F32),
-        [smem()] + [vmem()] * 5,
+        [smem(), vmem()] + [hbm()] * 4,
         vmem(),
-        [pltpu.VMEM((own, channels), F32)],
+        [
+            pltpu.VMEM((own, channels), F32),
+            pltpu.VMEM((wide, nodes), F32),
+            pltpu.VMEM((wide, wide), BF16),
+            pltpu.VMEM((wide, own // 2), BF16),
+            pltpu.VMEM((own, channels), F32),
+            pltpu.SemaphoreType.DMA((4,)),
+        ],
         flops=2 * nodes * wide * 3 * wide,
         nbytes=own * channels * 8,
         name="last",

time: 167 us -> 158 us (0.946)
  blocking collectives: 64.2 us -> 74.1 us
  local copies, waits for them, and re-layouts: 16.6 us -> 10.8 us
  waiting for transfers between devices: 11.2 us -> 6.62 us
  starting transfers between devices: 21.4 us -> 17 us
  Pallas kernels: 51.1 us -> 47.3 us
    all_to_all x4 -> x5, blocking collectives: 64.2 us -> 74.1 us  [exchange(): return lax.all_to_all(value, axes, split_axis=0, concat_axis=0, tiled=True)]
    unnamed x37 -> x29, local copies, waits for them, and re-layouts: 16.6 us -> 10.8 us
    all_to_all x3 -> x2, waiting for transfers between devices: 11.2 us -> 6.62 us  [exchange(): return lax.all_to_all(value, axes, split_axis=0, concat_axis=0, tiled=True)]
    all_to_all x3 -> x2, starting transfers between devices: 21.4 us -> 17 us  [exchange(): return lax.all_to_all(value, axes, split_axis=0, concat_axis=0, tiled=True)]
    pallas_call x1, Pallas kernels: 11.9 us -> 9.19 us  [shards(): call(second_kernel, shaped((own, channels), BF16), [smem()] + [vmem()] *...]
  transfers between devices with their start and end apart: 3 -> 2, of which waited for: 2 -> 1; matrix products, arithmetic and copies ran while one was open for 5% -> 4% of each run, Pallas kernels for 5% -> 5%
where the time goes in v2:
time: 158 us; the launch traced here: 156 us
  blocking collectives  74.1 us (47%)
  Pallas kernels  47.3 us (30%)
  starting transfers between devices  17 us (11%)
  local copies, waits for them, and re-layouts  10.8 us (7%)
  waiting for transfers between devices  6.62 us (4%)
    all_to_all x5, blocking collectives, exchange(): return lax.all_to_all(value, axes, split_axis=0, concat_axis=0, tiled=True)  74.1 us
    all_to_all x2, starting transfers between devices, exchange(): return lax.all_to_all(value, axes, split_axis=0, concat_axis=0, tiled=True)  17 us
    pallas_call x2, Pallas kernels, shards(): call(coarse_kernel, shaped((subs, size, nodes), BF16), [smem(), vmem()],...  13.3 us
    unnamed x29, local copies, waits for them, and re-layouts  10.8 us
    pallas_call x1, Pallas kernels, shards(): call(second_kernel, shaped((own, channels), BF16), [smem()] + [vmem()] *...  9.19 us
    pallas_call x1, Pallas kernels, shards(): call(first_kernel, shaped((own, channels), F32), [hbm()] * 3, vmem(), [pl...  7.04 us
    all_to_all x2, waiting for transfers between devices, exchange(): return lax.all_to_all(value, axes, split_axis=0, concat_axis=0, tiled=True)  6.62 us
    pallas_call x1, Pallas kernels, shards(): call(pool_kernel, (shaped((CHEADS, 3 * size, nodes), BF16), shaped((wide,...  6.11 us
  transfers between devices with their start and end apart: 2, of which 1 were waited for; matrix products, arithmetic and copies ran while one was open for 4% of the time, Pallas kernels for 5%

profile of v2, /device:TPU:1, one launch (start us, length us, event | category | flops | bytes accessed | tf_op | source)
XLA Modules:
  0.0 156.1 jit_solution(4525972761668806621)
XLA Ops:
  0.0 0.7 copy-done.8
  0.7 1.6 %route.1 = (s32[128,128]{1,0:T(8,128)}, s32[16,128]{1,0:T(8,128)S(1)}) custom-call(s32[16,128]{1,0:T(8,128)S(1)} %bitcast.27), custom_call_target="tpu_custom_call" | custom-call | flops 134217728 | bytes 100000 | tf_op jit(solution)/shard_map/route/pallas_call | solution.py:429
  2.3 11.5 %all-to-all-start = ((s32[128,1,128]{2,1,0:T(1,128)}), s32[128,1,128]{2,1,0:T(1,128)S(1)}, u32[]{:S(2)}, u32[]{:S(2)}) async-start(s32[128,1,128]{2,1,0:T(1,128)} %bitcast.4), calls=%async_computation | async-start | bytes 131072 | tf_op jit(solution)/shard_map/all_to_all | solution.py:406
  13.8 0.0 copy-start.3
  13.8 1.2 copy-done.3
  15.0 0.9 copy-done.4
  15.9 0.8 copy-done.6
  16.8 7.0 %first.1.x_ref = f32[2048,128]{1,0:T(8,128)S(1)} custom-call(f32[2048,128]{1,0:T(8,128)S(1)} %copy-done.3, bf16[2,128,384]{2,1,0:T(8,128)(2,1)S(1)} %copy-done.4, bf16[2,128,128]{2,1,0:T(8,128)(2,1)S(1)} %copy-done.6), custom_call_target="tpu_custom_call" | custom-call | flops 1342177280 | bytes 2097152 | tf_op jit(solution)/shard_map/first/pallas_call | solution.py:453
  23.8 0.0 all-to-all-done
  23.8 2.5 %answer.1 = (bf16[2048,128]{1,0:T(8,128)(2,1)S(1)}, s32[16,128]{1,0:T(8,128)S(1)}) custom-call(s32[128,128]{1,0:T(8,128)S(1)} %bitcast.23, f32[2048,128]{1,0:T(8,128)S(1)} %first.1.x_ref), custom_call_target="tpu_custom_call" | custom-call | bytes 1572864 | tf_op jit(solution)/shard_map/answer/pallas_call | solution.py:468
  26.3 23.1 %all_to_all.35 = bf16[128,16,128]{2,1,0:T(8,128)(2,1)S(1)} all-to-all(bf16[128,16,128]{2,1,0:T(8,128)(2,1)S(1)} %bitcast.21), channel_id=1, replica_groups=mesh['leaf'=16,'sub'=8] {'leaf','sub'}, dimensions={0} | all-to-all | bytes 1048576 | tf_op jit(solution)/shard_map/all_to_all | solution.py:406
  49.4 0.0 copy-done.5
  49.4 0.0 copy-done.7
  49.4 9.2 %second.1 = bf16[2048,128]{1,0:T(8,128)(2,1)} custom-call(s32[2048]{0:T(1024)S(1)} %bitcast.29, bf16[2048,128]{1,0:T(8,128)(2,1)S(1)} %bitcast.22, bf16[2,128,384]{2,1,0:T(8,128)(2,1)S(1)} %copy-done.5, bf16[2,128,128]{2,1,0:T(8,128)(2,1)S(1)} %copy-done.7), custom_call_target="tpu_custom_call" | custom-call | flops 1342177280 | bytes 1048576 | tf_op jit(solution)/shard_map/second/pallas_call | solution.py:483
  58.6 5.6 %all-to-all-start.2 = ((bf16[128,16,128]{2,1,0:T(8,128)(2,1)}), bf16[128,16,128]{2,1,0:T(8,128)(2,1)}, u32[]{:S(2)}, u32[]{:S(2)}) async-start(bf16[128,16,128]{2,1,0:T(8,128)(2,1)} %bitcast.10), calls=%async_computation.2 | async-start | bytes 1048576 | tf_op jit(solution)/shard_map/all_to_all | solution.py:406
  64.2 0.0 copy-done.11
  64.2 1.3 copy.15
  65.5 0.0 copy-done.12
  65.5 1.3 copy.17
  66.8 3.2 %copy.16 = bf16[2,512,1536]{1,2,0:T(8,128)(2,1)S(1)} copy(bf16[2,512,1536]{2,1,0:T(8,128)(2,1)} %param.17) | data formatting | bytes 6291456 | tf_op args[7]
  70.0 0.8 place.1
  70.8 6.6 %all-to-all-done.2 = bf16[128,16,128]{2,1,0:T(8,128)(2,1)} async-done(((bf16[128,16,128]{2,1,0:T(8,128)(2,1)}), bf16[128,16,128]{2,1,0:T(8,128)(2,1)}, u32[]{:S(2)}, u32[]{:S(2)}) %all-to-all-start.2) | async-done | bytes 524320 | tf_op jit(solution)/shard_map/all_to_all | solution.py:406
  77.4 1.2 copy-done.1
  78.7 6.1 %pool.1 = (bf16[8,192,256]{2,1,0:T(8,128)(2,1)S(1)}, bf16[512,256]{1,0:T(8,128)(2,1)S(1)}, f32[2048,128]{1,0:T(8,128)S(1)}) custom-call(s32[2048]{0:T(1024)S(1)} %bitcast.26, s32[2048]{0:T(1024)S(1)} %bitcast.24, bf16[2048,128]{1,0:T(8,128)(2,1)} %bitcast.11.x_ref, bf16[512,1024]{1,0:T(8,128)(2,1)S(1)} %bitcast.20, bf16[2,1536,512]{2,1,0:T(8,128)(2,1)S(1)} %bitcast.16), custom_call_target="tpu_custom_call" | custom-call | flops 671088640 | bytes 2097152 | tf_op jit(solution)/shard_map/pool/pallas_call | solution.py:500
  84.8 15.7 %all_to_all.36.x_ref = bf16[8,192,256]{2,1,0:T(8,128)(2,1)S(1)} all-to-all(bf16[8,192,256]{2,1,0:T(8,128)(2,1)S(1)} %get-tuple-element.25), channel_id=1, replica_groups=mesh['leaf'=16,'sub'=8] {'sub'}, dimensions={0} | all-to-all | bytes 1572864 | tf_op jit(solution)/shard_map/all_to_all | solution.py:406
  100.4 6.6 %coarse.2 = bf16[8,64,256]{2,1,0:T(8,128)(2,1)S(1)} custom-call(s32[1,8]{1,0:T(1,128)S(1)} %copy-done.10, bf16[8,192,256]{2,1,0:T(8,128)(2,1)S(1)} %all_to_all.36.x_ref), custom_call_target="tpu_custom_call" | custom-call | flops 402653184 | bytes 1048576 | tf_op jit(solution)/shard_map/coarse/pallas_call | solution.py:523
  107.1 9.9 %all_to_all.37.x_ref = bf16[8,64,256]{2,1,0:T(8,128)(2,1)S(1)} all-to-all(bf16[8,64,256]{2,1,0:T(8,128)(2,1)S(1)} %coarse.2), channel_id=1, replica_groups=mesh['leaf'=16,'sub'=8] {'sub'}, dimensions={0} | all-to-all | bytes 524288 | tf_op jit(solution)/shard_map/all_to_all | solution.py:406
  117.0 1.6 %between.1 = (bf16[8,192,256]{2,1,0:T(8,128)(2,1)S(1)}, f32[512,256]{1,0:T(8,128)S(1)}) custom-call(bf16[8,64,256]{2,1,0:T(8,128)(2,1)S(1)} %all_to_all.37.x_ref, bf16[512,256]{1,0:T(8,128)(2,1)S(1)} %get-tuple-element.26.features_ref, bf16[2,512,512]{2,1,0:T(8,128)(2,1)S(1)} %bitcast.18, bf16[2,1536,512]{2,1,0:T(8,128)(2,1)S(1)} %bitcast.17), custom_call_target="tpu_custom_call" | custom-call | flops 536870912 | bytes 1048576 | tf_op jit(solution)/shard_map/between/pallas_call | solution.py:536
  118.6 15.6 %all_to_all.38.x_ref = bf16[8,192,256]{2,1,0:T(8,128)(2,1)S(1)} all-to-all(bf16[8,192,256]{2,1,0:T(8,128)(2,1)S(1)} %get-tuple-element.28), channel_id=1, replica_groups=mesh['leaf'=16,'sub'=8] {'sub'}, dimensions={0} | all-to-all | bytes 1572864 | tf_op jit(solution)/shard_map/all_to_all | solution.py:406
  134.2 6.6 %coarse.3 = bf16[8,64,256]{2,1,0:T(8,128)(2,1)S(1)} custom-call(s32[1,8]{1,0:T(1,128)S(1)} %copy-done.10, bf16[8,192,256]{2,1,0:T(8,128)(2,1)S(1)} %all_to_all.38.x_ref), custom_call_target="tpu_custom_call" | custom-call | flops 402653184 | bytes 1048576 | tf_op jit(solution)/shard_map/coarse/pallas_call | solution.py:523
  140.8 9.9 %all_to_all.39.x_ref = bf16[8,64,256]{2,1,0:T(8,128)(2,1)S(1)} all-to-all(bf16[8,64,256]{2,1,0:T(8,128)(2,1)S(1)} %coarse.3), channel_id=1, replica_groups=mesh['leaf'=16,'sub'=8] {'sub'}, dimensions={0} | all-to-all | bytes 524288 | tf_op jit(solution)/shard_map/all_to_all | solution.py:406
  150.7 5.2 %last.1 = f32[2048,128]{1,0:T(8,128)} custom-call(s32[2048]{0:T(1024)S(1)} %bitcast.25, bf16[8,64,256]{2,1,0:T(8,128)(2,1)S(1)} %all_to_all.39.x_ref, f32[512,256]{1,0:T(8,128)S(1)} %get-tuple-element.29.features_ref, bf16[2,512,512]{2,1,0:T(8,128)(2,1)S(1)} %bitcast.19, bf16[512,1024]{1,0:T(8,128)(2,1)S(1)} %copy-done.2, ...), custom_call_target="tpu_custom_call" | custom-call | flops 402653184 | bytes 2097152 | tf_op jit(solution)/shard_map/last/pallas_call | solution.py:552
  (16 shorter events, 0.0 us)
Async XLA Ops:
  0.0 0.7 copy-start.8
  2.3 21.5 %all-to-all-start = ((s32[128,1,128]{2,1,0:T(1,128)}), s32[128,1,128]{2,1,0:T(1,128)S(1)}, u32[]{:S(2)}, u32[]{:S(2)}) async-start(s32[128,1,128]{2,1,0:T(1,128)} %bitcast.4), calls=%async_computation | async-start | bytes 131072 | tf_op jit(solution)/shard_map/all_to_all | solution.py:406
  13.8 1.2 copy-start.3
  15.0 0.9 copy-start.4
  15.9 0.8 copy-start.6
  16.8 32.6 %copy-start.5 = (bf16[2,128,384]{2,1,0:T(8,128)(2,1)S(1)}, bf16[2,128,384]{2,1,0:T(8,128)(2,1)}, u32[]{:S(2)}) copy-start(bf16[2,128,384]{2,1,0:T(8,128)(2,1)} %qkv_ref.3) | copy-start | bytes 589828
  16.8 32.6 %copy-start.7 = (bf16[2,128,128]{2,1,0:T(8,128)(2,1)S(1)}, bf16[2,128,128]{2,1,0:T(8,128)(2,1)}, u32[]{:S(2)}) copy-start(bf16[2,128,128]{2,1,0:T(8,128)(2,1)} %out_ref.3) | copy-start | bytes 196612
  49.4 14.8 %copy-start.11 = (bf16[1024,512]{1,0:T(8,128)(2,1)S(1)}, bf16[1024,512]{1,0:T(8,128)(2,1)}, u32[]{:S(2)}) copy-start(bf16[1024,512]{1,0:T(8,128)(2,1)} %param.16) | copy-start | bytes 3145732
  49.4 16.1 %copy-start.12 = (bf16[2,512,512]{2,1,0:T(8,128)(2,1)S(1)}, bf16[2,512,512]{2,1,0:T(8,128)(2,1)}, u32[]{:S(2)}) copy-start(bf16[2,512,512]{2,1,0:T(8,128)(2,1)} %param.18) | copy-start | bytes 3145732
  58.6 18.8 %all-to-all-start.2 = ((bf16[128,16,128]{2,1,0:T(8,128)(2,1)}), bf16[128,16,128]{2,1,0:T(8,128)(2,1)}, u32[]{:S(2)}, u32[]{:S(2)}) async-start(bf16[128,16,128]{2,1,0:T(8,128)(2,1)} %bitcast.10), calls=%async_computation.2 | async-start | bytes 1048576 | tf_op jit(solution)/shard_map/all_to_all | solution.py:406
  66.8 3.2 %copy-start.9 = (s32[2048]{0:T(1024)S(1)}, s32[2048]{0:T(1024)}, u32[]{:S(2)}) copy-start(s32[2048]{0:T(1024)} %param.12) | copy-start | bytes 24580
  77.4 1.2 copy-start.1
  78.7 21.8 %copy-start.10 = (s32[1,8]{1,0:T(1,128)S(1)}, s32[1,8]{1,0:T(1,128)}, u32[]{:S(2)}) copy-start(s32[1,8]{1,0:T(1,128)} %counts_ref.3) | copy-start | bytes 100
  78.7 38.3 %copy-start = (bf16[2,512,512]{1,2,0:T(8,128)(2,1)S(1)}, bf16[2,512,512]{1,2,0:T(8,128)(2,1)}, u32[]{:S(2)}) copy-start(bf16[2,512,512]{1,2,0:T(8,128)(2,1)} %copy.17) | copy-start | bytes 3145732
  117.0 33.7 %copy-start.2 = (bf16[512,1024]{1,0:T(8,128)(2,1)S(1)}, bf16[512,1024]{1,0:T(8,128)(2,1)}, u32[]{:S(2)}) copy-start(bf16[512,1024]{1,0:T(8,128)(2,1)} %unpool_ref.1) | copy-start | bytes 3145732

commit v3 on v2

--- a/solution.py
+++ b/solution.py
@@ -28,6 +28,10 @@
 
 def hbm():
     return pl.BlockSpec(memory_space=pltpu.HBM)
+
+
+def in_hbm(value):
+    return pltpu.with_memory_space_constraint(value, pltpu.HBM)
 
 
 def fetch(source, target, sem):
@@ -219,12 +223,12 @@
     y_ref[...] = to_ref[...].astype(BF16)
 
 
-def send_projected(features, weight_ref, message_ref):
+def send_projected(features, weight, message_ref):
     normed = norm_columns(features)
     channels = features.shape[0]
     size = channels // CHEADS
     for part in range(3):
-        projected = dot(weight_ref[part * channels : (part + 1) * channels, :], normed).astype(BF16)
+        projected = dot(weight[part * channels : (part + 1) * channels, :], normed).astype(BF16)
         for head in range(CHEADS):
             message_ref[head, part * size : (part + 1) * size, :] = projected[
                 head * size : (head + 1) * size
@@ -232,56 +236,36 @@
 
 
 def pool_kernel(
-    named_ref,
-    place_ref,
-    x_ref,
-    pool_ref,
-    qkv_ref,
-    message_ref,
-    pooled_ref,
-    placed_ref,
-    from_ref,
-    rows_ref,
-    pool_held,
-    qkv_held,
-    pooled_held,
-    sems,
+    named_ref, place_ref, x_ref, pool_ref, qkv_ref, message_ref, pooled_ref, placed_ref, from_ref, held_ref, sem
 ):
-    pool_copy = fetch(pool_ref, pool_held, sems.at[0])
-    qkv_copy = fetch(qkv_ref.at[0], qkv_held, sems.at[1])
+    weight_copy = fetch(pool_ref, held_ref, sem)
     from_ref[...] = x_ref[...].astype(F32)
 
     def move(slot):
-        rows_ref[pl.ds(place_ref[named_ref[slot]], 1), :] = from_ref[pl.ds(slot, 1), :]
+        placed_ref[pl.ds(place_ref[named_ref[slot]], 1), :] = from_ref[pl.ds(slot, 1), :]
 
     each_row(from_ref.shape[0], move)
-    placed_copy = fetch(rows_ref, placed_ref, sems.at[2])
     nodes = x_ref.shape[0] // 8
     channels = x_ref.shape[1]
-    pool_copy.wait()
+    weight_copy.wait()
     pooled = None
     for k in range(8):
         part = dot(
-            pool_held[:, k * channels : (k + 1) * channels],
-            rows_ref[k * nodes : (k + 1) * nodes, :].astype(BF16),
-            ((1,), (1,)),
+            placed_ref[k * nodes : (k + 1) * nodes, :].astype(BF16),
+            held_ref[k * channels : (k + 1) * channels, :],
         )
         pooled = part if pooled is None else pooled + part
-    pooled = pooled.astype(BF16)
-    pooled_held[...] = pooled
-    pooled_copy = fetch(pooled_held, pooled_ref, sems.at[3])
-    qkv_copy.wait()
-    send_projected(pooled.astype(F32), qkv_held, message_ref)
-    placed_copy.wait()
-    pooled_copy.wait()
-
-
-def coarse_kernel(counts_ref, x_ref, out_ref, keys_ref, values_ref, of_ref, first_ref, last_ref):
+    pooled = pooled.astype(BF16).astype(F32).T
+    pooled_ref[...] = pooled
+    send_projected(pooled, qkv_ref[0], message_ref)
+
+
+def coarse_kernel(counts_ref, x_ref, out_ref, keys_ref, values_ref, of_ref, first_ref, last_ref, most_ref, total_ref):
     tiles, parts, width = x_ref.shape
     size = parts // 3
     balls_here = counts_ref.shape[1]
     per_tile = width // GRAN
-    together = 4
+    top = 4
     scale = LOG2E / math.sqrt(size)
     for t in range(tiles):
         keys_ref[t] = x_ref[t, size : 2 * size, :].astype(F32).T.astype(BF16)
@@ -290,13 +274,11 @@
     ends = []
     for e in range(balls_here):
         end = start + counts_ref[0, e]
-
         def mark(block, _, e=e, start=start, end=end):
             of_ref[block] = e
             first_ref[block] = start
             last_ref[block] = end - 1
             return 0
-
         lax.fori_loop(start, end, mark, 0)
         ends.append(end)
         start = end
@@ -310,92 +292,84 @@
         low = first_ref[tile * per_tile] // per_tile
         high = last_ref[tile * per_tile + per_tile - 1] // per_tile
 
-        def add(step, carry):
-            most, total = carry
-            now = most
-            chunks, chunk_scores = [], []
-            for c in range(together):
-                chunk = low + step * together + c
-                live = chunk <= high
-                chunk = jnp.minimum(chunk, high)
-                scores = dot(keys_ref[chunk], queries)
-                masked = []
-                for g in range(per_tile):
-                    ball_of = jnp.where(live, of_ref[chunk * per_tile + g], -1)
-                    masked.append(jnp.where(own == ball_of, scores[g * GRAN : (g + 1) * GRAN], NEG))
-                scores = jnp.concatenate(masked, axis=0)
-                chunks.append(chunk)
-                chunk_scores.append(scores)
-                now = jnp.maximum(now, jnp.max(scores, axis=0, keepdims=True))
-            total = total * jnp.exp2((most - now) * scale)
-            for chunk, scores in zip(chunks, chunk_scores):
-                weights = jnp.exp2((scores - now) * scale).astype(BF16)
-                total = total + dot(values_ref[chunk], weights)
-            return now, total
-
-        begin = (jnp.full((1, width), NEG, F32), jnp.zeros((size + 16, width), F32))
-        _, total = lax.fori_loop(0, (high - low + together) // together, add, begin)
+        def scored(chunk):
+            scores = dot(keys_ref[chunk], queries)
+            return jnp.concatenate(
+                [
+                    jnp.where(own == of_ref[chunk * per_tile + g], scores[g * GRAN : (g + 1) * GRAN], NEG)
+                    for g in range(per_tile)
+                ],
+                axis=0,
+            )
+
+        def several(chunk, count, carried):
+            scores = [scored(chunk + c) for c in range(count)]
+            now = most = most_ref[...] if carried else None
+            for s in scores:
+                here = jnp.max(s, axis=0, keepdims=True)
+                now = here if now is None else jnp.maximum(now, here)
+            total = total_ref[...] * jnp.exp2((most - now) * scale) if carried else None
+            for c, s in enumerate(scores):
+                part = dot(values_ref[chunk + c], jnp.exp2((s - now) * scale).astype(BF16))
+                total = part if total is None else total + part
+            most_ref[...] = now
+            total_ref[...] = total
+
+        number = high - low + 1
+        head = jnp.where(number <= top, number, jnp.where(number == top + 1, top - 1, top))
+        for count in range(1, top + 1):
+            @pl.when(head == count)
+            def _(count=count):
+                several(low, count, False)
+        def more(step, _):
+            chunk = low + head + step * 2
+            left = high - chunk + 1
+            @pl.when(left >= 2)
+            def _(): several(chunk, 2, True)
+            @pl.when(left == 1)
+            def _(): several(chunk, 1, True)
+            return 0
+        lax.fori_loop(0, (number - head + 1) // 2, more, 0)
+        total = total_ref[...]
         out_ref[tile] = (total[:size] / total[size : size + 1]).astype(BF16)
         return 0
 
     lax.fori_loop(0, tiles, one, 0)
 
 
-def between_kernel(
-    x_ref, features_ref, turned_ref, qkv_ref, message_ref, next_ref, features_held, out_held, qkv_held, next_held, sems
+def between_kernel(x_ref, features_ref, turned_ref, qkv_ref, message_ref, next_ref):
+    heads, size, width = x_ref.shape
+    features = features_ref[...] + dot(turned_ref[0], x_ref[...].reshape(heads * size, width))
+    next_ref[...] = features
+    send_projected(features, qkv_ref[1], message_ref)
+
+
+def last_kernel(
+    place_ref, x_ref, features_ref, turned_ref, unpool_ref, placed_ref, out_ref, sum_ref, rows_ref, sems
 ):
-    out_copy = fetch(turned_ref.at[0], out_held, sems.at[0])
-    features_copy = fetch(features_ref, features_held, sems.at[1])
-    qkv_copy = fetch(qkv_ref.at[1], qkv_held, sems.at[2])
     heads, size, width = x_ref.shape
-    out_copy.wait()
-    added = dot(out_held[...], x_ref[...].reshape(heads * size, width))
-    features_copy.wait()
-    features = features_held[...].astype(F32) + added
-    next_held[...] = features
-    next_copy = fetch(next_held, next_ref, sems.at[3])
-    qkv_copy.wait()
-    send_projected(features, qkv_held, message_ref)
-    next_copy.wait()
-
-
-def last_kernel(
-    place_ref,
-    x_ref,
-    features_ref,
-    turned_ref,
-    unpool_ref,
-    placed_ref,
-    out_ref,
-    sum_ref,
-    features_held,
-    out_held,
-    unpool_held,
-    placed_held,
-    sems,
-):
-    out_copy = fetch(turned_ref.at[1], out_held, sems.at[0])
-    features_copy = fetch(features_ref, features_held, sems.at[1])
-    unpool_copy = fetch(unpool_ref, unpool_held, sems.at[2])
-    placed_copy = fetch(placed_ref, placed_held, sems.at[3])
-    heads, size, width = x_ref.shape
-    out_copy.wait()
-    added = dot(out_held[...], x_ref[...].reshape(heads * size, width))
-    features_copy.wait()
-    features = (features_held[...] + added).astype(BF16).astype(F32)
+    features = features_ref[...] + dot(turned_ref[1], x_ref[...].reshape(heads * size, width))
+    features = features.astype(BF16).astype(F32)
     normed = norm_columns(features).astype(F32).T.astype(BF16)
     channels = placed_ref.shape[1]
-    unpool_copy.wait()
-    placed_copy.wait()
     for k in range(8):
         rows = slice(k * width, (k + 1) * width)
-        expanded = dot(normed, unpool_held[:, k * channels : (k + 1) * channels])
-        sum_ref[rows, :] = placed_held[rows, :] + expanded
-
-    def move(row):
-        out_ref[pl.ds(row, 1), :] = sum_ref[pl.ds(place_ref[row], 1), :]
-
-    each_row(out_ref.shape[0], move)
+        expanded = dot(normed, unpool_ref[:, k * channels : (k + 1) * channels])
+        sum_ref[rows, :] = placed_ref[rows, :] + expanded
+    parts = sems.shape[0]
+    count = rows_ref.shape[0] // parts
+    copies = []
+    for p in range(parts):
+
+        def move(row, p=p):
+            at = p * count + row
+            rows_ref[pl.ds(at, 1), :] = sum_ref[pl.ds(place_ref[at], 1), :]
+
+        each_row(count, move)
+        mine = pl.ds(p * count, count)
+        copies.append(fetch(rows_ref.at[mine, :], out_ref.at[mine, :], sems.at[p]))
+    for copy in copies:
+        copy.wait()
 
 
 def shaped(shape, dtype):
@@ -464,7 +438,7 @@
         flops=ball_flops,
         nbytes=own * channels * 8,
         name="first",
-    )(beads, fine_qkv, fine_out)
+    )(in_hbm(beads), in_hbm(fine_qkv), in_hbm(fine_out))
     answer, named = call(
         functools.partial(answer_kernel, bucket=bucket),
         (shaped((own, channels), BF16), shaped((own // 128, 128), jnp.int32)),
@@ -491,33 +465,27 @@
         name="second",
     )(slots, arrived, fine_qkv, fine_out)
     coming = exchange(outgoing.reshape(devices, bucket, channels), both).reshape(own, channels)
-    pool_turned = pool_weight.T
     qkv_turned = coarse_qkv.transpose(0, 2, 1)
     out_turned = coarse_out.transpose(0, 2, 1)
-    coming, pool_turned, qkv_turned, out_turned = lax.optimization_barrier(
-        (coming, pool_turned, qkv_turned, out_turned)
-    )
+    coming, qkv_turned, out_turned = lax.optimization_barrier((coming, qkv_turned, out_turned))
     message, features, placed = call(
         pool_kernel,
         (
             shaped((CHEADS, 3 * size, nodes), BF16),
-            shaped((wide, nodes), BF16),
+            shaped((wide, nodes), F32),
             shaped((own, channels), F32),
         ),
-        [smem(), smem(), vmem(), hbm(), hbm()],
-        (vmem(), hbm(), hbm()),
+        [smem(), smem(), vmem(), hbm(), vmem()],
+        (vmem(), vmem(), vmem()),
         [
             pltpu.VMEM((own, channels), F32),
-            pltpu.VMEM((own, channels), F32),
-            pltpu.VMEM((wide, own // 2), BF16),
-            pltpu.VMEM((3 * wide, wide), BF16),
-            pltpu.VMEM((wide, nodes), BF16),
-            pltpu.SemaphoreType.DMA((4,)),
+            pltpu.VMEM((own // 2, wide), BF16),
+            pltpu.SemaphoreType.DMA(()),
         ],
         flops=2 * nodes * wide * (own // 2 + 3 * wide),
         nbytes=own * channels * 8,
         name="pool",
-    )(named, places, coming, pool_turned, qkv_turned)
+    )(named, places, coming, in_hbm(pool_weight), qkv_turned)
     for layer in range(2):
         received = exchange(message, "sub")
         attended = call(
@@ -526,7 +494,8 @@
             [smem(), vmem()],
             vmem(),
             [pltpu.VMEM((subs, nodes, size), BF16), pltpu.VMEM((subs, size + 16, nodes), BF16)]
-            + [pltpu.SMEM((subs * nodes // GRAN,), jnp.int32)] * 3,
+            + [pltpu.SMEM((subs * nodes // GRAN,), jnp.int32)] * 3
+            + [pltpu.VMEM((1, nodes), F32), pltpu.VMEM((size + 16, nodes), F32)],
             flops=subs * nodes * nodes * 3 * size * 4,
             nbytes=subs * nodes * size * 8,
             name="coarse",
@@ -536,15 +505,8 @@
             message, features = call(
                 between_kernel,
                 (shaped((CHEADS, 3 * size, nodes), BF16), shaped((wide, nodes), F32)),
-                [vmem(), hbm(), hbm(), hbm()],
-                (vmem(), hbm()),
-                [
-                    pltpu.VMEM((wide, nodes), BF16),
-                    pltpu.VMEM((wide, wide), BF16),
-                    pltpu.VMEM((3 * wide, wide), BF16),
-                    pltpu.VMEM((wide, nodes), F32),
-                    pltpu.SemaphoreType.DMA((4,)),
-                ],
+                [vmem()] * 4,
+                (vmem(), vmem()),
                 flops=2 * nodes * wide * 4 * wide,
                 nbytes=nodes * wide * 8,
                 name="between",
@@ -552,13 +514,10 @@
     return call(
         last_kernel,
         shaped((own, channels), F32),
-        [smem(), vmem()] + [hbm()] * 4,
-        vmem(),
+        [smem()] + [vmem()] * 5,
+        hbm(),
         [
             pltpu.VMEM((own, channels), F32),
-            pltpu.VMEM((wide, nodes), F32),
-            pltpu.VMEM((wide, wide), BF16),
-            pltpu.VMEM((wide, own // 2), BF16),
             pltpu.VMEM((own, channels), F32),
             pltpu.SemaphoreType.DMA((4,)),
         ],

time: 158 us -> 150 us (0.949)
  local copies, waits for them, and re-layouts: 10.8 us -> 5.26 us
  Pallas kernels: 47.3 us -> 44 us
  waiting for transfers between devices: 6.62 us -> 9.38 us
    unnamed x29 -> x18, local copies, waits for them, and re-layouts: 10.8 us -> 5.26 us
    all_to_all x2, waiting for transfers between devices: 6.62 us -> 9.38 us  [exchange(): return lax.all_to_all(value, axes, split_axis=0, concat_axis=0, tiled=True)]
    pallas_call x2, Pallas kernels: 13.3 us -> 11.1 us  [shards(): call(coarse_kernel, shaped((subs, size, nodes), BF16), [smem(), vmem()],...]
  transfers between devices with their start and end apart: 2 -> 2, of which waited for: 1 -> 2; matrix products, arithmetic and copies ran while one was open for 4% -> 3% of each run, Pallas kernels for 5% -> 6%
where the time goes in v3:
time: 150 us; the launch traced here: 149 us
  blocking collectives  72.7 us (48%)
  Pallas kernels  44 us (29%)
  starting transfers between devices  17 us (11%)
  waiting for transfers between devices  9.38 us (6%)
  local copies, waits for them, and re-layouts  5.26 us (4%)
    all_to_all x5, blocking collectives, exchange(): return lax.all_to_all(value, axes, split_axis=0, concat_axis=0, tiled=True)  72.7 us
    all_to_all x2, starting transfers between devices, exchange(): return lax.all_to_all(value, axes, split_axis=0, concat_axis=0, tiled=True)  17 us
    pallas_call x2, Pallas kernels, shards(): call(coarse_kernel, shaped((subs, size, nodes), BF16), [smem(), vmem()],...  11.1 us
    all_to_all x2, waiting for transfers between devices, exchange(): return lax.all_to_all(value, axes, split_axis=0, concat_axis=0, tiled=True)  9.38 us
    pallas_call x1, Pallas kernels, shards(): call(second_kernel, shaped((own, channels), BF16), [smem()] + [vmem()] *...  9.16 us
    pallas_call x1, Pallas kernels, shards(): call(first_kernel, shaped((own, channels), F32), [hbm()] * 3, vmem(), [pl...  7.97 us
    unnamed x18, local copies, waits for them, and re-layouts  5.26 us
    pallas_call x1, Pallas kernels, shards(): call(pool_kernel, (shaped((CHEADS, 3 * size, nodes), BF16), shaped((wide,...  5.04 us
  transfers between devices with their start and end apart: 2, of which 2 were waited for; matrix products, arithmetic and copies ran while one was open for 3% of the time, Pallas kernels for 6%

profile of v3, /device:TPU:1, one launch (start us, length us, event | category | flops | bytes accessed | tf_op | source)
XLA Modules:
  0.0 148.6 jit_solution(16543985125516385265)
XLA Ops:
  0.0 0.0 copy-start.4
  0.0 0.7 copy-done.4
  0.7 1.6 %route.1 = (s32[128,128]{1,0:T(8,128)}, s32[16,128]{1,0:T(8,128)S(1)}) custom-call(s32[16,128]{1,0:T(8,128)S(1)} %bitcast.25), custom_call_target="tpu_custom_call" | custom-call | flops 134217728 | bytes 100000 | tf_op jit(solution)/shard_map/route/pallas_call | solution.py:403
  2.3 11.5 %all-to-all-start = ((s32[128,1,128]{2,1,0:T(1,128)}), s32[128,1,128]{2,1,0:T(1,128)S(1)}, u32[]{:S(2)}, u32[]{:S(2)}) async-start(s32[128,1,128]{2,1,0:T(1,128)} %bitcast.4), calls=%async_computation | async-start | bytes 131072 | tf_op jit(solution)/shard_map/all_to_all | solution.py:380
  13.8 0.0 copy-start.2
  13.8 0.0 copy-start.3
  13.8 8.0 %first.1.x_ref = f32[2048,128]{1,0:T(8,128)S(1)} custom-call(f32[2048,128]{1,0:T(8,128)} %x_ref.1, bf16[2,128,384]{2,1,0:T(8,128)(2,1)} %qkv_ref.3, bf16[2,128,128]{2,1,0:T(8,128)(2,1)} %out_ref.3), custom_call_target="tpu_custom_call" | custom-call | flops 1342177280 | bytes 2097152 | tf_op jit(solution)/shard_map/first/pallas_call | solution.py:427
  21.8 1.4 all-to-all-done
  23.2 2.5 %answer.1 = (bf16[2048,128]{1,0:T(8,128)(2,1)S(1)}, s32[16,128]{1,0:T(8,128)S(1)}) custom-call(s32[128,128]{1,0:T(8,128)S(1)} %bitcast.21, f32[2048,128]{1,0:T(8,128)S(1)} %first.1.x_ref), custom_call_target="tpu_custom_call" | custom-call | bytes 1572864 | tf_op jit(solution)/shard_map/answer/pallas_call | solution.py:442
  25.7 21.6 %all_to_all.35 = bf16[128,16,128]{2,1,0:T(8,128)(2,1)S(1)} all-to-all(bf16[128,16,128]{2,1,0:T(8,128)(2,1)S(1)} %bitcast.19), channel_id=1, replica_groups=mesh['leaf'=16,'sub'=8] {'leaf','sub'}, dimensions={0} | all-to-all | bytes 1048576 | tf_op jit(solution)/shard_map/all_to_all | solution.py:380
  47.3 0.0 copy-done.2
  47.3 0.0 copy-done.3
  47.3 9.2 %second.1 = bf16[2048,128]{1,0:T(8,128)(2,1)} custom-call(s32[2048]{0:T(1024)S(1)} %bitcast.27, bf16[2048,128]{1,0:T(8,128)(2,1)S(1)} %bitcast.20, bf16[2,128,384]{2,1,0:T(8,128)(2,1)S(1)} %copy-done.2, bf16[2,128,128]{2,1,0:T(8,128)(2,1)S(1)} %copy-done.3), custom_call_target="tpu_custom_call" | custom-call | flops 1342177280 | bytes 1048576 | tf_op jit(solution)/shard_map/second/pallas_call | solution.py:457
  56.5 5.6 %all-to-all-start.2 = ((bf16[128,16,128]{2,1,0:T(8,128)(2,1)}), bf16[128,16,128]{2,1,0:T(8,128)(2,1)}, u32[]{:S(2)}, u32[]{:S(2)}) async-start(bf16[128,16,128]{2,1,0:T(8,128)(2,1)} %bitcast.10), calls=%async_computation.2 | async-start | bytes 1048576 | tf_op jit(solution)/shard_map/all_to_all | solution.py:380
  62.1 0.0 copy-done.7
  62.1 1.3 copy.15
  63.4 3.2 %copy.14 = bf16[2,512,1536]{1,2,0:T(8,128)(2,1)S(1)} copy(bf16[2,512,1536]{2,1,0:T(8,128)(2,1)} %param.17) | data formatting | bytes 6291456 | tf_op args[7]
  66.6 0.0 copy-done.5
  66.6 0.8 place.1
  67.4 7.9 %all-to-all-done.2 = bf16[128,16,128]{2,1,0:T(8,128)(2,1)} async-done(((bf16[128,16,128]{2,1,0:T(8,128)(2,1)}), bf16[128,16,128]{2,1,0:T(8,128)(2,1)}, u32[]{:S(2)}, u32[]{:S(2)}) %all-to-all-start.2) | async-done | bytes 524320 | tf_op jit(solution)/shard_map/all_to_all | solution.py:380
  75.3 5.0 %pool.1 = (bf16[8,192,256]{2,1,0:T(8,128)(2,1)S(1)}, f32[512,256]{1,0:T(8,128)S(1)}, f32[2048,128]{1,0:T(8,128)S(1)}) custom-call(s32[2048]{0:T(1024)S(1)} %bitcast.24, s32[2048]{0:T(1024)S(1)} %bitcast.22, bf16[2048,128]{1,0:T(8,128)(2,1)} %bitcast.11.x_ref, bf16[1024,512]{1,0:T(8,128)(2,1)} %pool_ref.1, bf16[2,1536,512]{2,1,0:T(8,128)(2,1)S(1)} %bitcast.15), custom_call_target="tpu_custom_call" | custom-call | flops 671088640 | bytes 2097152 | tf_op jit(solution)/shard_map/pool/pallas_call | solution.py:471
  80.4 15.7 %all_to_all.36.x_ref = bf16[8,192,256]{2,1,0:T(8,128)(2,1)S(1)} all-to-all(bf16[8,192,256]{2,1,0:T(8,128)(2,1)S(1)} %get-tuple-element.23), channel_id=1, replica_groups=mesh['leaf'=16,'sub'=8] {'sub'}, dimensions={0} | all-to-all | bytes 1572864 | tf_op jit(solution)/shard_map/all_to_all | solution.py:380
  96.1 0.0 copy-done.6
  96.1 5.6 %coarse.2 = bf16[8,64,256]{2,1,0:T(8,128)(2,1)S(1)} custom-call(s32[1,8]{1,0:T(1,128)S(1)} %copy-done.6, bf16[8,192,256]{2,1,0:T(8,128)(2,1)S(1)} %all_to_all.36.x_ref), custom_call_target="tpu_custom_call" | custom-call | flops 402653184 | bytes 1048576 | tf_op jit(solution)/shard_map/coarse/pallas_call | solution.py:491
  101.6 9.9 %all_to_all.37.x_ref = bf16[8,64,256]{2,1,0:T(8,128)(2,1)S(1)} all-to-all(bf16[8,64,256]{2,1,0:T(8,128)(2,1)S(1)} %coarse.2), channel_id=1, replica_groups=mesh['leaf'=16,'sub'=8] {'sub'}, dimensions={0} | all-to-all | bytes 524288 | tf_op jit(solution)/shard_map/all_to_all | solution.py:380
  111.5 0.0 copy-done
  111.5 1.2 between.1
  112.8 15.6 %all_to_all.38.x_ref = bf16[8,192,256]{2,1,0:T(8,128)(2,1)S(1)} all-to-all(bf16[8,192,256]{2,1,0:T(8,128)(2,1)S(1)} %get-tuple-element.26), channel_id=1, replica_groups=mesh['leaf'=16,'sub'=8] {'sub'}, dimensions={0} | all-to-all | bytes 1572864 | tf_op jit(solution)/shard_map/all_to_all | solution.py:380
  128.4 5.6 %coarse.3 = bf16[8,64,256]{2,1,0:T(8,128)(2,1)S(1)} custom-call(s32[1,8]{1,0:T(1,128)S(1)} %copy-done.6, bf16[8,192,256]{2,1,0:T(8,128)(2,1)S(1)} %all_to_all.38.x_ref), custom_call_target="tpu_custom_call" | custom-call | flops 402653184 | bytes 1048576 | tf_op jit(solution)/shard_map/coarse/pallas_call | solution.py:491
  133.9 9.9 %all_to_all.39.x_ref = bf16[8,64,256]{2,1,0:T(8,128)(2,1)S(1)} all-to-all(bf16[8,64,256]{2,1,0:T(8,128)(2,1)S(1)} %coarse.3), channel_id=1, replica_groups=mesh['leaf'=16,'sub'=8] {'sub'}, dimensions={0} | all-to-all | bytes 524288 | tf_op jit(solution)/shard_map/all_to_all | solution.py:380
  143.8 0.0 copy-done.1
  143.8 4.6 %last.1 = f32[2048,128]{1,0:T(8,128)} custom-call(s32[2048]{0:T(1024)S(1)} %bitcast.23, bf16[8,64,256]{2,1,0:T(8,128)(2,1)S(1)} %all_to_all.39.x_ref, f32[512,256]{1,0:T(8,128)S(1)} %get-tuple-element.27.features_ref, bf16[2,512,512]{2,1,0:T(8,128)(2,1)S(1)} %bitcast.18, bf16[512,1024]{1,0:T(8,128)(2,1)S(1)} %copy-done.1, ...), custom_call_target="tpu_custom_call" | custom-call | flops 402653184 | bytes 2097152 | tf_op jit(solution)/shard_map/last/pallas_call | solution.py:514
  (5 shorter events, 0.0 us)
Async XLA Ops:
  0.0 0.7 copy-start.4
  2.3 20.9 %all-to-all-start = ((s32[128,1,128]{2,1,0:T(1,128)}), s32[128,1,128]{2,1,0:T(1,128)S(1)}, u32[]{:S(2)}, u32[]{:S(2)}) async-start(s32[128,1,128]{2,1,0:T(1,128)} %bitcast.4), calls=%async_computation | async-start | bytes 131072 | tf_op jit(solution)/shard_map/all_to_all | solution.py:380
  13.8 33.6 %copy-start.2 = (bf16[2,128,384]{2,1,0:T(8,128)(2,1)S(1)}, bf16[2,128,384]{2,1,0:T(8,128)(2,1)}, u32[]{:S(2)}) copy-start(bf16[2,128,384]{2,1,0:T(8,128)(2,1)} %qkv_ref.3) | copy-start | bytes 589828
  13.8 33.6 %copy-start.3 = (bf16[2,128,128]{2,1,0:T(8,128)(2,1)S(1)}, bf16[2,128,128]{2,1,0:T(8,128)(2,1)}, u32[]{:S(2)}) copy-start(bf16[2,128,128]{2,1,0:T(8,128)(2,1)} %out_ref.3) | copy-start | bytes 196612
  47.3 14.7 %copy-start.7 = (bf16[2,512,512]{2,1,0:T(8,128)(2,1)S(1)}, bf16[2,512,512]{2,1,0:T(8,128)(2,1)}, u32[]{:S(2)}) copy-start(bf16[2,512,512]{2,1,0:T(8,128)(2,1)} %param.18) | copy-start | bytes 3145732
  56.5 18.8 %all-to-all-start.2 = ((bf16[128,16,128]{2,1,0:T(8,128)(2,1)}), bf16[128,16,128]{2,1,0:T(8,128)(2,1)}, u32[]{:S(2)}, u32[]{:S(2)}) async-start(bf16[128,16,128]{2,1,0:T(8,128)(2,1)} %bitcast.10), calls=%async_computation.2 | async-start | bytes 1048576 | tf_op jit(solution)/shard_map/all_to_all | solution.py:380
  63.4 3.2 %copy-start.5 = (s32[2048]{0:T(1024)S(1)}, s32[2048]{0:T(1024)}, u32[]{:S(2)}) copy-start(s32[2048]{0:T(1024)} %param.12) | copy-start | bytes 24580
  75.3 20.7 %copy-start.6 = (s32[1,8]{1,0:T(1,128)S(1)}, s32[1,8]{1,0:T(1,128)}, u32[]{:S(2)}) copy-start(s32[1,8]{1,0:T(1,128)} %counts_ref.3) | copy-start | bytes 100
  75.3 36.2 %copy-start = (bf16[2,512,512]{1,2,0:T(8,128)(2,1)S(1)}, bf16[2,512,512]{1,2,0:T(8,128)(2,1)}, u32[]{:S(2)}) copy-start(bf16[2,512,512]{1,2,0:T(8,128)(2,1)} %copy.15) | copy-start | bytes 3145732
  111.5 32.3 %copy-start.1 = (bf16[512,1024]{1,0:T(8,128)(2,1)S(1)}, bf16[512,1024]{1,0:T(8,128)(2,1)}, u32[]{:S(2)}) copy-start(bf16[512,1024]{1,0:T(8,128)(2,1)} %unpool_ref.1) | copy-start | bytes 3145732

commit v4 on v3

--- a/solution.py
+++ b/solution.py
@@ -92,16 +92,17 @@
 def route_kernel(rot_ref, wanted_ref, slot_ref, *, own, devices):
     bucket = own // devices
     named = row_pairs(rot_ref)
-    dest = [row // own for row in named]
+    own_bits = own.bit_length() - 1
+    dest = [row >> own_bits for row in named]
     hots, found = ranks(dest, devices)
     lanes = lax.broadcasted_iota(jnp.int32, (bucket, 256), 0)
     total = jnp.zeros((devices, 2 * bucket), F32)
     for r, row in enumerate(named):
         store_pair(slot_ref, r, dest[r] * bucket + found[r])
-        local = row % own
+        local = row & (own - 1)
         here = lanes == found[r]
-        high = jnp.where(here, (local // 64).astype(F32), 0.0)
-        low = jnp.where(here, (local % 64).astype(F32), 0.0)
+        high = jnp.where(here, (local >> 6).astype(F32), 0.0)
+        low = jnp.where(here, (local & 63).astype(F32), 0.0)
         parts = jnp.concatenate([high, low], axis=0).astype(BF16)
         total = total + dot(hots[r], parts, ((1,), (1,)))
     wanted = total[:, :bucket] * 64.0 + total[:, bucket:]
@@ -110,7 +111,7 @@
 
 
 def place_kernel(pool_ref, place_ref, *, nodes):
-    node = [row % nodes for row in row_pairs(pool_ref)]
+    node = [row & (nodes - 1) for row in row_pairs(pool_ref)]
     _, found = ranks(node, nodes)
     for r in range(len(node)):
         store_pair(place_ref, r, found[r] * nodes + node[r])
@@ -260,47 +261,43 @@
     send_projected(pooled, qkv_ref[0], message_ref)
 
 
-def coarse_kernel(counts_ref, x_ref, out_ref, keys_ref, values_ref, of_ref, first_ref, last_ref, most_ref, total_ref):
+def coarse_kernel(counts_ref, x_ref, out_ref, keys_ref, values_ref, most_ref, total_ref):
     tiles, parts, width = x_ref.shape
     size = parts // 3
-    balls_here = counts_ref.shape[1]
     per_tile = width // GRAN
     top = 4
     scale = LOG2E / math.sqrt(size)
     for t in range(tiles):
         keys_ref[t] = x_ref[t, size : 2 * size, :].astype(F32).T.astype(BF16)
         values_ref[t] = jnp.concatenate([x_ref[t, 2 * size :, :], jnp.ones((16, width), BF16)], axis=0)
-    start = 0
-    ends = []
-    for e in range(balls_here):
-        end = start + counts_ref[0, e]
-        def mark(block, _, e=e, start=start, end=end):
-            of_ref[block] = e
-            first_ref[block] = start
-            last_ref[block] = end - 1
-            return 0
-        lax.fori_loop(start, end, mark, 0)
-        ends.append(end)
-        start = end
+    edges = [counts_ref[0, 0]]
+    for e in range(1, counts_ref.shape[1] - 1):
+        edges.append(edges[-1] + counts_ref[0, e])
+    lane_block = lax.broadcasted_iota(jnp.int32, (1, width), 1) >> (GRAN.bit_length() - 1)
+    tile_bits = per_tile.bit_length() - 1
+
+    def ball_around(block):
+        begin, end = 0, tiles * per_tile
+        for edge in edges:
+            begin = jnp.where(edge <= block, edge, begin)
+        for edge in reversed(edges):
+            end = jnp.where(edge > block, edge, end)
+        return begin, end
 
     def one(tile, _):
         queries = x_ref[tile, :size, :]
-        blocks = tile * per_tile + lax.broadcasted_iota(jnp.int32, (1, width), 1) // GRAN
-        own = jnp.zeros((1, width), jnp.int32)
-        for e in range(balls_here):
-            own = own + jnp.where(blocks >= ends[e], 1, 0)
-        low = first_ref[tile * per_tile] // per_tile
-        high = last_ref[tile * per_tile + per_tile - 1] // per_tile
+        begin, end = ball_around(tile * per_tile + lane_block)
+        low = ball_around(tile * per_tile)[0] >> tile_bits
+        high = (ball_around(tile * per_tile + per_tile - 1)[1] - 1) >> tile_bits
 
         def scored(chunk):
             scores = dot(keys_ref[chunk], queries)
-            return jnp.concatenate(
-                [
-                    jnp.where(own == of_ref[chunk * per_tile + g], scores[g * GRAN : (g + 1) * GRAN], NEG)
-                    for g in range(per_tile)
-                ],
-                axis=0,
-            )
+            masked = []
+            for g in range(per_tile):
+                block = chunk * per_tile + g
+                seen = jnp.logical_and(block >= begin, block < end)
+                masked.append(jnp.where(seen, scores[g * GRAN : (g + 1) * GRAN], NEG))
+            return jnp.concatenate(masked, axis=0)
 
         def several(chunk, count, carried):
             scores = [scored(chunk + c) for c in range(count)]
@@ -318,18 +315,26 @@
         number = high - low + 1
         head = jnp.where(number <= top, number, jnp.where(number == top + 1, top - 1, top))
         for count in range(1, top + 1):
+
             @pl.when(head == count)
             def _(count=count):
                 several(low, count, False)
+
         def more(step, _):
             chunk = low + head + step * 2
             left = high - chunk + 1
+
             @pl.when(left >= 2)
-            def _(): several(chunk, 2, True)
+            def _():
+                several(chunk, 2, True)
+
             @pl.when(left == 1)
-            def _(): several(chunk, 1, True)
+            def _():
+                several(chunk, 1, True)
+
             return 0
-        lax.fori_loop(0, (number - head + 1) // 2, more, 0)
+
+        lax.fori_loop(0, (number - head + 1) >> 1, more, 0)
         total = total_ref[...]
         out_ref[tile] = (total[:size] / total[size : size + 1]).astype(BF16)
         return 0
@@ -494,7 +499,6 @@
             [smem(), vmem()],
             vmem(),
             [pltpu.VMEM((subs, nodes, size), BF16), pltpu.VMEM((subs, size + 16, nodes), BF16)]
-            + [pltpu.SMEM((subs * nodes // GRAN,), jnp.int32)] * 3
             + [pltpu.VMEM((1, nodes), F32), pltpu.VMEM((size + 16, nodes), F32)],
             flops=subs * nodes * nodes * 3 * size * 4,
             nbytes=subs * nodes * size * 8,

time: 150 us -> 149 us (level)
  no operation moved by 1% of the time
where the time goes in v4:
time: 149 us; the launch traced here: 148 us
  blocking collectives  72.7 us (49%)
  Pallas kernels  43.4 us (29%)
  starting transfers between devices  17.1 us (11%)
  waiting for transfers between devices  9.39 us (6%)
  local copies, waits for them, and re-layouts  5.26 us (4%)
    all_to_all x5, blocking collectives, exchange(): return lax.all_to_all(value, axes, split_axis=0, concat_axis=0, tiled=True)  72.7 us
    all_to_all x2, starting transfers between devices, exchange(): return lax.all_to_all(value, axes, split_axis=0, concat_axis=0, tiled=True)  17.1 us
    pallas_call x2, Pallas kernels, shards(): call(coarse_kernel, shaped((subs, size, nodes), BF16), [smem(), vmem()],...  10.6 us
    all_to_all x2, waiting for transfers between devices, exchange(): return lax.all_to_all(value, axes, split_axis=0, concat_axis=0, tiled=True)  9.39 us
    pallas_call x1, Pallas kernels, shards(): call(second_kernel, shaped((own, channels), BF16), [smem()] + [vmem()] *...  9.16 us
    pallas_call x1, Pallas kernels, shards(): call(first_kernel, shaped((own, channels), F32), [hbm()] * 3, vmem(), [pl...  7.97 us
    unnamed x18, local copies, waits for them, and re-layouts  5.26 us
    pallas_call x1, Pallas kernels, shards(): call(pool_kernel, (shaped((CHEADS, 3 * size, nodes), BF16), shaped((wide,...  5.04 us
  transfers between devices with their start and end apart: 2, of which 2 were waited for; matrix products, arithmetic and copies ran while one was open for 3% of the time, Pallas kernels for 6%

profile of v4, /device:TPU:1, one launch (start us, length us, event | category | flops | bytes accessed | tf_op | source)
XLA Modules:
  0.0 148.0 jit_solution(3712723473744137627)
XLA Ops:
  0.0 0.0 copy-start.4
  0.0 0.7 copy-done.4
  0.7 1.6 %route.1 = (s32[128,128]{1,0:T(8,128)}, s32[16,128]{1,0:T(8,128)S(1)}) custom-call(s32[16,128]{1,0:T(8,128)S(1)} %bitcast.25), custom_call_target="tpu_custom_call" | custom-call | flops 134217728 | bytes 100000 | tf_op jit(solution)/shard_map/route/pallas_call | solution.py:408
  2.3 11.5 %all-to-all-start = ((s32[128,1,128]{2,1,0:T(1,128)}), s32[128,1,128]{2,1,0:T(1,128)S(1)}, u32[]{:S(2)}, u32[]{:S(2)}) async-start(s32[128,1,128]{2,1,0:T(1,128)} %bitcast.4), calls=%async_computation | async-start | bytes 131072 | tf_op jit(solution)/shard_map/all_to_all | solution.py:385
  13.7 0.0 copy-start.2
  13.8 0.0 copy-start.3
  13.8 8.0 %first.1.x_ref = f32[2048,128]{1,0:T(8,128)S(1)} custom-call(f32[2048,128]{1,0:T(8,128)} %x_ref.1, bf16[2,128,384]{2,1,0:T(8,128)(2,1)} %qkv_ref.3, bf16[2,128,128]{2,1,0:T(8,128)(2,1)} %out_ref.3), custom_call_target="tpu_custom_call" | custom-call | flops 1342177280 | bytes 2097152 | tf_op jit(solution)/shard_map/first/pallas_call | solution.py:432
  21.7 1.4 all-to-all-done
  23.2 2.5 %answer.1 = (bf16[2048,128]{1,0:T(8,128)(2,1)S(1)}, s32[16,128]{1,0:T(8,128)S(1)}) custom-call(s32[128,128]{1,0:T(8,128)S(1)} %bitcast.21, f32[2048,128]{1,0:T(8,128)S(1)} %first.1.x_ref), custom_call_target="tpu_custom_call" | custom-call | bytes 1572864 | tf_op jit(solution)/shard_map/answer/pallas_call | solution.py:447
  25.7 21.6 %all_to_all.35 = bf16[128,16,128]{2,1,0:T(8,128)(2,1)S(1)} all-to-all(bf16[128,16,128]{2,1,0:T(8,128)(2,1)S(1)} %bitcast.19), channel_id=1, replica_groups=mesh['leaf'=16,'sub'=8] {'leaf','sub'}, dimensions={0} | all-to-all | bytes 1048576 | tf_op jit(solution)/shard_map/all_to_all | solution.py:385
  47.3 0.0 copy-done.2
  47.3 0.0 copy-done.3
  47.3 9.2 %second.1 = bf16[2048,128]{1,0:T(8,128)(2,1)} custom-call(s32[2048]{0:T(1024)S(1)} %bitcast.27, bf16[2048,128]{1,0:T(8,128)(2,1)S(1)} %bitcast.20, bf16[2,128,384]{2,1,0:T(8,128)(2,1)S(1)} %copy-done.2, bf16[2,128,128]{2,1,0:T(8,128)(2,1)S(1)} %copy-done.3), custom_call_target="tpu_custom_call" | custom-call | flops 1342177280 | bytes 1048576 | tf_op jit(solution)/shard_map/second/pallas_call | solution.py:462
  56.5 5.6 %all-to-all-start.2 = ((bf16[128,16,128]{2,1,0:T(8,128)(2,1)}), bf16[128,16,128]{2,1,0:T(8,128)(2,1)}, u32[]{:S(2)}, u32[]{:S(2)}) async-start(bf16[128,16,128]{2,1,0:T(8,128)(2,1)} %bitcast.10), calls=%async_computation.2 | async-start | bytes 1048576 | tf_op jit(solution)/shard_map/all_to_all | solution.py:385
  62.1 0.0 copy-done.7
  62.1 1.3 copy.15
  63.4 3.2 %copy.14 = bf16[2,512,1536]{1,2,0:T(8,128)(2,1)S(1)} copy(bf16[2,512,1536]{2,1,0:T(8,128)(2,1)} %param.17) | data formatting | bytes 6291456 | tf_op args[7]
  66.6 0.0 copy-done.5
  66.6 0.8 place.1
  67.4 7.9 %all-to-all-done.2 = bf16[128,16,128]{2,1,0:T(8,128)(2,1)} async-done(((bf16[128,16,128]{2,1,0:T(8,128)(2,1)}), bf16[128,16,128]{2,1,0:T(8,128)(2,1)}, u32[]{:S(2)}, u32[]{:S(2)}) %all-to-all-start.2) | async-done | bytes 524320 | tf_op jit(solution)/shard_map/all_to_all | solution.py:385
  75.3 5.0 %pool.1 = (bf16[8,192,256]{2,1,0:T(8,128)(2,1)S(1)}, f32[512,256]{1,0:T(8,128)S(1)}, f32[2048,128]{1,0:T(8,128)S(1)}) custom-call(s32[2048]{0:T(1024)S(1)} %bitcast.24, s32[2048]{0:T(1024)S(1)} %bitcast.22, bf16[2048,128]{1,0:T(8,128)(2,1)} %bitcast.11.x_ref, bf16[1024,512]{1,0:T(8,128)(2,1)} %pool_ref.1, bf16[2,1536,512]{2,1,0:T(8,128)(2,1)S(1)} %bitcast.15), custom_call_target="tpu_custom_call" | custom-call | flops 671088640 | bytes 2097152 | tf_op jit(solution)/shard_map/pool/pallas_call | solution.py:476
  80.4 15.7 %all_to_all.36.x_ref = bf16[8,192,256]{2,1,0:T(8,128)(2,1)S(1)} all-to-all(bf16[8,192,256]{2,1,0:T(8,128)(2,1)S(1)} %get-tuple-element.23), channel_id=1, replica_groups=mesh['leaf'=16,'sub'=8] {'sub'}, dimensions={0} | all-to-all | bytes 1572864 | tf_op jit(solution)/shard_map/all_to_all | solution.py:385
  96.0 0.0 copy-done.6
  96.0 5.3 %coarse.2 = bf16[8,64,256]{2,1,0:T(8,128)(2,1)S(1)} custom-call(s32[1,8]{1,0:T(1,128)S(1)} %copy-done.6, bf16[8,192,256]{2,1,0:T(8,128)(2,1)S(1)} %all_to_all.36.x_ref), custom_call_target="tpu_custom_call" | custom-call | flops 402653184 | bytes 1048576 | tf_op jit(solution)/shard_map/coarse/pallas_call | solution.py:496
  101.3 9.9 %all_to_all.37.x_ref = bf16[8,64,256]{2,1,0:T(8,128)(2,1)S(1)} all-to-all(bf16[8,64,256]{2,1,0:T(8,128)(2,1)S(1)} %coarse.2), channel_id=1, replica_groups=mesh['leaf'=16,'sub'=8] {'sub'}, dimensions={0} | all-to-all | bytes 524288 | tf_op jit(solution)/shard_map/all_to_all | solution.py:385
  111.2 0.0 copy-done
  111.2 1.2 between.1
  112.5 15.6 %all_to_all.38.x_ref = bf16[8,192,256]{2,1,0:T(8,128)(2,1)S(1)} all-to-all(bf16[8,192,256]{2,1,0:T(8,128)(2,1)S(1)} %get-tuple-element.26), channel_id=1, replica_groups=mesh['leaf'=16,'sub'=8] {'sub'}, dimensions={0} | all-to-all | bytes 1572864 | tf_op jit(solution)/shard_map/all_to_all | solution.py:385
  128.1 5.3 %coarse.3 = bf16[8,64,256]{2,1,0:T(8,128)(2,1)S(1)} custom-call(s32[1,8]{1,0:T(1,128)S(1)} %copy-done.6, bf16[8,192,256]{2,1,0:T(8,128)(2,1)S(1)} %all_to_all.38.x_ref), custom_call_target="tpu_custom_call" | custom-call | flops 402653184 | bytes 1048576 | tf_op jit(solution)/shard_map/coarse/pallas_call | solution.py:496
  133.3 9.9 %all_to_all.39.x_ref = bf16[8,64,256]{2,1,0:T(8,128)(2,1)S(1)} all-to-all(bf16[8,64,256]{2,1,0:T(8,128)(2,1)S(1)} %coarse.3), channel_id=1, replica_groups=mesh['leaf'=16,'sub'=8] {'sub'}, dimensions={0} | all-to-all | bytes 524288 | tf_op jit(solution)/shard_map/all_to_all | solution.py:385
  143.3 0.0 copy-done.1
  143.3 4.6 %last.1 = f32[2048,128]{1,0:T(8,128)} custom-call(s32[2048]{0:T(1024)S(1)} %bitcast.23, bf16[8,64,256]{2,1,0:T(8,128)(2,1)S(1)} %all_to_all.39.x_ref, f32[512,256]{1,0:T(8,128)S(1)} %get-tuple-element.27.features_ref, bf16[2,512,512]{2,1,0:T(8,128)(2,1)S(1)} %bitcast.18, bf16[512,1024]{1,0:T(8,128)(2,1)S(1)} %copy-done.1, ...), custom_call_target="tpu_custom_call" | custom-call | flops 402653184 | bytes 2097152 | tf_op jit(solution)/shard_map/last/pallas_call | solution.py:518
  (5 shorter events, 0.0 us)
Async XLA Ops:
  0.0 0.7 copy-start.4
  2.3 20.9 %all-to-all-start = ((s32[128,1,128]{2,1,0:T(1,128)}), s32[128,1,128]{2,1,0:T(1,128)S(1)}, u32[]{:S(2)}, u32[]{:S(2)}) async-start(s32[128,1,128]{2,1,0:T(1,128)} %bitcast.4), calls=%async_computation | async-start | bytes 131072 | tf_op jit(solution)/shard_map/all_to_all | solution.py:385
  13.7 33.6 %copy-start.2 = (bf16[2,128,384]{2,1,0:T(8,128)(2,1)S(1)}, bf16[2,128,384]{2,1,0:T(8,128)(2,1)}, u32[]{:S(2)}) copy-start(bf16[2,128,384]{2,1,0:T(8,128)(2,1)} %qkv_ref.3) | copy-start | bytes 589828
  13.8 33.6 %copy-start.3 = (bf16[2,128,128]{2,1,0:T(8,128)(2,1)S(1)}, bf16[2,128,128]{2,1,0:T(8,128)(2,1)}, u32[]{:S(2)}) copy-start(bf16[2,128,128]{2,1,0:T(8,128)(2,1)} %out_ref.3) | copy-start | bytes 196612
  47.3 14.8 %copy-start.7 = (bf16[2,512,512]{2,1,0:T(8,128)(2,1)S(1)}, bf16[2,512,512]{2,1,0:T(8,128)(2,1)}, u32[]{:S(2)}) copy-start(bf16[2,512,512]{2,1,0:T(8,128)(2,1)} %param.18) | copy-start | bytes 3145732
  56.5 18.9 %all-to-all-start.2 = ((bf16[128,16,128]{2,1,0:T(8,128)(2,1)}), bf16[128,16,128]{2,1,0:T(8,128)(2,1)}, u32[]{:S(2)}, u32[]{:S(2)}) async-start(bf16[128,16,128]{2,1,0:T(8,128)(2,1)} %bitcast.10), calls=%async_computation.2 | async-start | bytes 1048576 | tf_op jit(solution)/shard_map/all_to_all | solution.py:385
  63.4 3.2 %copy-start.5 = (s32[2048]{0:T(1024)S(1)}, s32[2048]{0:T(1024)}, u32[]{:S(2)}) copy-start(s32[2048]{0:T(1024)} %param.12) | copy-start | bytes 24580
  75.3 20.7 %copy-start.6 = (s32[1,8]{1,0:T(1,128)S(1)}, s32[1,8]{1,0:T(1,128)}, u32[]{:S(2)}) copy-start(s32[1,8]{1,0:T(1,128)} %counts_ref.3) | copy-start | bytes 100
  75.3 35.9 %copy-start = (bf16[2,512,512]{1,2,0:T(8,128)(2,1)S(1)}, bf16[2,512,512]{1,2,0:T(8,128)(2,1)}, u32[]{:S(2)}) copy-start(bf16[2,512,512]{1,2,0:T(8,128)(2,1)} %copy.15) | copy-start | bytes 3145732
  111.2 32.0 %copy-start.1 = (bf16[512,1024]{1,0:T(8,128)(2,1)S(1)}, bf16[512,1024]{1,0:T(8,128)(2,1)}, u32[]{:S(2)}) copy-start(bf16[512,1024]{1,0:T(8,128)(2,1)} %unpool_ref.1) | copy-start | bytes 3145732

commit v5 on v4

--- a/solution.py
+++ b/solution.py
@@ -169,7 +169,7 @@
 
 
 def each_row(count, move):
-    together = 64
+    together = min(count, 128)
 
     def some(step, _):
         for j in range(together):
@@ -224,6 +224,26 @@
     y_ref[...] = to_ref[...].astype(BF16)
 
 
+def place_in_message(message_ref, target, rows, value):
+    me = lax.axis_index("sub")
+    other = (target & 1) ^ (me & 1)
+    ahead = ((target >> 1) - (me >> 1)) & 3
+    message_ref[other, ahead, rows, :] = value
+
+
+def received_blocks(message_ref, swapped_ref, shifted_refs):
+    me = lax.axis_index("sub")
+    for back in range(4):
+        for other in range(2):
+            source = ((((me >> 1) - back) & 3) << 1) + ((me & 1) ^ other)
+            if back:
+                yield source, shifted_refs[back - 1].at[other]
+            elif other:
+                yield source, swapped_ref.at[0]
+            else:
+                yield source, message_ref.at[0, 0]
+
+
 def send_projected(features, weight, message_ref):
     normed = norm_columns(features)
     channels = features.shape[0]
@@ -231,9 +251,12 @@
     for part in range(3):
         projected = dot(weight[part * channels : (part + 1) * channels, :], normed).astype(BF16)
         for head in range(CHEADS):
-            message_ref[head, part * size : (part + 1) * size, :] = projected[
-                head * size : (head + 1) * size
-            ]
+            place_in_message(
+                message_ref,
+                head,
+                slice(part * size, (part + 1) * size),
+                projected[head * size : (head + 1) * size],
+            )
 
 
 def pool_kernel(
@@ -261,15 +284,29 @@
     send_projected(pooled, qkv_ref[0], message_ref)
 
 
-def coarse_kernel(counts_ref, x_ref, out_ref, keys_ref, values_ref, most_ref, total_ref):
-    tiles, parts, width = x_ref.shape
-    size = parts // 3
+def coarse_kernel(
+    counts_ref,
+    message_ref,
+    swapped_ref,
+    one_ref,
+    two_ref,
+    three_ref,
+    out_ref,
+    queries_ref,
+    keys_ref,
+    values_ref,
+    most_ref,
+    total_ref,
+):
+    tiles, size, width = queries_ref.shape
     per_tile = width // GRAN
     top = 4
     scale = LOG2E / math.sqrt(size)
-    for t in range(tiles):
-        keys_ref[t] = x_ref[t, size : 2 * size, :].astype(F32).T.astype(BF16)
-        values_ref[t] = jnp.concatenate([x_ref[t, 2 * size :, :], jnp.ones((16, width), BF16)], axis=0)
+    ones = jnp.ones((16, width), BF16)
+    for t, block_ref in received_blocks(message_ref, swapped_ref, (one_ref, two_ref, three_ref)):
+        queries_ref[t] = block_ref[:size, :]
+        keys_ref[t] = block_ref[size : 2 * size, :].astype(F32).T.astype(BF16)
+        values_ref[t] = jnp.concatenate([block_ref[2 * size :, :], ones], axis=0)
     edges = [counts_ref[0, 0]]
     for e in range(1, counts_ref.shape[1] - 1):
         edges.append(edges[-1] + counts_ref[0, e])
@@ -285,7 +322,7 @@
         return begin, end
 
     def one(tile, _):
-        queries = x_ref[tile, :size, :]
+        queries = queries_ref[tile]
         begin, end = ball_around(tile * per_tile + lane_block)
         low = ball_around(tile * per_tile)[0] >> tile_bits
         high = (ball_around(tile * per_tile + per_tile - 1)[1] - 1) >> tile_bits
@@ -336,24 +373,58 @@
 
         lax.fori_loop(0, (number - head + 1) >> 1, more, 0)
         total = total_ref[...]
-        out_ref[tile] = (total[:size] / total[size : size + 1]).astype(BF16)
+        place_in_message(out_ref, tile, slice(0, size), (total[:size] / total[size : size + 1]).astype(BF16))
         return 0
 
     lax.fori_loop(0, tiles, one, 0)
 
 
-def between_kernel(x_ref, features_ref, turned_ref, qkv_ref, message_ref, next_ref):
-    heads, size, width = x_ref.shape
-    features = features_ref[...] + dot(turned_ref[0], x_ref[...].reshape(heads * size, width))
+def attended_heads(message_ref, swapped_ref, shifted_refs, heads_ref):
+    heads, size, width = heads_ref.shape
+    for head, block_ref in received_blocks(message_ref, swapped_ref, shifted_refs):
+        heads_ref[head] = block_ref[...]
+    return heads_ref[...].reshape(heads * size, width)
+
+
+def between_kernel(
+    back_ref,
+    swapped_ref,
+    one_ref,
+    two_ref,
+    three_ref,
+    features_ref,
+    turned_ref,
+    qkv_ref,
+    message_ref,
+    next_ref,
+    heads_ref,
+):
+    attended = attended_heads(back_ref, swapped_ref, (one_ref, two_ref, three_ref), heads_ref)
+    features = features_ref[...] + dot(turned_ref[0], attended)
     next_ref[...] = features
     send_projected(features, qkv_ref[1], message_ref)
 
 
 def last_kernel(
-    place_ref, x_ref, features_ref, turned_ref, unpool_ref, placed_ref, out_ref, sum_ref, rows_ref, sems
+    place_ref,
+    back_ref,
+    swapped_ref,
+    one_ref,
+    two_ref,
+    three_ref,
+    features_ref,
+    turned_ref,
+    unpool_ref,
+    placed_ref,
+    out_ref,
+    sum_ref,
+    rows_ref,
+    heads_ref,
+    sems,
 ):
-    heads, size, width = x_ref.shape
-    features = features_ref[...] + dot(turned_ref[1], x_ref[...].reshape(heads * size, width))
+    attended = attended_heads(back_ref, swapped_ref, (one_ref, two_ref, three_ref), heads_ref)
+    width = attended.shape[1]
+    features = features_ref[...] + dot(turned_ref[1], attended)
     features = features.astype(BF16).astype(F32)
     normed = norm_columns(features).astype(F32).T.astype(BF16)
     channels = placed_ref.shape[1]
@@ -383,6 +454,17 @@
 
 def exchange(value, axes):
     return lax.all_to_all(value, axes, split_axis=0, concat_axis=0, tiled=True)
+
+
+def exchange_sub(message):
+    ring = lax.axis_size("sub")
+    swapped = lax.ppermute(message[1], "sub", [(i, i ^ 1) for i in range(ring)])
+    both = jnp.stack([message[0], swapped], axis=1)
+    shifted = {}
+    for ahead in (2, 1, 3):
+        pairs = [(i, (i + 2 * ahead) % ring) for i in range(ring)]
+        shifted[ahead] = lax.ppermute(both[ahead], "sub", pairs)
+    return message, swapped, shifted[1], shifted[2], shifted[3]
 
 
 def shards(
@@ -476,7 +558,7 @@
     message, features, placed = call(
         pool_kernel,
         (
-            shaped((CHEADS, 3 * size, nodes), BF16),
+            shaped((2, subs // 2, 3 * size, nodes), BF16),
             shaped((wide, nodes), F32),
             shaped((own, channels), F32),
         ),
@@ -492,43 +574,45 @@
         name="pool",
     )(named, places, coming, in_hbm(pool_weight), qkv_turned)
     for layer in range(2):
-        received = exchange(message, "sub")
+        received = exchange_sub(message)
         attended = call(
             coarse_kernel,
-            shaped((subs, size, nodes), BF16),
-            [smem(), vmem()],
+            shaped((2, subs // 2, size, nodes), BF16),
+            [smem()] + [vmem()] * 5,
             vmem(),
-            [pltpu.VMEM((subs, nodes, size), BF16), pltpu.VMEM((subs, size + 16, nodes), BF16)]
+            [pltpu.VMEM((subs, size, nodes), BF16), pltpu.VMEM((subs, nodes, size), BF16), pltpu.VMEM((subs, size + 16, nodes), BF16)]
             + [pltpu.VMEM((1, nodes), F32), pltpu.VMEM((size + 16, nodes), F32)],
             flops=subs * nodes * nodes * 3 * size * 4,
             nbytes=subs * nodes * size * 8,
             name="coarse",
-        )(ball_counts, received)
-        back = exchange(attended, "sub")
+        )(ball_counts, *received)
+        back = exchange_sub(attended)
         if layer == 0:
             message, features = call(
                 between_kernel,
-                (shaped((CHEADS, 3 * size, nodes), BF16), shaped((wide, nodes), F32)),
-                [vmem()] * 4,
+                (shaped((2, subs // 2, 3 * size, nodes), BF16), shaped((wide, nodes), F32)),
+                [vmem()] * 8,
                 (vmem(), vmem()),
+                [pltpu.VMEM((subs, size, nodes), BF16)],
                 flops=2 * nodes * wide * 4 * wide,
                 nbytes=nodes * wide * 8,
                 name="between",
-            )(back, features, out_turned, qkv_turned)
+            )(*back, features, out_turned, qkv_turned)
     return call(
         last_kernel,
         shaped((own, channels), F32),
-        [smem()] + [vmem()] * 5,
+        [smem()] + [vmem()] * 9,
         hbm(),
         [
             pltpu.VMEM((own, channels), F32),
             pltpu.VMEM((own, channels), F32),
+            pltpu.VMEM((subs, size, nodes), BF16),
             pltpu.SemaphoreType.DMA((4,)),
         ],
         flops=2 * nodes * wide * 3 * wide,
         nbytes=own * channels * 8,
         name="last",
-    )(places, back, features, out_turned, unpool_weight, placed)
+    )(places, *back, features, out_turned, unpool_weight, placed)
 
 
 def solution(mesh):

time: 149 us -> 147 us (0.987)
  blocking collectives: 72.7 us -> 21.6 us
  waiting for transfers between devices: 9.39 us -> 47 us
  starting transfers between devices: 17.1 us -> 28.3 us
    all_to_all x5 -> x1, blocking collectives: 72.7 us -> 21.6 us  [exchange(): return lax.all_to_all(value, axes, split_axis=0, concat_axis=0, tiled=True)]
    ppermute x0 -> x16, waiting for transfers between devices: none -> 37.6 us  [the longest x12 32.9 us: exchange_sub(): shifted[ahead] = lax.ppermute(both[ahead], 'sub', pairs)]
    ppermute x0 -> x16, starting transfers between devices: none -> 11.3 us  [the longest x12 7.78 us: exchange_sub(): shifted[ahead] = lax.ppermute(both[ahead], 'sub', pairs)]
  transfers between devices with their start and end apart: 2 -> 18, of which waited for: 2 -> 18; matrix products, arithmetic and copies ran while one was open for 3% -> 3% of each run, Pallas kernels for 6% -> 6%
where the time goes in v5:
time: 147 us; the launch traced here: 146 us
  waiting for transfers between devices  47 us (32%)
  Pallas kernels  43.2 us (29%)
  starting transfers between devices  28.3 us (19%)
  blocking collectives  21.6 us (15%)
  local copies, waits for them, and re-layouts  5.41 us (4%)
    ppermute x12, waiting for transfers between devices, exchange_sub(): shifted[ahead] = lax.ppermute(both[ahead], 'sub', pairs)  32.9 us
    all_to_all x1, blocking collectives, exchange(): return lax.all_to_all(value, axes, split_axis=0, concat_axis=0, tiled=True)  21.6 us
    all_to_all x2, starting transfers between devices, exchange(): return lax.all_to_all(value, axes, split_axis=0, concat_axis=0, tiled=True)  17 us
    pallas_call x2, Pallas kernels, shards(): call(coarse_kernel, shaped((2, subs // 2, size, nodes), BF16), [smem()] +...  10.5 us
    all_to_all x2, waiting for transfers between devices, exchange(): return lax.all_to_all(value, axes, split_axis=0, concat_axis=0, tiled=True)  9.39 us
    pallas_call x1, Pallas kernels, shards(): call(second_kernel, shaped((own, channels), BF16), [smem()] + [vmem()] *...  9.16 us
    pallas_call x1, Pallas kernels, shards(): call(first_kernel, shaped((own, channels), F32), [hbm()] * 3, vmem(), [pl...  7.97 us
    ppermute x12, starting transfers between devices, exchange_sub(): shifted[ahead] = lax.ppermute(both[ahead], 'sub', pairs)  7.78 us
  transfers between devices with their start and end apart: 18, of which 18 were waited for; matrix products, arithmetic and copies ran while one was open for 3% of the time, Pallas kernels for 6%

profile of v5, /device:TPU:1, one launch (start us, length us, event | category | flops | bytes accessed | tf_op | source)
XLA Modules:
  0.0 146.0 jit_solution(18416253770525415788)
XLA Ops:
  0.7 1.6 %route.1 = (s32[128,128]{1,0:T(8,128)}, s32[16,128]{1,0:T(8,128)S(1)}) custom-call(s32[16,128]{1,0:T(8,128)S(1)} %bitcast.73), custom_call_target="tpu_custom_call" | custom-call | flops 134217728 | bytes 100000 | tf_op jit(solution)/shard_map/route/pallas_call | solution.py:490
  2.3 11.5 %all-to-all-start = ((s32[128,1,128]{2,1,0:T(1,128)}), s32[128,1,128]{2,1,0:T(1,128)S(1)}, u32[]{:S(2)}, u32[]{:S(2)}) async-start(s32[128,1,128]{2,1,0:T(1,128)} %bitcast.4), calls=%async_computation | async-start | bytes 131072 | tf_op jit(solution)/shard_map/all_to_all | solution.py:456
  13.8 8.0 %first.1.x_ref = f32[2048,128]{1,0:T(8,128)S(1)} custom-call(f32[2048,128]{1,0:T(8,128)} %x_ref.1, bf16[2,128,384]{2,1,0:T(8,128)(2,1)} %qkv_ref.3, bf16[2,128,128]{2,1,0:T(8,128)(2,1)} %out_ref.3), custom_call_target="tpu_custom_call" | custom-call | flops 1342177280 | bytes 2097152 | tf_op jit(solution)/shard_map/first/pallas_call | solution.py:514
  21.7 1.4 all-to-all-done
  23.2 2.5 %answer.1 = (bf16[2048,128]{1,0:T(8,128)(2,1)S(1)}, s32[16,128]{1,0:T(8,128)S(1)}) custom-call(s32[128,128]{1,0:T(8,128)S(1)} %bitcast.69, f32[2048,128]{1,0:T(8,128)S(1)} %first.1.x_ref), custom_call_target="tpu_custom_call" | custom-call | bytes 1572864 | tf_op jit(solution)/shard_map/answer/pallas_call | solution.py:529
  25.7 21.6 %all_to_all.15 = bf16[128,16,128]{2,1,0:T(8,128)(2,1)S(1)} all-to-all(bf16[128,16,128]{2,1,0:T(8,128)(2,1)S(1)} %bitcast.65), channel_id=1, replica_groups=mesh['leaf'=16,'sub'=8] {'leaf','sub'}, dimensions={0} | all-to-all | bytes 1048576 | tf_op jit(solution)/shard_map/all_to_all | solution.py:456
  47.3 9.2 %second.1 = bf16[2048,128]{1,0:T(8,128)(2,1)} custom-call(s32[2048]{0:T(1024)S(1)} %bitcast.75, bf16[2048,128]{1,0:T(8,128)(2,1)S(1)} %bitcast.66, bf16[2,128,384]{2,1,0:T(8,128)(2,1)S(1)} %copy-done.3, bf16[2,128,128]{2,1,0:T(8,128)(2,1)S(1)} %copy-done.4), custom_call_target="tpu_custom_call" | custom-call | flops 1342177280 | bytes 1048576 | tf_op jit(solution)/shard_map/second/pallas_call | solution.py:544
  56.5 5.6 %all-to-all-start.2 = ((bf16[128,16,128]{2,1,0:T(8,128)(2,1)}), bf16[128,16,128]{2,1,0:T(8,128)(2,1)}, u32[]{:S(2)}, u32[]{:S(2)}) async-start(bf16[128,16,128]{2,1,0:T(8,128)(2,1)} %bitcast.10), calls=%async_computation.2 | async-start | bytes 1048576 | tf_op jit(solution)/shard_map/all_to_all | solution.py:456
  62.1 1.3 copy.15
  63.4 3.2 %copy.14 = bf16[2,512,1536]{1,2,0:T(8,128)(2,1)S(1)} copy(bf16[2,512,1536]{2,1,0:T(8,128)(2,1)} %param.17) | data formatting | bytes 6291456 | tf_op args[7]
  67.4 7.9 %all-to-all-done.2 = bf16[128,16,128]{2,1,0:T(8,128)(2,1)} async-done(((bf16[128,16,128]{2,1,0:T(8,128)(2,1)}), bf16[128,16,128]{2,1,0:T(8,128)(2,1)}, u32[]{:S(2)}, u32[]{:S(2)}) %all-to-all-start.2) | async-done | bytes 524320 | tf_op jit(solution)/shard_map/all_to_all | solution.py:456
  75.3 4.9 %pool.1 = (bf16[2,4,192,256]{3,2,1,0:T(8,128)(2,1)S(1)}, f32[512,256]{1,0:T(8,128)S(1)}, f32[2048,128]{1,0:T(8,128)S(1)}) custom-call(s32[2048]{0:T(1024)S(1)} %bitcast.72, s32[2048]{0:T(1024)S(1)} %bitcast.70, bf16[2048,128]{1,0:T(8,128)(2,1)} %bitcast.11.x_ref, bf16[1024,512]{1,0:T(8,128)(2,1)} %pool_ref.1, bf16[2,1536,512]{2,1,0:T(8,128)(2,1)S(1)} %bitcast.59), custom_call_target="tpu_custom_call" | custom-call | flops 671088640 | bytes 2097152 | tf_op jit(solution)/shard_map/pool/pallas_call | solution.py:558
  80.3 1.2 collective-permute-start
  81.5 1.3 collective-permute-done.swapped_ref
  83.4 1.4 collective-permute-start.2
  84.9 4.2 %collective-permute-done.3.three_ref = bf16[2,192,256]{2,1,0:T(8,128)(2,1)S(1)} collective-permute-done((bf16[2,192,256]{2,1,0:T(8,128)(2,1)S(1)}, bf16[2,192,256]{2,1,0:T(8,128)(2,1)S(1)}, u32[]{:S(2)}, u32[]{:S(2)}) %collective-permute-start.3) | collective-permute-done | bytes 196640 | tf_op jit(solution)/shard_map/ppermute | solution.py:466
  89.0 1.7 %collective-permute-done.2.two_ref = bf16[2,192,256]{2,1,0:T(8,128)(2,1)S(1)} collective-permute-done((bf16[2,192,256]{2,1,0:T(8,128)(2,1)S(1)}, bf16[2,192,256]{2,1,0:T(8,128)(2,1)S(1)}, u32[]{:S(2)}, u32[]{:S(2)}) %collective-permute-start.2) | collective-permute-done | bytes 196640 | tf_op jit(solution)/shard_map/ppermute | solution.py:466
  90.8 5.2 %collective-permute-done.1.one_ref = bf16[2,192,256]{2,1,0:T(8,128)(2,1)S(1)} collective-permute-done((bf16[2,192,256]{2,1,0:T(8,128)(2,1)S(1)}, bf16[2,192,256]{2,1,0:T(8,128)(2,1)S(1)}, u32[]{:S(2)}, u32[]{:S(2)}) %collective-permute-start.1) | collective-permute-done | bytes 196640 | tf_op jit(solution)/shard_map/ppermute | solution.py:466
  96.0 5.3 %coarse.2.back_ref = bf16[2,4,64,256]{3,2,1,0:T(8,128)(2,1)S(1)} custom-call(s32[1,8]{1,0:T(1,128)S(1)} %copy-done.2, bf16[2,4,192,256]{3,2,1,0:T(8,128)(2,1)S(1)} %get-tuple-element.23.message_ref, bf16[4,192,256]{2,1,0:T(8,128)(2,1)S(1)} %collective-permute-done.swapped_ref, bf16[2,192,256]{2,1,0:T(8,128)(2,1)S(1)} %collective-permute-done.1.one_ref, ...), custom_call_target="tpu_custom_call" | custom-call | flops 402653184 | bytes 1048576 | tf_op jit(solution)/shard_map/coarse/pallas_call | solution.py:578
  103.3 1.3 collective-permute-start.6
  106.0 1.9 %collective-permute-done.6.two_ref = bf16[2,64,256]{2,1,0:T(8,128)(2,1)S(1)} collective-permute-done((bf16[2,64,256]{2,1,0:T(8,128)(2,1)S(1)}, bf16[2,64,256]{2,1,0:T(8,128)(2,1)S(1)}, u32[]{:S(2)}, u32[]{:S(2)}) %collective-permute-start.6) | collective-permute-done | bytes 65568 | tf_op jit(solution)/shard_map/ppermute | solution.py:466
  108.0 2.0 %collective-permute-done.5.one_ref = bf16[2,64,256]{2,1,0:T(8,128)(2,1)S(1)} collective-permute-done((bf16[2,64,256]{2,1,0:T(8,128)(2,1)S(1)}, bf16[2,64,256]{2,1,0:T(8,128)(2,1)S(1)}, u32[]{:S(2)}, u32[]{:S(2)}) %collective-permute-start.5) | collective-permute-done | bytes 65568 | tf_op jit(solution)/shard_map/ppermute | solution.py:466
  110.0 1.3 between.1
  112.5 1.3 collective-permute-done.8.swapped_ref
  115.8 4.2 %collective-permute-done.11.three_ref = bf16[2,192,256]{2,1,0:T(8,128)(2,1)S(1)} collective-permute-done((bf16[2,192,256]{2,1,0:T(8,128)(2,1)S(1)}, bf16[2,192,256]{2,1,0:T(8,128)(2,1)S(1)}, u32[]{:S(2)}, u32[]{:S(2)}) %collective-permute-start.11) | collective-permute-done | bytes 196640 | tf_op jit(solution)/shard_map/ppermute | solution.py:466
  120.1 2.1 %collective-permute-done.10.two_ref = bf16[2,192,256]{2,1,0:T(8,128)(2,1)S(1)} collective-permute-done((bf16[2,192,256]{2,1,0:T(8,128)(2,1)S(1)}, bf16[2,192,256]{2,1,0:T(8,128)(2,1)S(1)}, u32[]{:S(2)}, u32[]{:S(2)}) %collective-permute-start.10) | collective-permute-done | bytes 196640 | tf_op jit(solution)/shard_map/ppermute | solution.py:466
  122.2 5.2 %collective-permute-done.9.one_ref = bf16[2,192,256]{2,1,0:T(8,128)(2,1)S(1)} collective-permute-done((bf16[2,192,256]{2,1,0:T(8,128)(2,1)S(1)}, bf16[2,192,256]{2,1,0:T(8,128)(2,1)S(1)}, u32[]{:S(2)}, u32[]{:S(2)}) %collective-permute-start.9) | collective-permute-done | bytes 196640 | tf_op jit(solution)/shard_map/ppermute | solution.py:466
  127.4 5.3 %coarse.3.back_ref = bf16[2,4,64,256]{3,2,1,0:T(8,128)(2,1)S(1)} custom-call(s32[1,8]{1,0:T(1,128)S(1)} %copy-done.2, bf16[2,4,192,256]{3,2,1,0:T(8,128)(2,1)S(1)} %get-tuple-element.26.message_ref, bf16[4,192,256]{2,1,0:T(8,128)(2,1)S(1)} %collective-permute-done.8.swapped_ref, bf16[2,192,256]{2,1,0:T(8,128)(2,1)S(1)} %collective-permute-done.9.one_ref, ...), custom_call_target="tpu_custom_call" | custom-call | flops 402653184 | bytes 1048576 | tf_op jit(solution)/shard_map/coarse/pallas_call | solution.py:578
  135.8 1.6 %collective-permute-done.15.three_ref = bf16[2,64,256]{2,1,0:T(8,128)(2,1)S(1)} collective-permute-done((bf16[2,64,256]{2,1,0:T(8,128)(2,1)S(1)}, bf16[2,64,256]{2,1,0:T(8,128)(2,1)S(1)}, u32[]{:S(2)}, u32[]{:S(2)}) %collective-permute-start.15) | collective-permute-done | bytes 65568 | tf_op jit(solution)/shard_map/ppermute | solution.py:466
  137.5 1.8 %collective-permute-done.14.two_ref = bf16[2,64,256]{2,1,0:T(8,128)(2,1)S(1)} collective-permute-done((bf16[2,64,256]{2,1,0:T(8,128)(2,1)S(1)}, bf16[2,64,256]{2,1,0:T(8,128)(2,1)S(1)}, u32[]{:S(2)}, u32[]{:S(2)}) %collective-permute-start.14) | collective-permute-done | bytes 65568 | tf_op jit(solution)/shard_map/ppermute | solution.py:466
  139.3 2.0 %collective-permute-done.13.one_ref = bf16[2,64,256]{2,1,0:T(8,128)(2,1)S(1)} collective-permute-done((bf16[2,64,256]{2,1,0:T(8,128)(2,1)S(1)}, bf16[2,64,256]{2,1,0:T(8,128)(2,1)S(1)}, u32[]{:S(2)}, u32[]{:S(2)}) %collective-permute-start.13) | collective-permute-done | bytes 65568 | tf_op jit(solution)/shard_map/ppermute | solution.py:466
  141.3 4.5 %last.1 = f32[2048,128]{1,0:T(8,128)} custom-call(s32[2048]{0:T(1024)S(1)} %bitcast.71, bf16[2,4,64,256]{3,2,1,0:T(8,128)(2,1)S(1)} %coarse.3.back_ref, bf16[4,64,256]{2,1,0:T(8,128)(2,1)S(1)} %collective-permute-done.12.swapped_ref, bf16[2,64,256]{2,1,0:T(8,128)(2,1)S(1)} %collective-permute-done.13.one_ref, ...), custom_call_target="tpu_custom_call" | custom-call | flops 402653184 | bytes 2097152 | tf_op jit(solution)/shard_map/last/pallas_call | solution.py:601
  (41 shorter events, 11.9 us)
Async XLA Ops:
  0.0 0.7 copy-start.5
  2.3 20.9 %all-to-all-start = ((s32[128,1,128]{2,1,0:T(1,128)}), s32[128,1,128]{2,1,0:T(1,128)S(1)}, u32[]{:S(2)}, u32[]{:S(2)}) async-start(s32[128,1,128]{2,1,0:T(1,128)} %bitcast.4), calls=%async_computation | async-start | bytes 131072 | tf_op jit(solution)/shard_map/all_to_all | solution.py:456
  13.7 33.6 %copy-start.3 = (bf16[2,128,384]{2,1,0:T(8,128)(2,1)S(1)}, bf16[2,128,384]{2,1,0:T(8,128)(2,1)}, u32[]{:S(2)}) copy-start(bf16[2,128,384]{2,1,0:T(8,128)(2,1)} %qkv_ref.3) | copy-start | bytes 589828
  13.8 33.6 %copy-start.4 = (bf16[2,128,128]{2,1,0:T(8,128)(2,1)S(1)}, bf16[2,128,128]{2,1,0:T(8,128)(2,1)}, u32[]{:S(2)}) copy-start(bf16[2,128,128]{2,1,0:T(8,128)(2,1)} %out_ref.3) | copy-start | bytes 196612
  47.3 14.7 %copy-start.7 = (bf16[2,512,512]{2,1,0:T(8,128)(2,1)S(1)}, bf16[2,512,512]{2,1,0:T(8,128)(2,1)}, u32[]{:S(2)}) copy-start(bf16[2,512,512]{2,1,0:T(8,128)(2,1)} %param.18) | copy-start | bytes 3145732
  56.5 18.8 %all-to-all-start.2 = ((bf16[128,16,128]{2,1,0:T(8,128)(2,1)}), bf16[128,16,128]{2,1,0:T(8,128)(2,1)}, u32[]{:S(2)}, u32[]{:S(2)}) async-start(bf16[128,16,128]{2,1,0:T(8,128)(2,1)} %bitcast.10), calls=%async_computation.2 | async-start | bytes 1048576 | tf_op jit(solution)/shard_map/all_to_all | solution.py:456
  63.4 3.2 %copy-start.6 = (s32[2048]{0:T(1024)S(1)}, s32[2048]{0:T(1024)}, u32[]{:S(2)}) copy-start(s32[2048]{0:T(1024)} %param.12) | copy-start | bytes 24580
  75.3 20.6 %copy-start.2 = (s32[1,8]{1,0:T(1,128)S(1)}, s32[1,8]{1,0:T(1,128)}, u32[]{:S(2)}) copy-start(s32[1,8]{1,0:T(1,128)} %counts_ref.3) | copy-start | bytes 100
  80.2 29.8 %copy-start = (bf16[2,512,512]{1,2,0:T(8,128)(2,1)S(1)}, bf16[2,512,512]{1,2,0:T(8,128)(2,1)}, u32[]{:S(2)}) copy-start(bf16[2,512,512]{1,2,0:T(8,128)(2,1)} %copy.15) | copy-start | bytes 3145732
  80.3 2.5 %collective-permute-start = (bf16[4,192,256]{2,1,0:T(8,128)(2,1)S(1)}, bf16[4,192,256]{2,1,0:T(8,128)(2,1)S(1)}, u32[]{:S(2)}, u32[]{:S(2)}) collective-permute-start(bf16[4,192,256]{2,1,0:T(8,128)(2,1)S(1)} %get-tuple-element.38), channel_id=1, source_target_pairs={{0,1},{1,0},{2,3},{3,2},{4,5},{5,4},{6,7},{7,6},{8,9},{9,8},{10,11... | collective-permute-start | bytes 1179656 | tf_op jit(solution)/shard_map/ppermute | solution.py:461
  82.9 6.2 %collective-permute-start.3 = (bf16[2,192,256]{2,1,0:T(8,128)(2,1)S(1)}, bf16[2,192,256]{2,1,0:T(8,128)(2,1)S(1)}, u32[]{:S(2)}, u32[]{:S(2)}) collective-permute-start(bf16[2,192,256]{2,1,0:T(8,128)(2,1)S(1)} %get-tuple-element.34), channel_id=1, source_target_pairs={{0,6},{1,7},{2,0},{3,1},{4,2},{5,3},{6,4},{7,5},{8,14},{9,15},{10,... | collective-permute-start | bytes 589832 | tf_op jit(solution)/shard_map/ppermute | solution.py:466
  83.4 7.3 %collective-permute-start.2 = (bf16[2,192,256]{2,1,0:T(8,128)(2,1)S(1)}, bf16[2,192,256]{2,1,0:T(8,128)(2,1)S(1)}, u32[]{:S(2)}, u32[]{:S(2)}) collective-permute-start(bf16[2,192,256]{2,1,0:T(8,128)(2,1)S(1)} %get-tuple-element.35), channel_id=1, source_target_pairs={{0,4},{1,5},{2,6},{3,7},{4,0},{5,1},{6,2},{7,3},{8,12},{9,13},{10,... | collective-permute-start | bytes 589832 | tf_op jit(solution)/shard_map/ppermute | solution.py:466
  84.9 11.1 %collective-permute-start.1 = (bf16[2,192,256]{2,1,0:T(8,128)(2,1)S(1)}, bf16[2,192,256]{2,1,0:T(8,128)(2,1)S(1)}, u32[]{:S(2)}, u32[]{:S(2)}) collective-permute-start(bf16[2,192,256]{2,1,0:T(8,128)(2,1)S(1)} %get-tuple-element.36), channel_id=1, source_target_pairs={{0,2},{1,3},{2,4},{3,5},{4,6},{5,7},{6,0},{7,1},{8,10},{9,11},{10,... | collective-permute-start | bytes 589832 | tf_op jit(solution)/shard_map/ppermute | solution.py:466
  101.3 1.6 %collective-permute-start.4 = (bf16[4,64,256]{2,1,0:T(8,128)(2,1)S(1)}, bf16[4,64,256]{2,1,0:T(8,128)(2,1)S(1)}, u32[]{:S(2)}, u32[]{:S(2)}) collective-permute-start(bf16[4,64,256]{2,1,0:T(8,128)(2,1)S(1)} %get-tuple-element.48), channel_id=1, source_target_pairs={{0,1},{1,0},{2,3},{3,2},{4,5},{5,4},{6,7},{7,6},{8,9},{9,8},{10,11... | collective-permute-start | bytes 393224 | tf_op jit(solution)/shard_map/ppermute | solution.py:461
  102.8 3.2 %collective-permute-start.7 = (bf16[2,64,256]{2,1,0:T(8,128)(2,1)S(1)}, bf16[2,64,256]{2,1,0:T(8,128)(2,1)S(1)}, u32[]{:S(2)}, u32[]{:S(2)}) collective-permute-start(bf16[2,64,256]{2,1,0:T(8,128)(2,1)S(1)} %get-tuple-element.44), channel_id=1, source_target_pairs={{0,6},{1,7},{2,0},{3,1},{4,2},{5,3},{6,4},{7,5},{8,14},{9,15},{10,... | collective-permute-start | bytes 196616 | tf_op jit(solution)/shard_map/ppermute | solution.py:466
  103.3 4.6 %collective-permute-start.6 = (bf16[2,64,256]{2,1,0:T(8,128)(2,1)S(1)}, bf16[2,64,256]{2,1,0:T(8,128)(2,1)S(1)}, u32[]{:S(2)}, u32[]{:S(2)}) collective-permute-start(bf16[2,64,256]{2,1,0:T(8,128)(2,1)S(1)} %get-tuple-element.45), channel_id=1, source_target_pairs={{0,4},{1,5},{2,6},{3,7},{4,0},{5,1},{6,2},{7,3},{8,12},{9,13},{10,... | collective-permute-start | bytes 196616 | tf_op jit(solution)/shard_map/ppermute | solution.py:466
  104.7 5.3 %collective-permute-start.5 = (bf16[2,64,256]{2,1,0:T(8,128)(2,1)S(1)}, bf16[2,64,256]{2,1,0:T(8,128)(2,1)S(1)}, u32[]{:S(2)}, u32[]{:S(2)}) collective-permute-start(bf16[2,64,256]{2,1,0:T(8,128)(2,1)S(1)} %get-tuple-element.46), channel_id=1, source_target_pairs={{0,2},{1,3},{2,4},{3,5},{4,6},{5,7},{6,0},{7,1},{8,10},{9,11},{10,... | collective-permute-start | bytes 196616 | tf_op jit(solution)/shard_map/ppermute | solution.py:466
  111.3 30.0 %copy-start.1 = (bf16[512,1024]{1,0:T(8,128)(2,1)S(1)}, bf16[512,1024]{1,0:T(8,128)(2,1)}, u32[]{:S(2)}) copy-start(bf16[512,1024]{1,0:T(8,128)(2,1)} %unpool_ref.1) | copy-start | bytes 3145732
  111.3 2.5 %collective-permute-start.8 = (bf16[4,192,256]{2,1,0:T(8,128)(2,1)S(1)}, bf16[4,192,256]{2,1,0:T(8,128)(2,1)S(1)}, u32[]{:S(2)}, u32[]{:S(2)}) collective-permute-start(bf16[4,192,256]{2,1,0:T(8,128)(2,1)S(1)} %get-tuple-element.33), channel_id=1, source_target_pairs={{0,1},{1,0},{2,3},{3,2},{4,5},{5,4},{6,7},{7,6},{8,9},{9,8},{10,11... | collective-permute-start | bytes 1179656 | tf_op jit(solution)/shard_map/ppermute | solution.py:461
  113.9 6.2 %collective-permute-start.11 = (bf16[2,192,256]{2,1,0:T(8,128)(2,1)S(1)}, bf16[2,192,256]{2,1,0:T(8,128)(2,1)S(1)}, u32[]{:S(2)}, u32[]{:S(2)}) collective-permute-start(bf16[2,192,256]{2,1,0:T(8,128)(2,1)S(1)} %get-tuple-element.29), channel_id=1, source_target_pairs={{0,6},{1,7},{2,0},{3,1},{4,2},{5,3},{6,4},{7,5},{8,14},{9,15},{10,... | collective-permute-start | bytes 589832 | tf_op jit(solution)/shard_map/ppermute | solution.py:466
  114.8 7.3 %collective-permute-start.10 = (bf16[2,192,256]{2,1,0:T(8,128)(2,1)S(1)}, bf16[2,192,256]{2,1,0:T(8,128)(2,1)S(1)}, u32[]{:S(2)}, u32[]{:S(2)}) collective-permute-start(bf16[2,192,256]{2,1,0:T(8,128)(2,1)S(1)} %get-tuple-element.30), channel_id=1, source_target_pairs={{0,4},{1,5},{2,6},{3,7},{4,0},{5,1},{6,2},{7,3},{8,12},{9,13},{10,... | collective-permute-start | bytes 589832 | tf_op jit(solution)/shard_map/ppermute | solution.py:466
  115.5 11.9 %collective-permute-start.9 = (bf16[2,192,256]{2,1,0:T(8,128)(2,1)S(1)}, bf16[2,192,256]{2,1,0:T(8,128)(2,1)S(1)}, u32[]{:S(2)}, u32[]{:S(2)}) collective-permute-start(bf16[2,192,256]{2,1,0:T(8,128)(2,1)S(1)} %get-tuple-element.31), channel_id=1, source_target_pairs={{0,2},{1,3},{2,4},{3,5},{4,6},{5,7},{6,0},{7,1},{8,10},{9,11},{10,... | collective-permute-start | bytes 589832 | tf_op jit(solution)/shard_map/ppermute | solution.py:466
  132.7 1.6 %collective-permute-start.12 = (bf16[4,64,256]{2,1,0:T(8,128)(2,1)S(1)}, bf16[4,64,256]{2,1,0:T(8,128)(2,1)S(1)}, u32[]{:S(2)}, u32[]{:S(2)}) collective-permute-start(bf16[4,64,256]{2,1,0:T(8,128)(2,1)S(1)} %get-tuple-element.43), channel_id=1, source_target_pairs={{0,1},{1,0},{2,3},{3,2},{4,5},{5,4},{6,7},{7,6},{8,9},{9,8},{10,11... | collective-permute-start | bytes 393224 | tf_op jit(solution)/shard_map/ppermute | solution.py:461
  134.3 3.2 %collective-permute-start.15 = (bf16[2,64,256]{2,1,0:T(8,128)(2,1)S(1)}, bf16[2,64,256]{2,1,0:T(8,128)(2,1)S(1)}, u32[]{:S(2)}, u32[]{:S(2)}) collective-permute-start(bf16[2,64,256]{2,1,0:T(8,128)(2,1)S(1)} %get-tuple-element.39), channel_id=1, source_target_pairs={{0,6},{1,7},{2,0},{3,1},{4,2},{5,3},{6,4},{7,5},{8,14},{9,15},{10,... | collective-permute-start | bytes 196616 | tf_op jit(solution)/shard_map/ppermute | solution.py:466
  134.7 4.6 %collective-permute-start.14 = (bf16[2,64,256]{2,1,0:T(8,128)(2,1)S(1)}, bf16[2,64,256]{2,1,0:T(8,128)(2,1)S(1)}, u32[]{:S(2)}, u32[]{:S(2)}) collective-permute-start(bf16[2,64,256]{2,1,0:T(8,128)(2,1)S(1)} %get-tuple-element.40), channel_id=1, source_target_pairs={{0,4},{1,5},{2,6},{3,7},{4,0},{5,1},{6,2},{7,3},{8,12},{9,13},{10,... | collective-permute-start | bytes 196616 | tf_op jit(solution)/shard_map/ppermute | solution.py:466
  135.3 6.0 %collective-permute-start.13 = (bf16[2,64,256]{2,1,0:T(8,128)(2,1)S(1)}, bf16[2,64,256]{2,1,0:T(8,128)(2,1)S(1)}, u32[]{:S(2)}, u32[]{:S(2)}) collective-permute-start(bf16[2,64,256]{2,1,0:T(8,128)(2,1)S(1)} %get-tuple-element.41), channel_id=1, source_target_pairs={{0,2},{1,3},{2,4},{3,5},{4,6},{5,7},{6,0},{7,1},{8,10},{9,11},{10,... | collective-permute-start | bytes 196616 | tf_op jit(solution)/shard_map/ppermute | solution.py:466

commit v6 on v5

--- a/solution.py
+++ b/solution.py
@@ -288,9 +288,9 @@
     counts_ref,
     message_ref,
     swapped_ref,
+    three_ref,
     one_ref,
     two_ref,
-    three_ref,
     out_ref,
     queries_ref,
     keys_ref,
@@ -389,9 +389,9 @@
 def between_kernel(
     back_ref,
     swapped_ref,
+    three_ref,
     one_ref,
     two_ref,
-    three_ref,
     features_ref,
     turned_ref,
     qkv_ref,
@@ -409,9 +409,9 @@
     place_ref,
     back_ref,
     swapped_ref,
+    three_ref,
     one_ref,
     two_ref,
-    three_ref,
     features_ref,
     turned_ref,
     unpool_ref,
@@ -464,7 +464,7 @@
     for ahead in (2, 1, 3):
         pairs = [(i, (i + 2 * ahead) % ring) for i in range(ring)]
         shifted[ahead] = lax.ppermute(both[ahead], "sub", pairs)
-    return message, swapped, shifted[1], shifted[2], shifted[3]
+    return message, swapped, shifted[3], shifted[1], shifted[2]
 
 
 def shards(

time: 147 us -> 146 us (level)
  waiting for transfers between devices: 47 us -> 37.5 us
  starting transfers between devices: 28.3 us -> 35.4 us
  Pallas kernels: 43.2 us -> 44.9 us
    ppermute x12, waiting for transfers between devices: 32.9 us -> 23.5 us  [exchange_sub(): shifted[ahead] = lax.ppermute(both[ahead], 'sub', pairs)]
    ppermute x12, starting transfers between devices: 7.78 us -> 15 us  [exchange_sub(): shifted[ahead] = lax.ppermute(both[ahead], 'sub', pairs)]
    pallas_call x2, Pallas kernels: 10.5 us -> 12.2 us  [shards(): call(coarse_kernel, shaped((2, subs // 2, size, nodes), BF16), [smem()] +...]
  transfers between devices with their start and end apart: 18 -> 18, of which waited for: 18 -> 14; matrix products, arithmetic and copies ran while one was open for 3% -> 3% of each run, Pallas kernels for 6% -> 6%
where the time goes in v6:
time: 146 us; the launch traced here: 145 us
  Pallas kernels  44.9 us (31%)
  waiting for transfers between devices  37.5 us (26%)
  starting transfers between devices  35.4 us (24%)
  blocking collectives  21.6 us (15%)
  local copies, waits for them, and re-layouts  5.41 us (4%)
    ppermute x12, waiting for transfers between devices, exchange_sub(): shifted[ahead] = lax.ppermute(both[ahead], 'sub', pairs)  23.5 us
    all_to_all x1, blocking collectives, exchange(): return lax.all_to_all(value, axes, split_axis=0, concat_axis=0, tiled=True)  21.6 us
    all_to_all x2, starting transfers between devices, exchange(): return lax.all_to_all(value, axes, split_axis=0, concat_axis=0, tiled=True)  17 us
    ppermute x12, starting transfers between devices, exchange_sub(): shifted[ahead] = lax.ppermute(both[ahead], 'sub', pairs)  15 us
    pallas_call x2, Pallas kernels, shards(): call(coarse_kernel, shaped((2, subs // 2, size, nodes), BF16), [smem()] +...  12.2 us
    all_to_all x2, waiting for transfers between devices, exchange(): return lax.all_to_all(value, axes, split_axis=0, concat_axis=0, tiled=True)  9.39 us
    pallas_call x1, Pallas kernels, shards(): call(second_kernel, shaped((own, channels), BF16), [smem()] + [vmem()] *...  9.17 us
    pallas_call x1, Pallas kernels, shards(): call(first_kernel, shaped((own, channels), F32), [hbm()] * 3, vmem(), [pl...  7.97 us
  transfers between devices with their start and end apart: 18, of which 14 were waited for; matrix products, arithmetic and copies ran while one was open for 3% of the time, Pallas kernels for 6%

profile of v6, /device:TPU:1, one launch (start us, length us, event | category | flops | bytes accessed | tf_op | source)
XLA Modules:
  0.0 145.3 jit_solution(3918472599527563602)
XLA Ops:
  0.7 1.6 %route.1 = (s32[128,128]{1,0:T(8,128)}, s32[16,128]{1,0:T(8,128)S(1)}) custom-call(s32[16,128]{1,0:T(8,128)S(1)} %bitcast.73), custom_call_target="tpu_custom_call" | custom-call | flops 134217728 | bytes 100000 | tf_op jit(solution)/shard_map/route/pallas_call | solution.py:490
  2.3 11.5 %all-to-all-start = ((s32[128,1,128]{2,1,0:T(1,128)}), s32[128,1,128]{2,1,0:T(1,128)S(1)}, u32[]{:S(2)}, u32[]{:S(2)}) async-start(s32[128,1,128]{2,1,0:T(1,128)} %bitcast.4), calls=%async_computation | async-start | bytes 131072 | tf_op jit(solution)/shard_map/all_to_all | solution.py:456
  13.8 8.0 %first.1.x_ref = f32[2048,128]{1,0:T(8,128)S(1)} custom-call(f32[2048,128]{1,0:T(8,128)} %x_ref.1, bf16[2,128,384]{2,1,0:T(8,128)(2,1)} %qkv_ref.3, bf16[2,128,128]{2,1,0:T(8,128)(2,1)} %out_ref.3), custom_call_target="tpu_custom_call" | custom-call | flops 1342177280 | bytes 2097152 | tf_op jit(solution)/shard_map/first/pallas_call | solution.py:514
  21.7 1.4 all-to-all-done
  23.2 2.5 %answer.1 = (bf16[2048,128]{1,0:T(8,128)(2,1)S(1)}, s32[16,128]{1,0:T(8,128)S(1)}) custom-call(s32[128,128]{1,0:T(8,128)S(1)} %bitcast.69, f32[2048,128]{1,0:T(8,128)S(1)} %first.1.x_ref), custom_call_target="tpu_custom_call" | custom-call | bytes 1572864 | tf_op jit(solution)/shard_map/answer/pallas_call | solution.py:529
  25.7 21.6 %all_to_all.15 = bf16[128,16,128]{2,1,0:T(8,128)(2,1)S(1)} all-to-all(bf16[128,16,128]{2,1,0:T(8,128)(2,1)S(1)} %bitcast.65), channel_id=1, replica_groups=mesh['leaf'=16,'sub'=8] {'leaf','sub'}, dimensions={0} | all-to-all | bytes 1048576 | tf_op jit(solution)/shard_map/all_to_all | solution.py:456
  47.3 9.2 %second.1 = bf16[2048,128]{1,0:T(8,128)(2,1)} custom-call(s32[2048]{0:T(1024)S(1)} %bitcast.75, bf16[2048,128]{1,0:T(8,128)(2,1)S(1)} %bitcast.66, bf16[2,128,384]{2,1,0:T(8,128)(2,1)S(1)} %copy-done.3, bf16[2,128,128]{2,1,0:T(8,128)(2,1)S(1)} %copy-done.4), custom_call_target="tpu_custom_call" | custom-call | flops 1342177280 | bytes 1048576 | tf_op jit(solution)/shard_map/second/pallas_call | solution.py:544
  56.5 5.5 %all-to-all-start.2 = ((bf16[128,16,128]{2,1,0:T(8,128)(2,1)}), bf16[128,16,128]{2,1,0:T(8,128)(2,1)}, u32[]{:S(2)}, u32[]{:S(2)}) async-start(bf16[128,16,128]{2,1,0:T(8,128)(2,1)} %bitcast.10), calls=%async_computation.2 | async-start | bytes 1048576 | tf_op jit(solution)/shard_map/all_to_all | solution.py:456
  62.0 1.3 copy.15
  63.4 3.2 %copy.14 = bf16[2,512,1536]{1,2,0:T(8,128)(2,1)S(1)} copy(bf16[2,512,1536]{2,1,0:T(8,128)(2,1)} %param.17) | data formatting | bytes 6291456 | tf_op args[7]
  67.4 7.9 %all-to-all-done.2 = bf16[128,16,128]{2,1,0:T(8,128)(2,1)} async-done(((bf16[128,16,128]{2,1,0:T(8,128)(2,1)}), bf16[128,16,128]{2,1,0:T(8,128)(2,1)}, u32[]{:S(2)}, u32[]{:S(2)}) %all-to-all-start.2) | async-done | bytes 524320 | tf_op jit(solution)/shard_map/all_to_all | solution.py:456
  75.3 4.9 %pool.1 = (bf16[2,4,192,256]{3,2,1,0:T(8,128)(2,1)S(1)}, f32[512,256]{1,0:T(8,128)S(1)}, f32[2048,128]{1,0:T(8,128)S(1)}) custom-call(s32[2048]{0:T(1024)S(1)} %bitcast.72, s32[2048]{0:T(1024)S(1)} %bitcast.70, bf16[2048,128]{1,0:T(8,128)(2,1)} %bitcast.11.x_ref, bf16[1024,512]{1,0:T(8,128)(2,1)} %pool_ref.1, bf16[2,1536,512]{2,1,0:T(8,128)(2,1)S(1)} %bitcast.59), custom_call_target="tpu_custom_call" | custom-call | flops 671088640 | bytes 2097152 | tf_op jit(solution)/shard_map/pool/pallas_call | solution.py:558
  80.3 1.2 collective-permute-start
  81.5 1.3 collective-permute-done.swapped_ref
  84.0 2.1 %collective-permute-start.1 = (bf16[2,192,256]{2,1,0:T(8,128)(2,1)S(1)}, bf16[2,192,256]{2,1,0:T(8,128)(2,1)S(1)}, u32[]{:S(2)}, u32[]{:S(2)}) collective-permute-start(bf16[2,192,256]{2,1,0:T(8,128)(2,1)S(1)} %get-tuple-element.36), channel_id=1, source_target_pairs={{0,6},{1,7},{2,0},{3,1},{4,2},{5,3},{6,4},{7,5},{8,14},{9,15},{10,... | collective-permute-start | bytes 589832 | tf_op jit(solution)/shard_map/ppermute | solution.py:466
  86.1 4.5 %collective-permute-done.3.two_ref = bf16[2,192,256]{2,1,0:T(8,128)(2,1)S(1)} collective-permute-done((bf16[2,192,256]{2,1,0:T(8,128)(2,1)S(1)}, bf16[2,192,256]{2,1,0:T(8,128)(2,1)S(1)}, u32[]{:S(2)}, u32[]{:S(2)}) %collective-permute-start.3) | collective-permute-done | bytes 196640 | tf_op jit(solution)/shard_map/ppermute | solution.py:466
  90.6 4.9 %collective-permute-done.2.one_ref = bf16[2,192,256]{2,1,0:T(8,128)(2,1)S(1)} collective-permute-done((bf16[2,192,256]{2,1,0:T(8,128)(2,1)S(1)}, bf16[2,192,256]{2,1,0:T(8,128)(2,1)S(1)}, u32[]{:S(2)}, u32[]{:S(2)}) %collective-permute-start.2) | collective-permute-done | bytes 196640 | tf_op jit(solution)/shard_map/ppermute | solution.py:466
  95.5 6.1 %coarse.2.back_ref = bf16[2,4,64,256]{3,2,1,0:T(8,128)(2,1)S(1)} custom-call(s32[1,8]{1,0:T(1,128)S(1)} %copy-done.2, bf16[2,4,192,256]{3,2,1,0:T(8,128)(2,1)S(1)} %get-tuple-element.23.message_ref, bf16[4,192,256]{2,1,0:T(8,128)(2,1)S(1)} %collective-permute-done.swapped_ref, bf16[2,192,256]{2,1,0:T(8,128)(2,1)S(1)} %collective-permute-done.1.three_ref, ...), custom_call_target="tpu_custom_call" | custom-call | flops 402653184 | bytes 1048576 | tf_op jit(solution)/shard_map/coarse/pallas_call | solution.py:578
  104.3 2.4 %collective-permute-start.5 = (bf16[2,64,256]{2,1,0:T(8,128)(2,1)S(1)}, bf16[2,64,256]{2,1,0:T(8,128)(2,1)S(1)}, u32[]{:S(2)}, u32[]{:S(2)}) collective-permute-start(bf16[2,64,256]{2,1,0:T(8,128)(2,1)S(1)} %get-tuple-element.46), channel_id=1, source_target_pairs={{0,6},{1,7},{2,0},{3,1},{4,2},{5,3},{6,4},{7,5},{8,14},{9,15},{10,... | collective-permute-start | bytes 196616 | tf_op jit(solution)/shard_map/ppermute | solution.py:466
  106.7 1.2 collective-permute-done.7.two_ref
  107.9 1.9 %collective-permute-done.6.one_ref = bf16[2,64,256]{2,1,0:T(8,128)(2,1)S(1)} collective-permute-done((bf16[2,64,256]{2,1,0:T(8,128)(2,1)S(1)}, bf16[2,64,256]{2,1,0:T(8,128)(2,1)S(1)}, u32[]{:S(2)}, u32[]{:S(2)}) %collective-permute-start.6) | collective-permute-done | bytes 65568 | tf_op jit(solution)/shard_map/ppermute | solution.py:466
  109.8 1.3 between.1
  112.1 1.3 collective-permute-done.8.swapped_ref
  113.5 1.5 %collective-permute-start.11 = (bf16[2,192,256]{2,1,0:T(8,128)(2,1)S(1)}, bf16[2,192,256]{2,1,0:T(8,128)(2,1)S(1)}, u32[]{:S(2)}, u32[]{:S(2)}) collective-permute-start(bf16[2,192,256]{2,1,0:T(8,128)(2,1)S(1)} %get-tuple-element.29), channel_id=1, source_target_pairs={{0,4},{1,5},{2,6},{3,7},{4,0},{5,1},{6,2},{7,3},{8,12},{9,13},{10,... | collective-permute-start | bytes 589832 | tf_op jit(solution)/shard_map/ppermute | solution.py:466
  115.1 1.5 %collective-permute-start.10 = (bf16[2,192,256]{2,1,0:T(8,128)(2,1)S(1)}, bf16[2,192,256]{2,1,0:T(8,128)(2,1)S(1)}, u32[]{:S(2)}, u32[]{:S(2)}) collective-permute-start(bf16[2,192,256]{2,1,0:T(8,128)(2,1)S(1)} %get-tuple-element.30), channel_id=1, source_target_pairs={{0,2},{1,3},{2,4},{3,5},{4,6},{5,7},{6,0},{7,1},{8,10},{9,11},{10,... | collective-permute-start | bytes 589832 | tf_op jit(solution)/shard_map/ppermute | solution.py:466
  117.8 3.5 %collective-permute-done.11.two_ref = bf16[2,192,256]{2,1,0:T(8,128)(2,1)S(1)} collective-permute-done((bf16[2,192,256]{2,1,0:T(8,128)(2,1)S(1)}, bf16[2,192,256]{2,1,0:T(8,128)(2,1)S(1)}, u32[]{:S(2)}, u32[]{:S(2)}) %collective-permute-start.11) | collective-permute-done | bytes 196640 | tf_op jit(solution)/shard_map/ppermute | solution.py:466
  121.3 4.9 %collective-permute-done.10.one_ref = bf16[2,192,256]{2,1,0:T(8,128)(2,1)S(1)} collective-permute-done((bf16[2,192,256]{2,1,0:T(8,128)(2,1)S(1)}, bf16[2,192,256]{2,1,0:T(8,128)(2,1)S(1)}, u32[]{:S(2)}, u32[]{:S(2)}) %collective-permute-start.10) | collective-permute-done | bytes 196640 | tf_op jit(solution)/shard_map/ppermute | solution.py:466
  126.2 6.1 %coarse.3.back_ref = bf16[2,4,64,256]{3,2,1,0:T(8,128)(2,1)S(1)} custom-call(s32[1,8]{1,0:T(1,128)S(1)} %copy-done.2, bf16[2,4,192,256]{3,2,1,0:T(8,128)(2,1)S(1)} %get-tuple-element.26.message_ref, bf16[4,192,256]{2,1,0:T(8,128)(2,1)S(1)} %collective-permute-done.8.swapped_ref, bf16[2,192,256]{2,1,0:T(8,128)(2,1)S(1)} %collective-permute-done.9.three_ref, ...), custom_call_target="tpu_custom_call" | custom-call | flops 402653184 | bytes 1048576 | tf_op jit(solution)/shard_map/coarse/pallas_call | solution.py:578
  133.9 1.5 %collective-permute-start.15 = (bf16[2,64,256]{2,1,0:T(8,128)(2,1)S(1)}, bf16[2,64,256]{2,1,0:T(8,128)(2,1)S(1)}, u32[]{:S(2)}, u32[]{:S(2)}) collective-permute-start(bf16[2,64,256]{2,1,0:T(8,128)(2,1)S(1)} %get-tuple-element.39), channel_id=1, source_target_pairs={{0,4},{1,5},{2,6},{3,7},{4,0},{5,1},{6,2},{7,3},{8,12},{9,13},{10,... | collective-permute-start | bytes 196616 | tf_op jit(solution)/shard_map/ppermute | solution.py:466
  135.4 1.5 %collective-permute-start.14 = (bf16[2,64,256]{2,1,0:T(8,128)(2,1)S(1)}, bf16[2,64,256]{2,1,0:T(8,128)(2,1)S(1)}, u32[]{:S(2)}, u32[]{:S(2)}) collective-permute-start(bf16[2,64,256]{2,1,0:T(8,128)(2,1)S(1)} %get-tuple-element.40), channel_id=1, source_target_pairs={{0,2},{1,3},{2,4},{3,5},{4,6},{5,7},{6,0},{7,1},{8,10},{9,11},{10,... | collective-permute-start | bytes 196616 | tf_op jit(solution)/shard_map/ppermute | solution.py:466
  138.6 2.0 %collective-permute-done.14.one_ref = bf16[2,64,256]{2,1,0:T(8,128)(2,1)S(1)} collective-permute-done((bf16[2,64,256]{2,1,0:T(8,128)(2,1)S(1)}, bf16[2,64,256]{2,1,0:T(8,128)(2,1)S(1)}, u32[]{:S(2)}, u32[]{:S(2)}) %collective-permute-start.14) | collective-permute-done | bytes 65568 | tf_op jit(solution)/shard_map/ppermute | solution.py:466
  140.6 4.5 %last.1 = f32[2048,128]{1,0:T(8,128)} custom-call(s32[2048]{0:T(1024)S(1)} %bitcast.71, bf16[2,4,64,256]{3,2,1,0:T(8,128)(2,1)S(1)} %coarse.3.back_ref, bf16[4,64,256]{2,1,0:T(8,128)(2,1)S(1)} %collective-permute-done.12.swapped_ref, bf16[2,64,256]{2,1,0:T(8,128)(2,1)S(1)} %collective-permute-done.13.three_ref, ...), custom_call_target="tpu_custom_call" | custom-call | flops 402653184 | bytes 2097152 | tf_op jit(solution)/shard_map/last/pallas_call | solution.py:601
  (41 shorter events, 11.0 us)
Async XLA Ops:
  0.0 0.7 copy-start.5
  2.3 20.9 %all-to-all-start = ((s32[128,1,128]{2,1,0:T(1,128)}), s32[128,1,128]{2,1,0:T(1,128)S(1)}, u32[]{:S(2)}, u32[]{:S(2)}) async-start(s32[128,1,128]{2,1,0:T(1,128)} %bitcast.4), calls=%async_computation | async-start | bytes 131072 | tf_op jit(solution)/shard_map/all_to_all | solution.py:456
  13.7 33.6 %copy-start.3 = (bf16[2,128,384]{2,1,0:T(8,128)(2,1)S(1)}, bf16[2,128,384]{2,1,0:T(8,128)(2,1)}, u32[]{:S(2)}) copy-start(bf16[2,128,384]{2,1,0:T(8,128)(2,1)} %qkv_ref.3) | copy-start | bytes 589828
  13.8 33.6 %copy-start.4 = (bf16[2,128,128]{2,1,0:T(8,128)(2,1)S(1)}, bf16[2,128,128]{2,1,0:T(8,128)(2,1)}, u32[]{:S(2)}) copy-start(bf16[2,128,128]{2,1,0:T(8,128)(2,1)} %out_ref.3) | copy-start | bytes 196612
  47.3 14.7 %copy-start.7 = (bf16[2,512,512]{2,1,0:T(8,128)(2,1)S(1)}, bf16[2,512,512]{2,1,0:T(8,128)(2,1)}, u32[]{:S(2)}) copy-start(bf16[2,512,512]{2,1,0:T(8,128)(2,1)} %param.18) | copy-start | bytes 3145732
  56.5 18.8 %all-to-all-start.2 = ((bf16[128,16,128]{2,1,0:T(8,128)(2,1)}), bf16[128,16,128]{2,1,0:T(8,128)(2,1)}, u32[]{:S(2)}, u32[]{:S(2)}) async-start(bf16[128,16,128]{2,1,0:T(8,128)(2,1)} %bitcast.10), calls=%async_computation.2 | async-start | bytes 1048576 | tf_op jit(solution)/shard_map/all_to_all | solution.py:456
  63.4 3.2 %copy-start.6 = (s32[2048]{0:T(1024)S(1)}, s32[2048]{0:T(1024)}, u32[]{:S(2)}) copy-start(s32[2048]{0:T(1024)} %param.12) | copy-start | bytes 24580
  75.3 20.2 %copy-start.2 = (s32[1,8]{1,0:T(1,128)S(1)}, s32[1,8]{1,0:T(1,128)}, u32[]{:S(2)}) copy-start(s32[1,8]{1,0:T(1,128)} %counts_ref.3) | copy-start | bytes 100
  80.2 29.6 %copy-start = (bf16[2,512,512]{1,2,0:T(8,128)(2,1)S(1)}, bf16[2,512,512]{1,2,0:T(8,128)(2,1)}, u32[]{:S(2)}) copy-start(bf16[2,512,512]{1,2,0:T(8,128)(2,1)} %copy.15) | copy-start | bytes 3145732
  80.3 2.5 %collective-permute-start = (bf16[4,192,256]{2,1,0:T(8,128)(2,1)S(1)}, bf16[4,192,256]{2,1,0:T(8,128)(2,1)S(1)}, u32[]{:S(2)}, u32[]{:S(2)}) collective-permute-start(bf16[4,192,256]{2,1,0:T(8,128)(2,1)S(1)} %get-tuple-element.38), channel_id=1, source_target_pairs={{0,1},{1,0},{2,3},{3,2},{4,5},{5,4},{6,7},{7,6},{8,9},{9,8},{10,11... | collective-permute-start | bytes 1179656 | tf_op jit(solution)/shard_map/ppermute | solution.py:461
  82.9 7.7 %collective-permute-start.3 = (bf16[2,192,256]{2,1,0:T(8,128)(2,1)S(1)}, bf16[2,192,256]{2,1,0:T(8,128)(2,1)S(1)}, u32[]{:S(2)}, u32[]{:S(2)}) collective-permute-start(bf16[2,192,256]{2,1,0:T(8,128)(2,1)S(1)} %get-tuple-element.34), channel_id=1, source_target_pairs={{0,4},{1,5},{2,6},{3,7},{4,0},{5,1},{6,2},{7,3},{8,12},{9,13},{10,... | collective-permute-start | bytes 589832 | tf_op jit(solution)/shard_map/ppermute | solution.py:466
  83.4 12.1 %collective-permute-start.2 = (bf16[2,192,256]{2,1,0:T(8,128)(2,1)S(1)}, bf16[2,192,256]{2,1,0:T(8,128)(2,1)S(1)}, u32[]{:S(2)}, u32[]{:S(2)}) collective-permute-start(bf16[2,192,256]{2,1,0:T(8,128)(2,1)S(1)} %get-tuple-element.35), channel_id=1, source_target_pairs={{0,2},{1,3},{2,4},{3,5},{4,6},{5,7},{6,0},{7,1},{8,10},{9,11},{10,... | collective-permute-start | bytes 589832 | tf_op jit(solution)/shard_map/ppermute | solution.py:466
  84.0 11.5 %collective-permute-start.1 = (bf16[2,192,256]{2,1,0:T(8,128)(2,1)S(1)}, bf16[2,192,256]{2,1,0:T(8,128)(2,1)S(1)}, u32[]{:S(2)}, u32[]{:S(2)}) collective-permute-start(bf16[2,192,256]{2,1,0:T(8,128)(2,1)S(1)} %get-tuple-element.36), channel_id=1, source_target_pairs={{0,6},{1,7},{2,0},{3,1},{4,2},{5,3},{6,4},{7,5},{8,14},{9,15},{10,... | collective-permute-start | bytes 589832 | tf_op jit(solution)/shard_map/ppermute | solution.py:466
  101.6 1.6 %collective-permute-start.4 = (bf16[4,64,256]{2,1,0:T(8,128)(2,1)S(1)}, bf16[4,64,256]{2,1,0:T(8,128)(2,1)S(1)}, u32[]{:S(2)}, u32[]{:S(2)}) collective-permute-start(bf16[4,64,256]{2,1,0:T(8,128)(2,1)S(1)} %get-tuple-element.48), channel_id=1, source_target_pairs={{0,1},{1,0},{2,3},{3,2},{4,5},{5,4},{6,7},{7,6},{8,9},{9,8},{10,11... | collective-permute-start | bytes 393224 | tf_op jit(solution)/shard_map/ppermute | solution.py:461
  103.2 4.7 %collective-permute-start.7 = (bf16[2,64,256]{2,1,0:T(8,128)(2,1)S(1)}, bf16[2,64,256]{2,1,0:T(8,128)(2,1)S(1)}, u32[]{:S(2)}, u32[]{:S(2)}) collective-permute-start(bf16[2,64,256]{2,1,0:T(8,128)(2,1)S(1)} %get-tuple-element.44), channel_id=1, source_target_pairs={{0,4},{1,5},{2,6},{3,7},{4,0},{5,1},{6,2},{7,3},{8,12},{9,13},{10,... | collective-permute-start | bytes 196616 | tf_op jit(solution)/shard_map/ppermute | solution.py:466
  104.0 5.8 %collective-permute-start.6 = (bf16[2,64,256]{2,1,0:T(8,128)(2,1)S(1)}, bf16[2,64,256]{2,1,0:T(8,128)(2,1)S(1)}, u32[]{:S(2)}, u32[]{:S(2)}) collective-permute-start(bf16[2,64,256]{2,1,0:T(8,128)(2,1)S(1)} %get-tuple-element.45), channel_id=1, source_target_pairs={{0,2},{1,3},{2,4},{3,5},{4,6},{5,7},{6,0},{7,1},{8,10},{9,11},{10,... | collective-permute-start | bytes 196616 | tf_op jit(solution)/shard_map/ppermute | solution.py:466
  104.3 5.5 %collective-permute-start.5 = (bf16[2,64,256]{2,1,0:T(8,128)(2,1)S(1)}, bf16[2,64,256]{2,1,0:T(8,128)(2,1)S(1)}, u32[]{:S(2)}, u32[]{:S(2)}) collective-permute-start(bf16[2,64,256]{2,1,0:T(8,128)(2,1)S(1)} %get-tuple-element.46), channel_id=1, source_target_pairs={{0,6},{1,7},{2,0},{3,1},{4,2},{5,3},{6,4},{7,5},{8,14},{9,15},{10,... | collective-permute-start | bytes 196616 | tf_op jit(solution)/shard_map/ppermute | solution.py:466
  111.1 29.5 %copy-start.1 = (bf16[512,1024]{1,0:T(8,128)(2,1)S(1)}, bf16[512,1024]{1,0:T(8,128)(2,1)}, u32[]{:S(2)}) copy-start(bf16[512,1024]{1,0:T(8,128)(2,1)} %unpool_ref.1) | copy-start | bytes 3145732
  111.2 2.3 %collective-permute-start.8 = (bf16[4,192,256]{2,1,0:T(8,128)(2,1)S(1)}, bf16[4,192,256]{2,1,0:T(8,128)(2,1)S(1)}, u32[]{:S(2)}, u32[]{:S(2)}) collective-permute-start(bf16[4,192,256]{2,1,0:T(8,128)(2,1)S(1)} %get-tuple-element.33), channel_id=1, source_target_pairs={{0,1},{1,0},{2,3},{3,2},{4,5},{5,4},{6,7},{7,6},{8,9},{9,8},{10,11... | collective-permute-start | bytes 1179656 | tf_op jit(solution)/shard_map/ppermute | solution.py:461
  113.5 7.7 %collective-permute-start.11 = (bf16[2,192,256]{2,1,0:T(8,128)(2,1)S(1)}, bf16[2,192,256]{2,1,0:T(8,128)(2,1)S(1)}, u32[]{:S(2)}, u32[]{:S(2)}) collective-permute-start(bf16[2,192,256]{2,1,0:T(8,128)(2,1)S(1)} %get-tuple-element.29), channel_id=1, source_target_pairs={{0,4},{1,5},{2,6},{3,7},{4,0},{5,1},{6,2},{7,3},{8,12},{9,13},{10,... | collective-permute-start | bytes 589832 | tf_op jit(solution)/shard_map/ppermute | solution.py:466
  115.1 11.1 %collective-permute-start.10 = (bf16[2,192,256]{2,1,0:T(8,128)(2,1)S(1)}, bf16[2,192,256]{2,1,0:T(8,128)(2,1)S(1)}, u32[]{:S(2)}, u32[]{:S(2)}) collective-permute-start(bf16[2,192,256]{2,1,0:T(8,128)(2,1)S(1)} %get-tuple-element.30), channel_id=1, source_target_pairs={{0,2},{1,3},{2,4},{3,5},{4,6},{5,7},{6,0},{7,1},{8,10},{9,11},{10,... | collective-permute-start | bytes 589832 | tf_op jit(solution)/shard_map/ppermute | solution.py:466
  116.6 9.6 %collective-permute-start.9 = (bf16[2,192,256]{2,1,0:T(8,128)(2,1)S(1)}, bf16[2,192,256]{2,1,0:T(8,128)(2,1)S(1)}, u32[]{:S(2)}, u32[]{:S(2)}) collective-permute-start(bf16[2,192,256]{2,1,0:T(8,128)(2,1)S(1)} %get-tuple-element.31), channel_id=1, source_target_pairs={{0,6},{1,7},{2,0},{3,1},{4,2},{5,3},{6,4},{7,5},{8,14},{9,15},{10,... | collective-permute-start | bytes 589832 | tf_op jit(solution)/shard_map/ppermute | solution.py:466
  132.3 1.6 %collective-permute-start.12 = (bf16[4,64,256]{2,1,0:T(8,128)(2,1)S(1)}, bf16[4,64,256]{2,1,0:T(8,128)(2,1)S(1)}, u32[]{:S(2)}, u32[]{:S(2)}) collective-permute-start(bf16[4,64,256]{2,1,0:T(8,128)(2,1)S(1)} %get-tuple-element.43), channel_id=1, source_target_pairs={{0,1},{1,0},{2,3},{3,2},{4,5},{5,4},{6,7},{7,6},{8,9},{9,8},{10,11... | collective-permute-start | bytes 393224 | tf_op jit(solution)/shard_map/ppermute | solution.py:461
  133.9 4.7 %collective-permute-start.15 = (bf16[2,64,256]{2,1,0:T(8,128)(2,1)S(1)}, bf16[2,64,256]{2,1,0:T(8,128)(2,1)S(1)}, u32[]{:S(2)}, u32[]{:S(2)}) collective-permute-start(bf16[2,64,256]{2,1,0:T(8,128)(2,1)S(1)} %get-tuple-element.39), channel_id=1, source_target_pairs={{0,4},{1,5},{2,6},{3,7},{4,0},{5,1},{6,2},{7,3},{8,12},{9,13},{10,... | collective-permute-start | bytes 196616 | tf_op jit(solution)/shard_map/ppermute | solution.py:466
  135.4 5.2 %collective-permute-start.14 = (bf16[2,64,256]{2,1,0:T(8,128)(2,1)S(1)}, bf16[2,64,256]{2,1,0:T(8,128)(2,1)S(1)}, u32[]{:S(2)}, u32[]{:S(2)}) collective-permute-start(bf16[2,64,256]{2,1,0:T(8,128)(2,1)S(1)} %get-tuple-element.40), channel_id=1, source_target_pairs={{0,2},{1,3},{2,4},{3,5},{4,6},{5,7},{6,0},{7,1},{8,10},{9,11},{10,... | collective-permute-start | bytes 196616 | tf_op jit(solution)/shard_map/ppermute | solution.py:466
  136.9 3.7 %collective-permute-start.13 = (bf16[2,64,256]{2,1,0:T(8,128)(2,1)S(1)}, bf16[2,64,256]{2,1,0:T(8,128)(2,1)S(1)}, u32[]{:S(2)}, u32[]{:S(2)}) collective-permute-start(bf16[2,64,256]{2,1,0:T(8,128)(2,1)S(1)} %get-tuple-element.41), channel_id=1, source_target_pairs={{0,6},{1,7},{2,0},{3,1},{4,2},{5,3},{6,4},{7,5},{8,14},{9,15},{10,... | collective-permute-start | bytes 196616 | tf_op jit(solution)/shard_map/ppermute | solution.py:466
